TPU v7x, 32 devices: a whole 2x2x4 slice. The times are simulated.
32 devices in a mesh: clips: 2 (over x), segment: 2 (over core), rows: 8 (over z, y).
Axes of the slice: x: 2, y: 2, z: 4, core: 2. Of those that a mesh axis runs over, the one named last changes fastest.
Arguments:
- latent: float32 [4, 48, 512], P('clips', 'rows', 'segment'), parts along dimension 0, may hold values from -6 to 6
- stale: bfloat16 [2, 4, 48, 128, 320], P('segment', 'clips', 'rows'), parts along dimension 1, may hold values from -6 to 6
- timesteps: int32 [4], P('clips'), parts along dimension 0, may hold values from 0 to 999
- w_in: bfloat16 [4, 320], replicated, may hold values from -3 to 3
- w_enc: bfloat16 [3, 3, 320, 320], replicated, may hold values from -0.109375 to 0.109375
- w_down: bfloat16 [3, 3, 320, 640], replicated, may hold values from -0.109375 to 0.109375
- w_tmid: bfloat16 [3, 640, 640], replicated, may hold values from -0.125 to 0.125
- w_up: bfloat16 [640, 320], replicated, may hold values from -0.25 to 0.25
- w_skip: bfloat16 [640, 320], replicated, may hold values from -0.25 to 0.25
- w_dec: bfloat16 [3, 3, 320, 320], replicated, may hold values from -0.109375 to 0.109375
- w_out: bfloat16 [3, 3, 320, 4], replicated, may hold values from -0.109375 to 0.109375
- w_time: bfloat16 [320, 1280], replicated, may hold values from -0.3125 to 0.3125
Outputs:
- next_latent: float32 [4, 48, 512], P('clips', 'rows', 'segment'), parts along dimension 0
- features: bfloat16 [2, 4, 48, 128, 320], P('segment', 'clips', 'rows'), parts along dimension 1
There are 2 independent parts, one for each index of `clips`. A program takes and returns all parts, laid end to end along the dimension named above; an argument that names none is the same for every part. Nothing has to cross between parts.
Inputs may be any that keep to these rules, and one draw needn't show every extreme that they name: `timesteps`: one diffusion timestep index a step.
All inputs are finite; a program needn't handle non-finite values.
Results may differ from a plain program's by a relative error of at most 0.006.
Values may be sent and summed in bfloat16 or wider, within the bound.
No kernel may reach another device: no remote copies, remote signals or barrier semaphores. Data moves between devices by JAX's collectives and lax.ppermute only.
A program may use at most 128 MiB of HBM per device.

v0:
```python
import math

import jax
import jax.numpy as jnp
from jax import lax
from jax.sharding import PartitionSpec as P

EPSILON = 1e-06


def with_halo(value, sides, width):
    for axis, dim in sides:
        size, length = (lax.axis_size(axis), value.shape[dim])
        up = [(i, (i + 1) % size) for i in range(size - 1)]
        down = [(j, i) for i, j in up]
        last = lax.slice_in_dim(value, length - width, length, axis=dim)
        first = lax.slice_in_dim(value, 0, width, axis=dim)
        before = lax.ppermute(last, axis, up)
        after = lax.ppermute(first, axis, down)
        value = jnp.concatenate([before, value, after], axis=dim)
    return value


def swapped(value, axis, stride):
    mask = 2**stride
    pairs = [(source, source ^ mask) for source in range(lax.axis_size(axis))]
    return lax.ppermute(value, axis, pairs)


def from_behind(value, axis, by):
    length = lax.axis_size(axis)
    pairs = [(i, i + by) for i in range(length) if 0 <= i + by < length]
    return lax.ppermute(value, axis, pairs)


def normed(values):
    scale = lax.rsqrt(jnp.mean(values * values, axis=-1, keepdims=True) + EPSILON)
    return jax.nn.silu(values * scale)


def conv_rows(extended, weight, count):
    padded = jnp.pad(extended, ((0, 0), (0, 0), (1, 1), (0, 0)))
    columns = extended.shape[2]
    total = jnp.zeros((extended.shape[0], count, columns, weight.shape[3]), jnp.float32)
    for row_off in range(3):
        for col_off in range(3):
            window = padded[:, row_off : row_off + count, col_off : col_off + columns, :]
            total = total + jnp.einsum(
                "fhwc,co->fhwo",
                window,
                weight[row_off, col_off],
                preferred_element_type=jnp.float32,
            )
    return total


def conv_down(extended, weight, count):
    padded = jnp.pad(extended, ((0, 0), (0, 0), (1, 1), (0, 0)))
    columns = extended.shape[2] // 2
    total = jnp.zeros((extended.shape[0], count, columns, weight.shape[3]), jnp.float32)
    for row_off in range(3):
        for col_off in range(3):
            window = padded[
                :, row_off : row_off + 2 * count : 2, col_off : col_off + 2 * columns : 2, :
            ]
            total = total + jnp.einsum(
                "fhwc,co->fhwo",
                window,
                weight[row_off, col_off],
                preferred_element_type=jnp.float32,
            )
    return total


def temporal(values, weight):
    frames = values.shape[0]
    padded = jnp.pad(values, ((1, 1), (0, 0), (0, 0), (0, 0)))
    total = jnp.zeros(values.shape[:3] + (weight.shape[2],), jnp.float32)
    for offset in range(3):
        total = total + jnp.einsum(
            "fhwc,co->fhwo",
            padded[offset : offset + frames],
            weight[offset],
            preferred_element_type=jnp.float32,
        )
    return total


def time_bias(step_time, w_time):
    half = w_time.shape[0] // 2
    freqs = jnp.exp(-math.log(10000.0) * jnp.arange(half).astype(jnp.float32) / half)
    angles = step_time.astype(jnp.float32) * freqs
    embedded = jnp.concatenate([jnp.sin(angles), jnp.cos(angles)])
    gated = jax.nn.silu(embedded).astype(jnp.bfloat16)
    return jnp.dot(gated[None, :], w_time, preferred_element_type=jnp.float32)[0]


def skip_mix(mid_map, enc_map, w_skip):
    joined = jnp.concatenate([mid_map, enc_map], axis=-1)
    mixed = jnp.einsum("fhwc,co->fhwo", joined, w_skip, preferred_element_type=jnp.float32)
    return (mixed, normed(mixed).astype(jnp.bfloat16))


def body(latent, stale, timesteps, w_in, w_enc, w_down, w_tmid, w_up, w_skip, w_dec, w_out, w_time):
    first = lax.axis_index("segment") == 0
    state = stale[0]
    frames, rows_dev, columns, chans = state.shape
    mid_chans = w_down.shape[3]
    lat_chans = w_in.shape[0]
    half_cols = latent.shape[2]
    current = lax.all_gather(latent, "segment", axis=2, tiled=True)

    def rims(values):
        return with_halo(values, (("rows", 1),), 1)

    for step in range(timesteps.shape[0]):
        other = swapped(state, "segment", 0)
        biases = time_bias(timesteps[step], w_time)
        bias_enc = biases[:chans]
        bias_mid = biases[chans : chans + mid_chans]
        bias_dec = biases[chans + mid_chans :]
        inputs = current.reshape(frames, rows_dev, columns, lat_chans).astype(jnp.bfloat16)

        def enc_front(operands):
            inputs_here, state_here, other_here = operands
            lifted = jnp.einsum(
                "fhwc,co->fhwo", inputs_here, w_in, preferred_element_type=jnp.float32
            )
            return (normed(lifted).astype(jnp.bfloat16), lifted)

        def mid_front(operands):
            inputs_here, state_here, other_here = operands
            gated_enc = normed(other_here.astype(jnp.float32)).astype(jnp.bfloat16)
            return (gated_enc, jnp.zeros(state_here.shape, jnp.float32))

        activated, lifted = lax.cond(first, enc_front, mid_front, (inputs, state, other))
        spread = rims(activated)

        def enc_middle(operands):
            spread_here, lifted_here, state_here, other_here = operands
            fresh = (lifted_here + conv_rows(spread_here, w_enc, rows_dev) + bias_enc).astype(
                jnp.bfloat16
            )
            mixed, gated = skip_mix(other_here, state_here, w_skip)
            return (fresh, mixed, gated)

        def mid_middle(operands):
            spread_here, lifted_here, state_here, other_here = operands
            lowered = conv_down(spread_here, w_down, rows_dev // 2) + bias_mid
            mixed_time = lowered + temporal(normed(lowered).astype(jnp.bfloat16), w_tmid)
            raised = jnp.einsum(
                "fhwc,co->fhwo",
                mixed_time.astype(jnp.bfloat16),
                w_up,
                preferred_element_type=jnp.float32,
            ).astype(jnp.bfloat16)
            fresh = jnp.repeat(jnp.repeat(raised, 2, axis=1), 2, axis=2)
            mixed = jnp.zeros(state_here.shape, jnp.float32)
            gated = jnp.zeros(state_here.shape, jnp.bfloat16)
            return (fresh, mixed, gated)

        fresh, mixed, gated = lax.cond(
            first, enc_middle, mid_middle, (spread, lifted, state, other)
        )
        sheared = rims(gated)

        def enc_tail(operands):
            sheared_here, mixed_here = operands
            decoded = mixed_here + conv_rows(sheared_here, w_dec, rows_dev) + bias_dec
            return normed(decoded).astype(jnp.bfloat16)

        def mid_tail(operands):
            sheared_here, mixed_here = operands
            return jnp.zeros(mixed_here.shape, jnp.bfloat16)

        outlet = lax.cond(first, enc_tail, mid_tail, (sheared, mixed))
        widened = rims(outlet)
        noise = conv_rows(widened, w_out, rows_dev)
        coefficient = (timesteps[step].astype(jnp.float32) + 1.0) / 1000.0
        current = current - coefficient * noise.reshape(frames, rows_dev, columns * lat_chans)
        state = fresh
    spare = from_behind(current[:, :, half_cols:], "segment", 1)
    result = jnp.where(first, current[:, :, :half_cols], spare)
    return (result, state[None])


def solution(mesh):
    placed = (
        P("clips", "rows", "segment"),
        P("segment", "clips", "rows", None, None),
        P("clips"),
        P(),
        P(),
        P(),
        P(),
        P(),
        P(),
        P(),
        P(),
        P(),
    )
    return jax.shard_map(
        body,
        mesh=mesh,
        in_specs=placed,
        out_specs=(P("clips", "rows", "segment"), P("segment", "clips", "rows", None, None)),
        check_vma=False,
    )
```

profile of v0, /device:TPU:0, one launch (start us, length us, event | category | flops | bytes accessed | tf_op | source)
XLA Modules:
  0.0 245.5 jit_solution(10601966086027622090)
XLA Ops:
  3.2 2.1 all_gather.3
  5.3 5.4 %conditional.16 = (bf16[2,6,128,320]{2,3,1,0:T(8,128)(2,1)S(1)}, f32[2,6,128,320]{2,3,1,0:T(8,128)}) conditional(s32[]{:T(128)} %convert_element_type.116, bf16[2,6,128,320]{2,3,1,0:T(8,128)(2,1)} %collective-permute-done, (f32[2,6,512]{2,0,1:T(2,128)S(1)}, bf16[4,320]{1,0:T(4,128)(2,1)}) %tuple.61), branch_computations={%region_0.2_spmd, %region_2.4_spmd} | conditional | flops 7872000 | bytes 5016080
  6.3 2.5 %multiply_reduce_fusion = (f32[2,6,128]{2,1,0:T(8,128)S(1)}, f32[2,6,128,320]{2,3,1,0:T(8,128)}) fusion(bf16[4,320]{1,0:T(4,128)(2,1)} %get-tuple-element.98, bf16[2,6,128,4]{3,2,0,1:T(8,128)(2,1)S(1)} %convert_element_type.87), kind=kOutput, calls=%fused_computation.10 | convolution fusion | flops 4913664 | bytes 1987072 | tf_op jit(solution)/shard_map/cond/branch_1_fun/fhwc,co->fhwo/dot_general | solution.py:126
  8.7 2.1 divide_multiply_fusion
  10.8 4.6 %collective-permute-start.1 = (bf16[2,1,128,320]{2,3,1,0:T(8,128)(2,1)S(1)}, bf16[2,1,128,320]{2,3,1,0:T(8,128)(2,1)S(1)}, u32[]{:S(2)}, u32[]{:S(2)}) collective-permute-start(bf16[2,1,128,320]{2,3,1,0:T(8,128)(2,1)S(1)} %get-tuple-element.307), channel_id=1, source_target_pairs={{0,1},{1,2},{2,3},{3,4},{4,5},{5,6},{6,7},{8,9},{9,10},{10,11},{11... | collective-permute-start | bytes 491528 | tf_op jit(solution)/shard_map/ppermute | solution.py:18
  18.6 4.1 %collective-permute-done.2 = bf16[2,1,128,320]{2,3,1,0:T(8,128)(2,1)S(1)} collective-permute-done((bf16[2,1,128,320]{2,3,1,0:T(8,128)(2,1)S(1)}, bf16[2,1,128,320]{2,3,1,0:T(8,128)(2,1)S(1)}, u32[]{:S(2)}, u32[]{:S(2)}) %collective-permute-start.2) | collective-permute-done | bytes 163872 | tf_op jit(solution)/shard_map/ppermute | solution.py:19
  22.9 39.1 %conditional.17 = (bf16[2,6,128,320]{3,0,2,1:T(2,128)(2,1)S(1)}, f32[2,6,128,320]{3,2,1,0:T(8,128)}, bf16[2,6,128,320]{3,2,1,0:T(8,128)(2,1)}, bf16[2,6,128,320]{2,3,1,0:T(8,128)(2,1)}) conditional(s32[]{:T(128)} %convert_element_type.116, (bf16[2,8,128,320]{2,3,1,0:T(8,128)(2,1)S(1)}, bf16[3,3,320,640]{3,2,1,0:T(8,128)(2,1)}, f32[1280]{0:T(1024)S(1)}, ...), branch_computations={%region_4.6_spmd, %region_6.8_spmd} | conditional | flops 3473573376 | bytes 85471832 | solution.py:162
  30.3 4.2 %copy.85 = bf16[3,3,320,320]{2,3,1,0:T(8,128)(2,1)} copy(bf16[3,3,320,320]{3,2,1,0:T(8,128)(2,1)} %get-tuple-element.251) | data formatting | bytes 3686400 | tf_op jit(solution)/shard_map
  41.6 4.1 %add_convert_fusion = bf16[2,6,128,320]{2,3,1,0:T(8,128)(2,1)} fusion(f32[2,6,128,320]{2,3,1,0:T(8,128)} %get-tuple-element.104, f32[2,6,128,320]{2,3,1,0:T(8,128)S(1)} %fusion.52, f32[2,6,128,320]{2,3,1,0:T(8,128)S(1)} %fusion.51, f32[2,6,128,320]{2,3,1,0:T(8,128)S(1)} %fusion.50, f32[2,6,128,320]{2,3,1,0:T(8,128)S(1)} %fusion.54, ...), kind=kOutput, calls=%fused_computation.72 | convolution fusion | flops 319979520 | bytes 20236288 | tf_op jit(solution)/shard_map/cond/branch_1_fun/fhwc,co->fhwo/dot_general | solution.py:48
  45.7 3.6 %copy.76 = bf16[2,6,128,320]{3,0,2,1:T(2,128)(2,1)S(1)} copy(bf16[2,6,128,320]{2,3,1,0:T(8,128)(2,1)} %add_convert_fusion) | data formatting | bytes 1966080 | tf_op jit(solution)/shard_map
  51.0 2.4 copy.87
  53.4 2.4 multiply_reduce_fusion.2
  58.9 3.0 %copy.77 = f32[2,6,128,320]{3,2,1,0:T(8,128)} copy(f32[2,6,128,320]{2,3,1,0:T(8,128)} %copy-done.6) | data formatting | bytes 3932160 | tf_op jit(solution)/shard_map
  63.7 4.3 %collective-permute-start.3 = (bf16[2,1,128,320]{2,3,1,0:T(8,128)(2,1)S(1)}, bf16[2,1,128,320]{2,3,1,0:T(8,128)(2,1)S(1)}, u32[]{:S(2)}, u32[]{:S(2)}) collective-permute-start(bf16[2,1,128,320]{2,3,1,0:T(8,128)(2,1)S(1)} %get-tuple-element.305), channel_id=1, source_target_pairs={{0,1},{1,2},{2,3},{3,4},{4,5},{5,6},{6,7},{8,9},{9,10},{10,11},{11... | collective-permute-start | bytes 491528 | tf_op jit(solution)/shard_map/ppermute | solution.py:18
  70.0 11.8 %collective-permute-start.7 = (bf16[2,6,128,320]{2,3,1,0:T(8,128)(2,1)}, bf16[2,6,128,320]{2,3,1,0:T(8,128)(2,1)}, u32[]{:S(2)}, u32[]{:S(2)}) collective-permute-start(bf16[2,6,128,320]{2,3,1,0:T(8,128)(2,1)} %get-tuple-element.279), channel_id=1, source_target_pairs={{0,8},{8,0},{1,9},{9,1},{2,10},{10,2},{3,11},{11,3},{4,12},{12,4},... | collective-permute-start | bytes 2949128 | tf_op jit(solution)/shard_map/ppermute | solution.py:27
  83.3 33.3 %conditional.18 = (bf16[2,6,128,320]{2,3,1,0:T(8,128)(2,1)S(1)}) conditional(s32[]{:T(128)} %convert_element_type.116, () %tuple.60, (bf16[2,8,128,320]{2,3,1,0:T(8,128)(2,1)S(1)}, bf16[3,3,320,320]{3,2,1,0:T(8,128)(2,1)}, f32[2,6,128,320]{3,2,1,0:T(8,128)}, f32[1280]{0:T(1024)S(1)}) %tuple.64), branch_computations={%region_8.9_spmd, %region_9.11_spmd} | conditional | flops 2840004096 | bytes 66383652 | solution.py:176
  83.7 4.2 %copy.91 = bf16[3,3,320,320]{2,3,1,0:T(8,128)(2,1)} copy(bf16[3,3,320,320]{3,2,1,0:T(8,128)(2,1)} %get-tuple-element.258) | data formatting | bytes 3686400 | tf_op jit(solution)/shard_map
  87.9 3.2 %fusion.66 = f32[2,6,128,320]{2,3,1,0:T(8,128)} fusion(bf16[2,8,128,320]{2,3,1,0:T(8,128)(2,1)S(1)} %get-tuple-element.112, bf16[3,3,320,320]{2,3,1,0:T(8,128)(2,1)} %copy.91), kind=kOutput, calls=%fused_computation.111 | convolution fusion | flops 314572800 | bytes 3522560 | tf_op jit(solution)/shard_map/cond/branch_1_fun/fhwc,co->fhwo/dot_general | solution.py:48
  91.1 2.1 fusion.67
  93.1 2.1 fusion.68
  95.2 2.1 fusion.69
  97.3 2.1 fusion.70
  105.3 3.0 %copy.92 = f32[2,6,128,320]{2,3,1,0:T(8,128)} copy(f32[2,6,128,320]{3,2,1,0:T(8,128)} %get-tuple-element.259) | data formatting | bytes 3932160 | tf_op jit(solution)/shard_map
  108.4 7.6 %multiply_reduce_fusion.3 = (f32[2,6,128]{2,1,0:T(8,128)S(1)}, f32[2,6,128,320]{2,3,1,0:T(8,128)S(1)}) fusion(f32[320]{0:T(512)S(1)} %slice.436, f32[2,6,128,320]{2,3,1,0:T(8,128)} %copy.92, bf16[2,8,128,320]{2,3,1,0:T(8,128)(2,1)S(1)} %get-tuple-element.112, bf16[3,3,320,320]{2,3,1,0:T(8,128)(2,1)} %copy.91, f32[2,6,128,320]{2,3,1,0:T(8,128)} %fusion.71, ...), kind=kOutput, calls=%fused_computation.109 | convolution fusion | flops 320469504 | bytes 21224704 | tf_op jit(solution)/shard_map/cond/branch_1_fun/fhwc,co->fhwo/dot_general | solution.py:48
  116.6 5.7 %collective-permute-start.5 = (bf16[2,1,128,320]{2,3,1,0:T(8,128)(2,1)S(1)}, bf16[2,1,128,320]{2,3,1,0:T(8,128)(2,1)S(1)}, u32[]{:S(2)}, u32[]{:S(2)}) collective-permute-start(bf16[2,1,128,320]{2,3,1,0:T(8,128)(2,1)S(1)} %get-tuple-element.303), channel_id=1, source_target_pairs={{0,1},{1,2},{2,3},{3,4},{4,5},{5,6},{6,7},{8,9},{9,10},{10,11},{11... | collective-permute-start | bytes 491528 | tf_op jit(solution)/shard_map/ppermute | solution.py:18
  125.1 5.0 %collective-permute-done.6 = bf16[2,1,128,320]{2,3,1,0:T(8,128)(2,1)S(1)} collective-permute-done((bf16[2,1,128,320]{2,3,1,0:T(8,128)(2,1)S(1)}, bf16[2,1,128,320]{2,3,1,0:T(8,128)(2,1)S(1)}, u32[]{:S(2)}, u32[]{:S(2)}) %collective-permute-start.6) | collective-permute-done | bytes 163872 | tf_op jit(solution)/shard_map/ppermute | solution.py:19
  135.4 4.9 %conditional.19 = (bf16[2,6,128,320]{2,3,1,0:T(8,128)(2,1)S(1)}, f32[2,6,128,320]{2,3,1,0:T(8,128)}) conditional(s32[]{:T(128)} %convert_element_type.116, bf16[2,6,128,320]{2,3,1,0:T(8,128)(2,1)} %collective-permute-done.7, (f32[2,6,512]{2,0,1:T(2,128)S(1)}, bf16[4,320]{1,0:T(4,128)(2,1)S(1)}) %tuple.134), branch_computations={%region_11.13_spmd, %region_13.15_spmd} | conditional | flops 7872000 | bytes 5016080
  138.2 2.1 divide_multiply_fusion.1
  140.3 4.8 %collective-permute-start.8 = (bf16[2,1,128,320]{2,3,1,0:T(8,128)(2,1)S(1)}, bf16[2,1,128,320]{2,3,1,0:T(8,128)(2,1)S(1)}, u32[]{:S(2)}, u32[]{:S(2)}) collective-permute-start(bf16[2,1,128,320]{2,3,1,0:T(8,128)(2,1)S(1)} %get-tuple-element.301), channel_id=1, source_target_pairs={{0,1},{1,2},{2,3},{3,4},{4,5},{5,6},{6,7},{8,9},{9,10},{10,11},{11... | collective-permute-start | bytes 491528 | tf_op jit(solution)/shard_map/ppermute | solution.py:18
  148.0 4.4 %collective-permute-done.9 = bf16[2,1,128,320]{2,3,1,0:T(8,128)(2,1)S(1)} collective-permute-done((bf16[2,1,128,320]{2,3,1,0:T(8,128)(2,1)S(1)}, bf16[2,1,128,320]{2,3,1,0:T(8,128)(2,1)S(1)}, u32[]{:S(2)}, u32[]{:S(2)}) %collective-permute-start.9) | collective-permute-done | bytes 163872 | tf_op jit(solution)/shard_map/ppermute | solution.py:19
  153.7 26.2 %conditional.20 = (f32[2,6,128,320]{3,2,1,0:T(8,128)}, bf16[2,6,128,320]{3,2,1,0:T(8,128)(2,1)}, bf16[1,2,6,128,320]{3,4,2,1,0:T(8,128)(2,1)}) conditional(s32[]{:T(128)} %convert_element_type.116, (bf16[2,8,128,320]{2,3,1,0:T(8,128)(2,1)S(1)}, bf16[3,3,320,640]{3,2,1,0:T(8,128)(2,1)}, f32[1280]{0:T(1024)S(1)}, bf16[3,640,640]{2,1,0:T(8,128)(2,1)}, ...), branch_computations={%region_15.17_spmd, %region_17.19_spmd} | conditional | flops 3473573376 | bytes 81212008 | solution.py:162
  154.0 4.2 %copy.98 = bf16[3,3,320,320]{2,3,1,0:T(8,128)(2,1)} copy(bf16[3,3,320,320]{3,2,1,0:T(8,128)(2,1)} %get-tuple-element.270) | data formatting | bytes 3686400 | tf_op jit(solution)/shard_map
  165.2 4.1 %fusion.130 = bf16[1,2,6,128,320]{3,4,2,1,0:T(8,128)(2,1)} fusion(f32[2,6,128,320]{2,3,1,0:T(8,128)} %get-tuple-element.125, f32[2,6,128,320]{2,3,1,0:T(8,128)S(1)} %fusion.136, f32[2,6,128,320]{2,3,1,0:T(8,128)S(1)} %fusion.135, f32[2,6,128,320]{2,3,1,0:T(8,128)S(1)} %fusion.134, f32[2,6,128,320]{2,3,1,0:T(8,128)S(1)} %fusion.138, ...), kind=kOutput, calls=%fused_computation.211 | convolution fusion | flops 319979520 | bytes 20236288 | tf_op jit(solution)/shard_map/cond/branch_1_fun/fhwc,co->fhwo/dot_general | solution.py:48
  169.4 2.4 copy.96
  175.6 2.4 copy.82
  181.7 2.9 %collective-permute-start.10 = (bf16[2,1,128,320]{2,3,1,0:T(8,128)(2,1)S(1)}, bf16[2,1,128,320]{2,3,1,0:T(8,128)(2,1)S(1)}, u32[]{:S(2)}, u32[]{:S(2)}) collective-permute-start(bf16[2,1,128,320]{2,3,1,0:T(8,128)(2,1)S(1)} %get-tuple-element.299), channel_id=1, source_target_pairs={{0,1},{1,2},{2,3},{3,4},{4,5},{5,6},{6,7},{8,9},{9,10},{10,11},{11... | collective-permute-start | bytes 491528 | tf_op jit(solution)/shard_map/ppermute | solution.py:18
  187.4 4.4 %collective-permute-done.11 = bf16[2,1,128,320]{2,3,1,0:T(8,128)(2,1)S(1)} collective-permute-done((bf16[2,1,128,320]{2,3,1,0:T(8,128)(2,1)S(1)}, bf16[2,1,128,320]{2,3,1,0:T(8,128)(2,1)S(1)}, u32[]{:S(2)}, u32[]{:S(2)}) %collective-permute-start.11) | collective-permute-done | bytes 163872 | tf_op jit(solution)/shard_map/ppermute | solution.py:19
  192.0 33.2 %conditional.21 = (bf16[2,6,128,320]{2,3,1,0:T(8,128)(2,1)S(1)}) conditional(s32[]{:T(128)} %convert_element_type.116, () %tuple.65, (bf16[2,8,128,320]{2,3,1,0:T(8,128)(2,1)S(1)}, bf16[3,3,320,320]{3,2,1,0:T(8,128)(2,1)}, f32[2,6,128,320]{3,2,1,0:T(8,128)}, f32[1280]{0:T(1024)S(1)}) %tuple.69), branch_computations={%region_19.20_spmd, %region_20.22_spmd} | conditional | flops 2840004096 | bytes 66383652 | solution.py:176
  192.3 4.2 %copy.102 = bf16[3,3,320,320]{2,3,1,0:T(8,128)(2,1)} copy(bf16[3,3,320,320]{3,2,1,0:T(8,128)(2,1)} %get-tuple-element.274) | data formatting | bytes 3686400 | tf_op jit(solution)/shard_map
  196.5 3.2 %fusion.150 = f32[2,6,128,320]{2,3,1,0:T(8,128)} fusion(bf16[2,8,128,320]{2,3,1,0:T(8,128)(2,1)S(1)} %get-tuple-element.130, bf16[3,3,320,320]{2,3,1,0:T(8,128)(2,1)} %copy.102), kind=kOutput, calls=%fused_computation.250 | convolution fusion | flops 314572800 | bytes 3522560 | tf_op jit(solution)/shard_map/cond/branch_1_fun/fhwc,co->fhwo/dot_general | solution.py:48
  199.6 2.1 fusion.151
  201.7 2.1 fusion.152
  203.8 2.1 fusion.153
  205.9 2.1 fusion.154
  213.9 3.0 %copy.103 = f32[2,6,128,320]{2,3,1,0:T(8,128)} copy(f32[2,6,128,320]{3,2,1,0:T(8,128)} %get-tuple-element.275) | data formatting | bytes 3932160 | tf_op jit(solution)/shard_map
  217.0 7.6 %multiply_reduce_fusion.7 = (f32[2,6,128]{2,1,0:T(8,128)S(1)}, f32[2,6,128,320]{2,3,1,0:T(8,128)S(1)}) fusion(f32[320]{0:T(512)S(1)} %slice.498, f32[2,6,128,320]{2,3,1,0:T(8,128)} %copy.103, bf16[2,8,128,320]{2,3,1,0:T(8,128)(2,1)S(1)} %get-tuple-element.130, bf16[3,3,320,320]{2,3,1,0:T(8,128)(2,1)} %copy.102, f32[2,6,128,320]{2,3,1,0:T(8,128)} %fusion.155, ...), kind=kOutput, calls=%fused_computation.248 | convolution fusion | flops 320469504 | bytes 21224704 | tf_op jit(solution)/shard_map/cond/branch_1_fun/fhwc,co->fhwo/dot_general | solution.py:48
  225.2 4.8 %collective-permute-start.12 = (bf16[2,1,128,320]{2,3,1,0:T(8,128)(2,1)S(1)}, bf16[2,1,128,320]{2,3,1,0:T(8,128)(2,1)S(1)}, u32[]{:S(2)}, u32[]{:S(2)}) collective-permute-start(bf16[2,1,128,320]{2,3,1,0:T(8,128)(2,1)S(1)} %get-tuple-element.297), channel_id=1, source_target_pairs={{0,1},{1,2},{2,3},{3,4},{4,5},{5,6},{6,7},{8,9},{9,10},{10,11},{11... | collective-permute-start | bytes 491528 | tf_op jit(solution)/shard_map/ppermute | solution.py:18
  232.9 4.4 %collective-permute-done.13 = bf16[2,1,128,320]{2,3,1,0:T(8,128)(2,1)S(1)} collective-permute-done((bf16[2,1,128,320]{2,3,1,0:T(8,128)(2,1)S(1)}, bf16[2,1,128,320]{2,3,1,0:T(8,128)(2,1)S(1)}, u32[]{:S(2)}, u32[]{:S(2)}) %collective-permute-start.13) | collective-permute-done | bytes 163872 | tf_op jit(solution)/shard_map/ppermute | solution.py:19
  (141 shorter events, 78.6 us)
Async XLA Ops:
  0.6 16.2 %copy-start = (bf16[320,1280]{1,0:T(8,128)(2,1)S(1)}, bf16[320,1280]{1,0:T(8,128)(2,1)}, u32[]{:S(2)}) copy-start(bf16[320,1280]{1,0:T(8,128)(2,1)} %param.35) | copy-start | bytes 2457604
  0.6 4.7 %collective-permute-start = (bf16[2,6,128,320]{2,3,1,0:T(8,128)(2,1)}, bf16[2,6,128,320]{2,3,1,0:T(8,128)(2,1)}, u32[]{:S(2)}, u32[]{:S(2)}) collective-permute-start(bf16[2,6,128,320]{2,3,1,0:T(8,128)(2,1)} %bitcast.599), channel_id=1, source_target_pairs={{0,8},{8,0},{1,9},{9,1},{2,10},{10,2},{3,11},{11,3},{4,12},{12,4},... | collective-permute-start | bytes 2949128 | tf_op jit(solution)/shard_map/ppermute | solution.py:27
  10.8 7.7 %collective-permute-start.1 = (bf16[2,1,128,320]{2,3,1,0:T(8,128)(2,1)S(1)}, bf16[2,1,128,320]{2,3,1,0:T(8,128)(2,1)S(1)}, u32[]{:S(2)}, u32[]{:S(2)}) collective-permute-start(bf16[2,1,128,320]{2,3,1,0:T(8,128)(2,1)S(1)} %get-tuple-element.307), channel_id=1, source_target_pairs={{0,1},{1,2},{2,3},{3,4},{4,5},{5,6},{6,7},{8,9},{9,10},{10,11},{11... | collective-permute-start | bytes 491528 | tf_op jit(solution)/shard_map/ppermute | solution.py:18
  15.4 7.3 %collective-permute-start.2 = (bf16[2,1,128,320]{2,3,1,0:T(8,128)(2,1)S(1)}, bf16[2,1,128,320]{2,3,1,0:T(8,128)(2,1)S(1)}, u32[]{:S(2)}, u32[]{:S(2)}) collective-permute-start(bf16[2,1,128,320]{2,3,1,0:T(8,128)(2,1)S(1)} %get-tuple-element.308), channel_id=1, source_target_pairs={{1,0},{2,1},{3,2},{4,3},{5,4},{6,5},{7,6},{9,8},{10,9},{11,10},{12... | collective-permute-start | bytes 491528 | tf_op jit(solution)/shard_map/ppermute | solution.py:19
  34.5 1.9 copy-start.4
  55.7 1.3 copy-start.6
  63.6 18.2 %copy-start.7 = (bf16[2,6,128,320]{2,3,1,0:T(8,128)(2,1)}, bf16[2,6,128,320]{2,3,1,0:T(8,128)(2,1)S(1)}, u32[]{:S(2)}) copy-start(bf16[2,6,128,320]{2,3,1,0:T(8,128)(2,1)S(1)} %copy.88) | copy-start | bytes 2949124
  63.7 18.1 %collective-permute-start.3 = (bf16[2,1,128,320]{2,3,1,0:T(8,128)(2,1)S(1)}, bf16[2,1,128,320]{2,3,1,0:T(8,128)(2,1)S(1)}, u32[]{:S(2)}, u32[]{:S(2)}) collective-permute-start(bf16[2,1,128,320]{2,3,1,0:T(8,128)(2,1)S(1)} %get-tuple-element.305), channel_id=1, source_target_pairs={{0,1},{1,2},{2,3},{3,4},{4,5},{5,6},{6,7},{8,9},{9,10},{10,11},{11... | collective-permute-start | bytes 491528 | tf_op jit(solution)/shard_map/ppermute | solution.py:18
  68.0 13.8 %collective-permute-start.4 = (bf16[2,1,128,320]{2,3,1,0:T(8,128)(2,1)S(1)}, bf16[2,1,128,320]{2,3,1,0:T(8,128)(2,1)}, u32[]{:S(2)}, u32[]{:S(2)}) collective-permute-start(bf16[2,1,128,320]{2,3,1,0:T(8,128)(2,1)S(1)} %get-tuple-element.306), channel_id=1, source_target_pairs={{1,0},{2,1},{3,2},{4,3},{5,4},{6,5},{7,6},{9,8},{10,9},{11,10},{12... | collective-permute-start | bytes 491528 | tf_op jit(solution)/shard_map/ppermute | solution.py:19
  70.0 65.4 %collective-permute-start.7 = (bf16[2,6,128,320]{2,3,1,0:T(8,128)(2,1)}, bf16[2,6,128,320]{2,3,1,0:T(8,128)(2,1)}, u32[]{:S(2)}, u32[]{:S(2)}) collective-permute-start(bf16[2,6,128,320]{2,3,1,0:T(8,128)(2,1)} %get-tuple-element.279), channel_id=1, source_target_pairs={{0,8},{8,0},{1,9},{9,1},{2,10},{10,2},{3,11},{11,3},{4,12},{12,4},... | collective-permute-start | bytes 2949128 | tf_op jit(solution)/shard_map/ppermute | solution.py:27
  87.9 3.2 %copy-start.2 = (bf16[3,3,320,320]{2,3,1,0:T(8,128)(2,1)S(1)}, bf16[3,3,320,320]{2,3,1,0:T(8,128)(2,1)}, u32[]{:S(2)}) copy-start(bf16[3,3,320,320]{2,3,1,0:T(8,128)(2,1)} %copy.91) | copy-start | bytes 5529604 | tf_op jit(solution)/shard_map/cond
  116.6 8.5 %collective-permute-start.5 = (bf16[2,1,128,320]{2,3,1,0:T(8,128)(2,1)S(1)}, bf16[2,1,128,320]{2,3,1,0:T(8,128)(2,1)S(1)}, u32[]{:S(2)}, u32[]{:S(2)}) collective-permute-start(bf16[2,1,128,320]{2,3,1,0:T(8,128)(2,1)S(1)} %get-tuple-element.303), channel_id=1, source_target_pairs={{0,1},{1,2},{2,3},{3,4},{4,5},{5,6},{6,7},{8,9},{9,10},{10,11},{11... | collective-permute-start | bytes 491528 | tf_op jit(solution)/shard_map/ppermute | solution.py:18
  122.3 7.8 %collective-permute-start.6 = (bf16[2,1,128,320]{2,3,1,0:T(8,128)(2,1)S(1)}, bf16[2,1,128,320]{2,3,1,0:T(8,128)(2,1)S(1)}, u32[]{:S(2)}, u32[]{:S(2)}) collective-permute-start(bf16[2,1,128,320]{2,3,1,0:T(8,128)(2,1)S(1)} %get-tuple-element.304), channel_id=1, source_target_pairs={{1,0},{2,1},{3,2},{4,3},{5,4},{6,5},{7,6},{9,8},{10,9},{11,10},{12... | collective-permute-start | bytes 491528 | tf_op jit(solution)/shard_map/ppermute | solution.py:19
  124.5 7.3 %copy-start.11 = (bf16[3,3,320,4]{2,3,1,0:T(4,128)(2,1)S(1)}, bf16[3,3,320,4]{2,3,1,0:T(4,128)(2,1)}, u32[]{:S(2)}) copy-start(bf16[3,3,320,4]{2,3,1,0:T(4,128)(2,1)} %param.34) | copy-start | bytes 69124
  133.8 1.5 copy-start.10
  140.3 7.7 %copy-start.8 = (bf16[2,6,128,320]{2,3,1,0:T(8,128)(2,1)}, bf16[2,6,128,320]{2,3,1,0:T(8,128)(2,1)S(1)}, u32[]{:S(2)}) copy-start(bf16[2,6,128,320]{2,3,1,0:T(8,128)(2,1)S(1)} %get-tuple-element.150) | copy-start | bytes 2949124
  140.3 7.6 %collective-permute-start.8 = (bf16[2,1,128,320]{2,3,1,0:T(8,128)(2,1)S(1)}, bf16[2,1,128,320]{2,3,1,0:T(8,128)(2,1)S(1)}, u32[]{:S(2)}, u32[]{:S(2)}) collective-permute-start(bf16[2,1,128,320]{2,3,1,0:T(8,128)(2,1)S(1)} %get-tuple-element.301), channel_id=1, source_target_pairs={{0,1},{1,2},{2,3},{3,4},{4,5},{5,6},{6,7},{8,9},{9,10},{10,11},{11... | collective-permute-start | bytes 491528 | tf_op jit(solution)/shard_map/ppermute | solution.py:18
  145.2 7.2 %collective-permute-start.9 = (bf16[2,1,128,320]{2,3,1,0:T(8,128)(2,1)S(1)}, bf16[2,1,128,320]{2,3,1,0:T(8,128)(2,1)S(1)}, u32[]{:S(2)}, u32[]{:S(2)}) collective-permute-start(bf16[2,1,128,320]{2,3,1,0:T(8,128)(2,1)S(1)} %get-tuple-element.302), channel_id=1, source_target_pairs={{1,0},{2,1},{3,2},{4,3},{5,4},{6,5},{7,6},{9,8},{10,9},{11,10},{12... | collective-permute-start | bytes 491528 | tf_op jit(solution)/shard_map/ppermute | solution.py:19
  158.2 1.9 copy-start.5
  169.4 2.6 %copy-start.17 = (bf16[640,320]{0,1:T(8,128)(2,1)S(1)}, bf16[640,320]{0,1:T(8,128)(2,1)}, u32[]{:S(2)}) copy-start(bf16[640,320]{0,1:T(8,128)(2,1)} %get-tuple-element.124) | copy-start | bytes 1228804 | tf_op jit(solution)/shard_map/cond
  171.8 1.3 copy-start.9
  181.7 5.8 %collective-permute-start.10 = (bf16[2,1,128,320]{2,3,1,0:T(8,128)(2,1)S(1)}, bf16[2,1,128,320]{2,3,1,0:T(8,128)(2,1)S(1)}, u32[]{:S(2)}, u32[]{:S(2)}) collective-permute-start(bf16[2,1,128,320]{2,3,1,0:T(8,128)(2,1)S(1)} %get-tuple-element.299), channel_id=1, source_target_pairs={{0,1},{1,2},{2,3},{3,4},{4,5},{5,6},{6,7},{8,9},{9,10},{10,11},{11... | collective-permute-start | bytes 491528 | tf_op jit(solution)/shard_map/ppermute | solution.py:18
  184.6 7.2 %collective-permute-start.11 = (bf16[2,1,128,320]{2,3,1,0:T(8,128)(2,1)S(1)}, bf16[2,1,128,320]{2,3,1,0:T(8,128)(2,1)S(1)}, u32[]{:S(2)}, u32[]{:S(2)}) collective-permute-start(bf16[2,1,128,320]{2,3,1,0:T(8,128)(2,1)S(1)} %get-tuple-element.300), channel_id=1, source_target_pairs={{1,0},{2,1},{3,2},{4,3},{5,4},{6,5},{7,6},{9,8},{10,9},{11,10},{12... | collective-permute-start | bytes 491528 | tf_op jit(solution)/shard_map/ppermute | solution.py:19
  192.0 39.4 %copy-start.12 = (bf16[3,3,320,4]{2,3,1,0:T(4,128)(2,1)S(1)}, bf16[3,3,320,4]{2,3,1,0:T(4,128)(2,1)}, u32[]{:S(2)}) copy-start(bf16[3,3,320,4]{2,3,1,0:T(4,128)(2,1)} %param.34) | copy-start | bytes 69124
  196.5 3.2 %copy-start.3 = (bf16[3,3,320,320]{2,3,1,0:T(8,128)(2,1)S(1)}, bf16[3,3,320,320]{2,3,1,0:T(8,128)(2,1)}, u32[]{:S(2)}) copy-start(bf16[3,3,320,320]{2,3,1,0:T(8,128)(2,1)} %copy.102) | copy-start | bytes 5529604 | tf_op jit(solution)/shard_map/cond
  225.2 7.6 %collective-permute-start.12 = (bf16[2,1,128,320]{2,3,1,0:T(8,128)(2,1)S(1)}, bf16[2,1,128,320]{2,3,1,0:T(8,128)(2,1)S(1)}, u32[]{:S(2)}, u32[]{:S(2)}) collective-permute-start(bf16[2,1,128,320]{2,3,1,0:T(8,128)(2,1)S(1)} %get-tuple-element.297), channel_id=1, source_target_pairs={{0,1},{1,2},{2,3},{3,4},{4,5},{5,6},{6,7},{8,9},{9,10},{10,11},{11... | collective-permute-start | bytes 491528 | tf_op jit(solution)/shard_map/ppermute | solution.py:18
  230.0 7.2 %collective-permute-start.13 = (bf16[2,1,128,320]{2,3,1,0:T(8,128)(2,1)S(1)}, bf16[2,1,128,320]{2,3,1,0:T(8,128)(2,1)S(1)}, u32[]{:S(2)}, u32[]{:S(2)}) collective-permute-start(bf16[2,1,128,320]{2,3,1,0:T(8,128)(2,1)S(1)} %get-tuple-element.298), channel_id=1, source_target_pairs={{1,0},{2,1},{3,2},{4,3},{5,4},{6,5},{7,6},{9,8},{10,9},{11,10},{12... | collective-permute-start | bytes 491528 | tf_op jit(solution)/shard_map/ppermute | solution.py:19
  241.2 4.0 %copy-start.1 = (bf16[320,1280]{1,0:T(8,128)(2,1)S(1)}, bf16[320,1280]{1,0:T(8,128)(2,1)}, u32[]{:S(2)}) copy-start(bf16[320,1280]{1,0:T(8,128)(2,1)} %param.35) | copy-start | bytes 2457604
  242.5 2.1 collective-permute-start.14
where the time goes:
time: 250 us; the launch traced here: 245 us
  matrix products  86.9 us (35%)
  local copies, waits for them, and re-layouts  52.4 us (21%)
  starting transfers between devices  48.6 us (19%)
  waiting for transfers between devices  29.2 us (12%)
  other arithmetic  14.8 us (6%)
  loops' own time  8.88 us (4%)
  between operations  2.59 us (1%)
    dot_general x54, matrix products, conv_rows(): jnp.einsum('fhwc,co->fhwo', window, weight[row_off, col_off], preferred_e...  78.9 us
    another operation x15, local copies, waits for them, and re-layouts  41.7 us
    ppermute x6, starting transfers between devices, with_halo(): before = lax.ppermute(last, axis, up)  27.1 us
    ppermute x6, waiting for transfers between devices, with_halo(): after = lax.ppermute(first, axis, down)  22.3 us
    ppermute x2, starting transfers between devices, swapped(): return lax.ppermute(value, axis, pairs)  12.4 us
    another operation x2, loops' own time, body(): lax.cond(first, enc_middle, mid_middle, (spread, lifted, state, other))  7.9 us
    ppermute x6, starting transfers between devices, with_halo(): after = lax.ppermute(first, axis, down)  7.75 us
    concatenate x6, other arithmetic, with_halo(): value = jnp.concatenate([before, value, after], axis=dim)  6.62 us
  transfers between devices with their start and end apart: 15, of which 11 were waited for; matrix products, arithmetic and copies ran while one was open for 17% of the time, Pallas kernels for 0%

commit v1 on v0

v1 whole, which is shorter than its diff:
```python
import functools
import math

import jax
import jax.numpy as jnp
from jax import lax
from jax.experimental import pallas as pl
from jax.experimental.pallas import tpu as pltpu
from jax.sharding import PartitionSpec as P

EPSILON = 1e-06
LANES = 128
LANE_CH = 8
F32 = jnp.float32
BF16 = jnp.bfloat16

VMEM = pl.BlockSpec(memory_space=pltpu.VMEM)
SMEM = pl.BlockSpec(memory_space=pltpu.SMEM)


def act(values):
    scale = lax.rsqrt(jnp.mean(values * values, axis=-1, keepdims=True) + EPSILON)
    half = values * (0.5 * scale)
    return half + half * jnp.tanh(half)


def dot(left, right):
    return jnp.dot(left, right, preferred_element_type=F32)


def shifted(values, by):
    count = values.shape[0]
    column = lax.broadcasted_iota(jnp.int32, values.shape, 0)
    edge = 0 if by == 1 else count - 1
    return jnp.where(column == edge, 0.0, pltpu.roll(values, by % count, 0))


def lane_shifted(values, by):
    count = values.shape[1]
    column = lax.broadcasted_iota(jnp.int32, values.shape, 1)
    edge = 0 if by == 1 else count - 1
    return jnp.where(column == edge, 0.0, pltpu.roll(values, by % count, 1))


def call(kernel, outs, in_specs, scratch=(), name=None):
    return pl.pallas_call(
        kernel,
        out_shape=[jax.ShapeDtypeStruct(s, d) for s, d in outs],
        in_specs=in_specs,
        out_specs=[VMEM] * len(outs),
        scratch_shapes=[pltpu.VMEM(s, d) for s, d in scratch],
        name=name,
    )


def prep_kernel(enc_ref, dec_ref, enc_out, dec_out):
    chans = enc_ref.shape[3]
    for src, dst in ((enc_ref, enc_out), (dec_ref, dec_out)):
        for dy in range(3):
            for dx in range(3):
                dst[dy * chans : (dy + 1) * chans, dx * chans : (dx + 1) * chans] = src[dy, dx]


def spread_rows(acat_ref, row, value, cols, chans):
    for dy in range(3):
        start = pl.multiple_of((row - dy + 2) * cols, cols)
        acat_ref[pl.ds(start, cols), dy * chans : (dy + 1) * chans] = value


def conv_sum(acc_ref, row, cols, chans):
    taps = acc_ref.at[pl.ds(pl.multiple_of(row * cols, cols), cols), :]
    return (
        taps[:, chans : 2 * chans]
        + shifted(taps[:, :chans], 1)
        + shifted(taps[:, 2 * chans :], -1)
    )


def conv_product(acat_ref, wcat_ref, acc_ref, rows, cols):
    acc_ref[...] = dot(acat_ref[2 * cols : (2 + rows) * cols, :], wcat_ref[...])


def encode_rows(read_row, w_in_ref, wcat_ref, bias_ref, edges, out_ref, lift_ref, acat_ref, acc_ref):
    count, cols, chans = out_ref.shape
    border = edges[2]

    def front(row, carry):
        lifted = lax.dot_general(
            read_row(row), w_in_ref[...], (((0,), (0,)), ((), ())), preferred_element_type=F32
        )
        lift_ref[row] = lifted
        spread_rows(acat_ref, row, act(lifted).astype(BF16), cols, chans)
        return carry

    lax.fori_loop(0, count + 2, front, 0)
    conv_product(acat_ref, wcat_ref, acc_ref, count, cols)

    def back(row, carry):
        total = lift_ref[row + 1] + conv_sum(acc_ref, row, cols, chans) + bias_ref[...]
        outside = ((row < border) & (edges[0] == 1)) | ((row >= count - border) & (edges[1] == 1))
        out_ref[row] = jnp.where(outside, 0.0, total).astype(BF16)
        return carry

    lax.fori_loop(0, count, back, 0)


def enc_first_kernel(edge_ref, x_ref, w_in_ref, wcat_ref, bias_ref, out_ref, lift_ref, acat_ref, acc_ref):
    edges = (edge_ref[0], edge_ref[1], 2)
    encode_rows(
        lambda row: x_ref[row], w_in_ref, wcat_ref, bias_ref, edges, out_ref, lift_ref, acat_ref, acc_ref
    )


def enc_last_kernel(
    edge_ref, base_ref, near_ref, up_ref, down_ref, w_in_ref, wcat_ref, bias_ref,
    out_ref, x_ref, ext_ref, lift_ref, acat_ref, acc_ref,
):
    rows = base_ref.shape[0]
    lanes = base_ref.shape[2]
    low_cols = up_ref.shape[0] - 4 * LANE_CH

    def received(ref):
        span = 2 * LANE_CH
        high = ref[low_cols : low_cols + span, :lanes].astype(F32)
        low = ref[low_cols + span : low_cols + 2 * span, :lanes].astype(F32)
        both = high + low
        return both[:LANE_CH], both[LANE_CH:]

    from_up, base_up = received(up_ref)
    from_down, base_down = received(down_ref)
    x_ref[...] = base_ref[...]
    x_ref[0] = x_ref[0] - from_up
    x_ref[rows - 1] = x_ref[rows - 1] - from_down
    ext_ref[0] = jnp.where(edge_ref[0] == 1, 0.0, base_up - near_ref[0]).astype(BF16)
    ext_ref[rows + 1] = jnp.where(edge_ref[1] == 1, 0.0, base_down - near_ref[1]).astype(BF16)
    ext_ref[1 : rows + 1] = x_ref[...].astype(BF16)
    encode_rows(
        lambda row: ext_ref[row], w_in_ref, wcat_ref, bias_ref, (edge_ref[0], edge_ref[1], 0),
        out_ref, lift_ref, acat_ref, acc_ref,
    )


def down_kernel(enc_ref, w_ref, bias_ref, low_ref, q_ref, gate_ref, acat_ref, *, first):
    cols, chans = enc_ref.shape[1:]
    half = cols // 2
    low_rows = low_ref.shape[0] // half
    spare = jnp.zeros((half, chans), F32)
    column = lax.broadcasted_iota(jnp.int32, spare.shape, 0)
    for row in range(2 * low_rows + 1):
        gate = act(enc_ref[first + row].astype(F32))
        for start in range(0, chans, LANES):
            wide = min(LANES, chans - start)
            gate_ref[row, start // LANES, :, :wide] = gate[:, start : start + wide]
        even, odd = (
            jnp.concatenate(
                [
                    gate_ref[row, start // LANES, pl.ds(offset, half, stride=2), :][:, : chans - start]
                    for start in range(0, chans, LANES)
                ],
                axis=1,
            )
            for offset in range(2)
        )
        before = jnp.where(column == 0, 0.0, pltpu.roll(odd, 1, 0))
        for dy in range(3):
            if (row - dy) % 2 or not 0 <= (row - dy) // 2 < low_rows:
                continue
            low = (row - dy) // 2
            for dx, part in enumerate((before, even, odd)):
                lane = (3 * dy + dx) * chans
                acat_ref[low * half : (low + 1) * half, lane : lane + chans] = part.astype(BF16)
    low_ref[...] = dot(acat_ref[...], w_ref[...]) + bias_ref[...]
    q_ref[...] = act(low_ref[...]).astype(BF16)


def raise_rows(pick_ref, low_ref, q_ref, other_ref, w_tmid_ref, w_up_ref):
    mixed = low_ref[...] + dot(q_ref[...], w_tmid_ref[1]) + dot(other_ref[...], w_tmid_ref[pick_ref[0]])
    return dot(mixed.astype(BF16), w_up_ref[...]).astype(BF16)


def mid_first_kernel(
    pick_ref, low_ref, q_ref, other_ref, w_tmid_ref, w_up_ref, base_ref, near_ref,
    raised_ref, up_ref, down_ref,
):
    raised_ref[...] = raise_rows(pick_ref, low_ref, q_ref, other_ref, w_tmid_ref, w_up_ref)
    rows, _, lanes = base_ref.shape
    half = up_ref.shape[0] - 4 * LANE_CH
    total = raised_ref.shape[0]
    span = 2 * LANE_CH
    for ref, start, edge, index in ((up_ref, 0, 0, 0), (down_ref, total - half, rows - 1, 1)):
        ref[:half, :] = raised_ref[start : start + half, :]
        sent = jnp.concatenate([near_ref[index], base_ref[edge]], axis=0)
        high = sent.astype(BF16)
        ref[half : half + span, :lanes] = high
        ref[half + span :, :lanes] = (sent - high.astype(F32)).astype(BF16)


def doubling(cols, half):
    row = lax.broadcasted_iota(jnp.int32, (cols, half), 0)
    col = lax.broadcasted_iota(jnp.int32, (cols, half), 1)
    return jnp.where((row == 2 * col) | (row == 2 * col + 1), 1.0, 0.0).astype(BF16)


def mid_last_kernel(
    pick_ref, low_ref, q_ref, other_ref, w_tmid_ref, w_up_ref, out_ref, raised_ref
):
    raised_ref[...] = raise_rows(pick_ref, low_ref, q_ref, other_ref, w_tmid_ref, w_up_ref)
    rows, cols, _ = out_ref.shape
    half = cols // 2
    twice = doubling(cols, half)
    for low in range(rows // 2):
        wide = dot(twice, raised_ref[low * half : (low + 1) * half, :]).astype(BF16)
        out_ref[2 * low] = wide
        out_ref[2 * low + 1] = wide


def decode_rows(count, cols, read_mixed, wcat_ref, bias_ref, edges, w_out_ref, mixed_ref, acat_ref, acc_ref, out_rows_ref):
    chans = bias_ref.shape[1]

    def front(row, carry):
        mixed = read_mixed(row)
        mixed_ref[row] = mixed
        spread_rows(acat_ref, row, act(mixed).astype(BF16), cols, chans)
        return carry

    lax.fori_loop(0, count + 2, front, 0)
    conv_product(acat_ref, wcat_ref, acc_ref, count, cols)

    def back(row, carry):
        total = mixed_ref[row + 1] + conv_sum(acc_ref, row, cols, chans) + bias_ref[...]
        value = act(total)
        if edges is not None:
            outside = ((row == 0) & (edges[0] == 1)) | ((row == count - 1) & (edges[1] == 1))
            value = jnp.where(outside, 0.0, value)
        start = pl.multiple_of(row * cols, cols)
        out_rows_ref[pl.ds(start, cols), :] = value.astype(BF16)
        return carry

    lax.fori_loop(0, count, back, 0)
    taps = lax.dot_general(
        w_out_ref[...], out_rows_ref[...], (((1,), (1,)), ((), ())), preferred_element_type=F32
    )
    span = 3 * LANE_CH
    parts = []
    for row in range(count):
        tap = taps[:, row * cols : (row + 1) * cols]
        parts.append(
            lane_shifted(tap[:span], 1) + tap[span : 2 * span] + lane_shifted(tap[2 * span :], -1)
        )
    return parts


def tap_sum(parts, row):
    total = None
    for dy in range(3):
        source = row + dy - 1
        if 0 <= source < len(parts):
            piece = parts[source][dy * LANE_CH : (dy + 1) * LANE_CH]
            total = piece if total is None else total + piece
    return total


def dec_first_kernel(
    coef_ref, enc_ref, mid_ref, x_ref, w_skip_ref, wcat_ref, bias_ref, w_out_ref,
    base_ref, near_ref, mixed_ref, acat_ref, acc_ref, out_rows_ref,
):
    rows = base_ref.shape[0]
    cols, chans = enc_ref.shape[1:]

    def read_mixed(row):
        return dot(mid_ref[row], w_skip_ref[:chans, :]) + dot(enc_ref[row], w_skip_ref[chans:, :])

    parts = decode_rows(
        rows, cols, read_mixed, wcat_ref, bias_ref, None, w_out_ref, mixed_ref, acat_ref, acc_ref, out_rows_ref
    )
    coef = coef_ref[0]
    halo = (x_ref.shape[0] - rows) // 2
    near_ref[0] = coef * tap_sum(parts, -1)
    near_ref[1] = coef * tap_sum(parts, rows)
    for row in range(rows):
        base_ref[row] = x_ref[halo + row] - coef * tap_sum(parts, row)


def dec_last_kernel(
    edge_ref, coef_ref, enc_ref, mid_ref, up_ref, down_ref, x_ref, w_skip_ref, wcat_ref, bias_ref, w_out_ref,
    next_ref, joined_ref, mixed_ref, acat_ref, acc_ref, out_rows_ref,
):
    rows = x_ref.shape[0]
    cols, chans = enc_ref.shape[1:]
    half = cols // 2
    inner = mid_ref.shape[0] // half
    twice = doubling(cols, half)
    for low in range(inner + 2):
        if low == 0:
            piece = up_ref[:half, :]
        elif low == inner + 1:
            piece = down_ref[:half, :]
        else:
            piece = mid_ref[(low - 1) * half : low * half, :]
        joined_ref[low] = dot(twice, piece).astype(BF16)

    def read_mixed(row):
        return dot(joined_ref[row // 2], w_skip_ref[:chans, :]) + dot(enc_ref[row], w_skip_ref[chans:, :])

    parts = decode_rows(
        rows + 2, cols, read_mixed, wcat_ref, bias_ref, (edge_ref[0], edge_ref[1]), w_out_ref,
        mixed_ref, acat_ref, acc_ref, out_rows_ref,
    )
    coef = coef_ref[1]
    for row in range(rows):
        next_ref[row] = x_ref[row] - coef * tap_sum(parts, row + 1)


def time_biases(timesteps, w_time):
    half = w_time.shape[0] // 2
    freqs = jnp.exp(-math.log(10000.0) * jnp.arange(half).astype(F32) / half)
    angles = timesteps.astype(F32)[:, None] * freqs[None, :]
    embedded = jnp.concatenate([jnp.sin(angles), jnp.cos(angles)], axis=1)
    gated = jax.nn.silu(embedded).astype(BF16)
    return jnp.dot(gated, w_time, preferred_element_type=F32)


def body(latent, stale, timesteps, w_in, w_enc, w_down, w_tmid, w_up, w_skip, w_dec, w_out, w_time):
    segment = lax.axis_index("segment")
    first = segment == 0
    size = lax.axis_size("rows")
    place = lax.axis_index("rows")
    state = stale[0]
    frames, rows, cols, chans = state.shape
    mid = w_down.shape[3]
    lat = w_in.shape[0]
    half = cols // 2
    low = (rows // 2) * half
    assert frames == 2 and lax.axis_size("segment") == 2

    up_pairs = [(i + 1, i) for i in range(size - 1)]
    down_pairs = [(i, i + 1) for i in range(size - 1)]

    def swap(value):
        return lax.ppermute(value, "segment", [(0, 1), (1, 0)])

    def from_above(value):
        return lax.ppermute(value, "rows", down_pairs)

    def from_below(value):
        return lax.ppermute(value, "rows", up_pairs)

    def mine(value):
        return lax.dynamic_index_in_dim(value, segment, 0, keepdims=False)

    def theirs(value):
        return lax.dynamic_index_in_dim(value, 1 - segment, 0, keepdims=False)

    halo = 3
    edge = latent.astype(BF16)
    x_up = from_above(edge[:, rows - halo :])
    x_down = from_below(edge[:, :halo])
    x_raw = jnp.concatenate([x_up.astype(F32), latent, x_down.astype(F32)], axis=1)
    x_mine, x_other = mine(x_raw), swap(theirs(x_raw))
    x_full = jnp.where(
        first,
        jnp.concatenate([x_mine, x_other], axis=1),
        jnp.concatenate([x_other, x_mine], axis=1),
    )
    x_t = x_full.reshape(rows + 2 * halo, cols, lat).transpose(0, 2, 1)
    x_t = jnp.pad(x_t, ((0, 0), (0, LANE_CH - lat), (0, 0)))

    s_up = from_above(state[:, rows - 1 :])
    s_down = from_below(state[:, :1])
    s_raw = jnp.concatenate([s_up, state, s_down], axis=1)
    s_mine, s_other = mine(s_raw), swap(theirs(s_raw))
    enc0 = jnp.where(first, s_mine, s_other)
    mid0 = jnp.where(first, s_other, s_mine)

    biases = time_biases(timesteps, w_time)
    b_enc = biases[:, :chans]
    b_mid = biases[:, chans : chans + mid]
    b_dec = biases[:, chans + mid :]
    coefs = (timesteps.astype(F32) + 1.0) / 1000.0
    edges = jnp.stack([place == 0, place == size - 1]).astype(jnp.int32)
    pick = (2 - 2 * segment).astype(jnp.int32)[None]

    w_in8 = jnp.pad(w_in, ((0, LANE_CH - lat), (0, 0)))
    w_taps = jnp.pad(w_out.transpose(1, 0, 3, 2), ((0, 0), (0, 0), (0, LANE_CH - lat), (0, 0)))
    w_taps = w_taps.reshape(9 * LANE_CH, chans)
    w_down2 = w_down.reshape(9 * chans, mid)

    enc_cat, dec_cat = call(
        prep_kernel, [((3 * chans, 3 * chans), BF16)] * 2, [VMEM] * 2, name="prep"
    )(w_enc, w_dec)

    def enc_scratch(count):
        return [
            ((count + 2, cols, chans), F32),
            (((count + 4) * cols, 3 * chans), BF16),
            ((count * cols, 3 * chans), F32),
        ]

    def dec_scratch(count):
        return enc_scratch(count) + [((count * cols, chans), BF16)]

    ext = rows + 4
    (enc1,) = call(
        enc_first_kernel, [((ext, cols, chans), BF16)], [SMEM] + [VMEM] * 4, enc_scratch(ext), "enc_first"
    )(edges, x_t.astype(BF16), w_in8, enc_cat, b_enc[0:1])

    down_outs = [((low, mid), F32), ((low, mid), BF16)]
    down_scratch = [((rows + 1, -(-chans // LANES), cols, LANES), F32), ((low, 9 * chans), BF16)]
    low0, q0 = call(
        functools.partial(down_kernel, first=0), down_outs, [VMEM] * 3, down_scratch, "down_first"
    )(enc0, w_down2, b_mid[0:1])
    q0_other = swap(q0)

    base, near = call(
        dec_first_kernel,
        [((rows, LANE_CH, cols), F32), ((2, LANE_CH, cols), F32)],
        [SMEM] + [VMEM] * 7,
        dec_scratch(rows),
        "dec_first",
    )(coefs, enc0, mid0, x_t, w_skip, dec_cat, b_dec[0:1], w_taps)

    bundle = (half + 4 * LANE_CH, chans)
    mid1, to_up, to_down = call(
        mid_first_kernel, [((low, chans), BF16), (bundle, BF16), (bundle, BF16)], [SMEM] + [VMEM] * 7, (), "mid_first"
    )(pick, low0, q0, q0_other, w_tmid, w_up, base, near)
    got_up = from_above(to_down)
    got_down = from_below(to_up)

    low1, q1 = call(
        functools.partial(down_kernel, first=1), down_outs, [VMEM] * 3, down_scratch, "down_last"
    )(enc1, w_down2, b_mid[1:2])
    q1_other = swap(q1)

    enc2, x1 = call(
        enc_last_kernel,
        [((rows, cols, chans), BF16), ((rows, LANE_CH, cols), F32)],
        [SMEM] + [VMEM] * 7,
        [((rows + 2, LANE_CH, cols), BF16)] + enc_scratch(rows),
        "enc_last",
    )(edges, base, near, got_up, got_down, w_in8, enc_cat, b_enc[1:2])

    (mid2,) = call(
        mid_last_kernel, [((rows, cols, chans), BF16)], [SMEM] + [VMEM] * 5, [((low, chans), BF16)], "mid_last"
    )(pick, low1, q1, q1_other, w_tmid, w_up)

    feat_other = swap(jnp.where(first, mid2, enc2))

    (x2,) = call(
        dec_last_kernel,
        [((rows, LANE_CH, cols), F32)],
        [SMEM] * 2 + [VMEM] * 9,
        [((rows // 2 + 2, cols, chans), BF16)] + dec_scratch(rows + 2),
        "dec_last",
    )(edges, coefs, enc1, mid1, got_up, got_down, x1, w_skip, dec_cat, b_dec[1:2], w_taps)

    flat = x2[:, :lat].transpose(0, 2, 1).reshape(rows, cols * lat)
    halves = jnp.stack([flat[:, : cols * lat // 2], flat[:, cols * lat // 2 :]])
    x_keep, x_got = mine(halves), swap(theirs(halves))
    result = jnp.where(first, jnp.stack([x_keep, x_got]), jnp.stack([x_got, x_keep]))
    features = jnp.where(first, jnp.stack([enc2, feat_other]), jnp.stack([feat_other, mid2]))
    return (result, features[None])


def solution(mesh):
    placed = (
        P("clips", "rows", "segment"),
        P("segment", "clips", "rows", None, None),
        P("clips"),
    ) + (P(),) * 9
    return jax.shard_map(
        body,
        mesh=mesh,
        in_specs=placed,
        out_specs=(P("clips", "rows", "segment"), P("segment", "clips", "rows", None, None)),
        check_vma=False,
    )
```

time: 250 us -> 118 us (0.47); the launches traced: 245 us -> 117 us
  matrix products: 86.9 us -> 0.28 us
  Pallas kernels: 0 us -> 68.2 us
  local copies, waits for them, and re-layouts: 52.4 us -> 16 us
  starting transfers between devices: 48.6 us -> 20.1 us
  waiting for transfers between devices: 29.2 us -> 6.08 us
  other arithmetic: 14.8 us -> 5.13 us
  loops' own time: 8.88 us -> 0 us
    dot_general x60 -> x1, matrix products: 86.9 us -> 0.28 us  [time_biases(): return jnp.dot(gated, w_time, preferred_element_type=F32)]
    pallas_call x0 -> x9, Pallas kernels: none -> 68.2 us  [the longest x1 13.2 us: body(): call(dec_last_kernel, [((rows, LANE_CH, cols), F32)], [SMEM] * 2 + [VMEM]...]
    another operation x15 -> x1, local copies, waits for them, and re-layouts: 41.7 us -> 0.01 us  [body(): halves = jnp.stack([flat[:, :cols * lat // 2], flat[:, cols * lat // 2:]])]
    ppermute x15 -> x12, starting transfers between devices: 48.6 us -> 20.1 us  [the longest x3 14.2 us: from_above(): return lax.ppermute(value, 'rows', down_pairs)]
    ppermute x15 -> x12, waiting for transfers between devices: 29.2 us -> 6.08 us  [the longest x3 4.9 us: from_below(): return lax.ppermute(value, 'rows', up_pairs)]
    another operation x4 -> x0, loops' own time: 8.64 us -> none  [the longest x2 7.9 us: body(): lax.cond(first, enc_middle, mid_middle, (spread, lifted, state, other))]
    unnamed x14 -> x33, local copies, waits for them, and re-layouts: 0.04 us -> 6.98 us
    concatenate x6 -> x2, other arithmetic: 6.62 us -> 0.17 us  [the longest x1 0.16 us: body(): s_raw = jnp.concatenate([s_up, state, s_down], axis=1)]
  transfers between devices with their start and end apart: 15 -> 12, of which waited for: 11 -> 3; matrix products, arithmetic and copies ran while one was open for 17% -> 10% of each run, Pallas kernels for 0% -> 47%
where the time goes in v1:
time: 118 us; the launch traced here: 117 us
  Pallas kernels  68.2 us (58%)
  starting transfers between devices  20.1 us (17%)
  local copies, waits for them, and re-layouts  16 us (14%)
  waiting for transfers between devices  6.08 us (5%)
  other arithmetic  5.13 us (4%)
    ppermute x3, starting transfers between devices, from_above(): return lax.ppermute(value, 'rows', down_pairs)  14.2 us
    pallas_call x1, Pallas kernels, body(): call(dec_last_kernel, [((rows, LANE_CH, cols), F32)], [SMEM] * 2 + [VMEM]...  13.2 us
    pallas_call x1, Pallas kernels, body(): call(enc_first_kernel, [((ext, cols, chans), BF16)], [SMEM] + [VMEM] * 4,...  12.8 us
    pallas_call x1, Pallas kernels, body(): call(dec_first_kernel, [((rows, LANE_CH, cols), F32), ((2, LANE_CH, cols)...  10.9 us
    pallas_call x1, Pallas kernels, body(): call(enc_last_kernel, [((rows, cols, chans), BF16), ((rows, LANE_CH, cols...  9.03 us
    unnamed x33, local copies, waits for them, and re-layouts  6.98 us
    pallas_call x1, Pallas kernels, body(): call(functools.partial(down_kernel, first=1), down_outs, [VMEM] * 3, down...  4.91 us
    ppermute x3, waiting for transfers between devices, from_below(): return lax.ppermute(value, 'rows', up_pairs)  4.9 us
  transfers between devices with their start and end apart: 12, of which 3 were waited for; matrix products, arithmetic and copies ran while one was open for 10% of the time, Pallas kernels for 47%

profile of v1, /device:TPU:0, one launch (start us, length us, event | category | flops | bytes accessed | tf_op | source)
XLA Modules:
  0.0 116.6 jit_solution(17513351873311874302)
XLA Ops:
  0.7 0.8 copy.64
  1.5 4.9 %collective-permute-start = (bf16[2,3,256]{2,1,0:T(4,128)(2,1)S(1)}, bf16[2,3,256]{2,1,0:T(4,128)(2,1)S(1)}, u32[]{:S(2)}, u32[]{:S(2)}) collective-permute-start(bf16[2,3,256]{2,1,0:T(4,128)(2,1)S(1)} %get-tuple-element.52), channel_id=1, source_target_pairs={{0,1},{1,2},{2,3},{3,4},{4,5},{5,6},{6,7},{8,9},{9,10},{10,11},{11... | collective-permute-start | bytes 9224 | tf_op jit(solution)/shard_map/ppermute | solution.py:343
  6.4 1.3 %collective-permute-start.1 = (bf16[2,3,256]{2,1,0:T(4,128)(2,1)S(1)}, bf16[2,3,256]{2,1,0:T(4,128)(2,1)S(1)}, u32[]{:S(2)}, u32[]{:S(2)}) collective-permute-start(bf16[2,3,256]{2,1,0:T(4,128)(2,1)S(1)} %get-tuple-element.53), channel_id=1, source_target_pairs={{1,0},{2,1},{3,2},{4,3},{5,4},{6,5},{7,6},{9,8},{10,9},{11,10},{12... | collective-permute-start | bytes 9224 | tf_op jit(solution)/shard_map/ppermute | solution.py:346
  7.7 1.0 fusion.10
  8.7 4.6 %collective-permute-start.3 = (bf16[2,1,128,320]{2,3,1,0:T(8,128)(2,1)S(1)}, bf16[2,1,128,320]{2,3,1,0:T(8,128)(2,1)S(1)}, u32[]{:S(2)}, u32[]{:S(2)}) collective-permute-start(bf16[2,1,128,320]{2,3,1,0:T(8,128)(2,1)S(1)} %get-tuple-element.38), channel_id=1, source_target_pairs={{0,1},{1,2},{2,3},{3,4},{4,5},{5,6},{6,7},{8,9},{9,10},{10,11},{11... | collective-permute-start | bytes 491528 | tf_op jit(solution)/shard_map/ppermute | solution.py:343
  13.3 1.3 %collective-permute-start.4 = (bf16[2,1,128,320]{2,3,1,0:T(8,128)(2,1)S(1)}, bf16[2,1,128,320]{2,3,1,0:T(8,128)(2,1)S(1)}, u32[]{:S(2)}, u32[]{:S(2)}) collective-permute-start(bf16[2,1,128,320]{2,3,1,0:T(8,128)(2,1)S(1)} %get-tuple-element.39), channel_id=1, source_target_pairs={{1,0},{2,1},{3,2},{4,3},{5,4},{6,5},{7,6},{9,8},{10,9},{11,10},{12... | collective-permute-start | bytes 491528 | tf_op jit(solution)/shard_map/ppermute | solution.py:346
  14.6 0.7 convert_element_type.36
  15.4 0.3 fusion.5
  15.7 0.7 fusion.11
  16.4 4.6 %collective-permute-done.4 = bf16[2,1,128,320]{2,3,1,0:T(8,128)(2,1)S(1)} collective-permute-done((bf16[2,1,128,320]{2,3,1,0:T(8,128)(2,1)S(1)}, bf16[2,1,128,320]{2,3,1,0:T(8,128)(2,1)S(1)}, u32[]{:S(2)}, u32[]{:S(2)}) %collective-permute-start.4) | collective-permute-done | bytes 163872 | tf_op jit(solution)/shard_map/ppermute | solution.py:346
  21.4 0.7 fusion.12
  22.2 0.6 collective-permute-start.2
  22.7 0.7 add_convert_fusion.edge_ref
  23.4 0.6 pad.13.w_in_ref
  24.0 0.6 pad.14.clone
  24.6 1.0 copy.54.w_up_ref
  25.6 1.0 copy.53.w_skip_ref
  26.7 4.9 %prep.1 = (bf16[960,960]{1,0:T(8,128)(2,1)}, bf16[960,960]{1,0:T(8,128)(2,1)}) custom-call(bf16[3,3,320,320]{3,2,1,0:T(8,128)(2,1)} %enc_ref.1, bf16[3,3,320,320]{3,2,1,0:T(8,128)(2,1)} %dec_ref.1), custom_call_target="tpu_custom_call" | custom-call | tf_op jit(solution)/shard_map/prep/pallas_call | solution.py:388
  32.1 0.4 copy.49
  32.4 1.4 %copy.50 = bf16[8,128,320]{2,1,0:T(8,128)(2,1)S(1)} copy(bf16[8,128,320]{1,2,0:T(8,128)(2,1)} %collective-permute-done.5) | data formatting | bytes 1310720 | tf_op jit(solution)/shard_map/ppermute | solution.py:340
  33.9 1.3 %bitcast_select_fusion = (bf16[8,128,320]{2,1,0:T(8,128)(2,1)}, bf16[8,128,320]{2,1,0:T(8,128)(2,1)}) fusion(bf16[8,128,320]{2,1,0:T(8,128)(2,1)S(1)} %copy.50, bf16[1,8,128,320]{3,2,1,0:T(8,128)(2,1)S(1)} %copy.49, pred[]{:T(512)S(6)} %eq.9), kind=kLoop, calls=%fused_computation.2 | loop fusion | flops 655360 | bytes 2621441 | tf_op jit(solution)/shard_map/jit(_where)/select_n | solution.py:373
  35.2 4.9 %down_first.1 = (f32[192,640]{1,0:T(8,128)}, bf16[192,640]{1,0:T(8,128)(2,1)}) custom-call(bf16[8,128,320]{2,1,0:T(8,128)(2,1)} %get-tuple-element.35.enc_ref, bf16[2880,640]{1,0:T(8,128)(2,1)} %bitcast.31, f32[1,640]{1,0:T(1,128)} %get-tuple-element.47.bias_ref), custom_call_target="tpu_custom_call" | custom-call | tf_op jit(solution)/shard_map/down_first/pallas_call | solution.py:409
  40.1 0.6 pad_convert_fusion.x_ref
  40.7 12.8 %enc_first.1.enc_ref = bf16[10,128,320]{2,1,0:T(8,128)(2,1)} custom-call(s32[2]{0:T(128)} %add_convert_fusion.edge_ref, bf16[12,8,128]{2,1,0:T(8,128)(2,1)} %pad_convert_fusion.x_ref, bf16[8,320]{1,0:T(8,128)(2,1)} %pad.13.w_in_ref, bf16[960,960]{1,0:T(8,128)(2,1)} %get-tuple-element.15.wcat_ref, f32[1,320]{1,0:T(1,128)} %get-tuple-element.51.bias_ref), custom_call_target="tpu_custom_call" | custom-call | tf_op jit(solution)/shard_map/enc_first/pallas_call | solution.py:403
  53.5 4.9 %down_last.1 = (f32[192,640]{1,0:T(8,128)}, bf16[192,640]{1,0:T(8,128)(2,1)}) custom-call(bf16[10,128,320]{2,1,0:T(8,128)(2,1)} %enc_first.1.enc_ref, bf16[2880,640]{1,0:T(8,128)(2,1)} %bitcast.32, f32[1,640]{1,0:T(1,128)} %get-tuple-element.46.bias_ref), custom_call_target="tpu_custom_call" | custom-call | tf_op jit(solution)/shard_map/down_last/pallas_call | solution.py:429
  58.4 0.5 collective-permute-start.10
  58.9 0.5 add_multiply_fusion.coef_ref
  59.5 0.6 pad.12.x_ref
  60.1 10.9 %dec_first.1 = (f32[6,8,128]{2,1,0:T(8,128)}, f32[2,8,128]{2,1,0:T(8,128)}) custom-call(f32[2]{0:T(128)} %add_multiply_fusion.coef_ref, bf16[8,128,320]{2,1,0:T(8,128)(2,1)} %get-tuple-element.35.enc_ref, bf16[8,128,320]{2,1,0:T(8,128)(2,1)} %get-tuple-element.34.mid_ref, f32[12,8,128]{2,1,0:T(8,128)} %pad.12.x_ref, bf16[640,320]{1,0:T(8,128)(2,1)} %copy.53.w_skip_ref, ...), custom_call_target="tpu_custom_call" | custom-call | tf_op jit(solution)/shard_map/dec_first/pallas_call | solution.py:414
  71.0 0.7 copy-done.8
  71.7 3.6 %mid_first.1 = (bf16[192,320]{1,0:T(8,128)(2,1)}, bf16[96,320]{1,0:T(8,128)(2,1)}, bf16[96,320]{1,0:T(8,128)(2,1)}) custom-call(s32[1]{0:T(128)} %bitcast.6.pick_ref, f32[192,640]{1,0:T(8,128)} %get-tuple-element.16.low_ref, bf16[192,640]{1,0:T(8,128)(2,1)} %get-tuple-element.17.q_ref, bf16[192,640]{1,0:T(8,128)(2,1)} %copy-done.8, ...), custom_call_target="tpu_custom_call" | custom-call | tf_op jit(solution)/shard_map/mid_first/pallas_call | solution.py:423
  75.3 4.7 %collective-permute-start.7 = (bf16[96,320]{1,0:T(8,128)(2,1)}, bf16[96,320]{1,0:T(8,128)(2,1)S(1)}, u32[]{:S(2)}, u32[]{:S(2)}) collective-permute-start(bf16[96,320]{1,0:T(8,128)(2,1)} %get-tuple-element.22), channel_id=1, source_target_pairs={{0,1},{1,2},{2,3},{3,4},{4,5},{5,6},{6,7},{8,9},{9,10},{10,11},{11... | collective-permute-start | bytes 184328 | tf_op jit(solution)/shard_map/ppermute | solution.py:343
  80.1 1.5 %collective-permute-start.8 = (bf16[96,320]{1,0:T(8,128)(2,1)}, bf16[96,320]{1,0:T(8,128)(2,1)S(1)}, u32[]{:S(2)}, u32[]{:S(2)}) collective-permute-start(bf16[96,320]{1,0:T(8,128)(2,1)} %get-tuple-element.23), channel_id=1, source_target_pairs={{1,0},{2,1},{3,2},{4,3},{5,4},{6,5},{7,6},{9,8},{10,9},{11,10},{12... | collective-permute-start | bytes 184328 | tf_op jit(solution)/shard_map/ppermute | solution.py:346
  81.6 0.7 copy-done.7
  82.3 4.0 %mid_last.1 = bf16[6,128,320]{2,1,0:T(8,128)(2,1)} custom-call(s32[1]{0:T(128)} %bitcast.6.pick_ref, f32[192,640]{1,0:T(8,128)} %get-tuple-element.26.low_ref, bf16[192,640]{1,0:T(8,128)(2,1)} %get-tuple-element.27.q_ref, bf16[192,640]{1,0:T(8,128)(2,1)} %copy-done.7, bf16[3,640,640]{2,1,0:T(8,128)(2,1)} %w_tmid_ref.3, bf16[640,320]{1,0:T(8,128)(2,1)} %copy.54.w_up_ref), custom_call_target="tpu_custom_call" | custom-call | tf_op jit(solution)/shard_map/mid_last/pallas_call | solution.py:442
  86.2 0.3 collective-permute-done.8.down_ref
  86.5 0.3 copy-done.5
  86.9 0.3 copy-done.6
  87.2 9.0 %enc_last.1 = (bf16[6,128,320]{2,1,0:T(8,128)(2,1)}, f32[6,8,128]{2,1,0:T(8,128)}) custom-call(s32[2]{0:T(128)} %add_convert_fusion.edge_ref, f32[6,8,128]{2,1,0:T(8,128)} %get-tuple-element.19.base_ref, f32[2,8,128]{2,1,0:T(8,128)} %get-tuple-element.20.near_ref, bf16[96,320]{1,0:T(8,128)(2,1)} %copy-done.5, bf16[96,320]{1,0:T(8,128)(2,1)} %copy-done.6, ...), custom_call_target="tpu_custom_call" | custom-call | tf_op jit(solution)/shard_map/enc_last/pallas_call | solution.py:434
  96.3 0.3 copy.58
  96.6 0.6 collective-permute-start.11
  97.2 13.2 %dec_last.1 = f32[6,8,128]{2,1,0:T(8,128)} custom-call(s32[2]{0:T(128)} %add_convert_fusion.edge_ref, f32[2]{0:T(128)} %add_multiply_fusion.coef_ref, bf16[10,128,320]{2,1,0:T(8,128)(2,1)} %enc_first.1.enc_ref, bf16[192,320]{1,0:T(8,128)(2,1)} %get-tuple-element.21.mid_ref, bf16[96,320]{1,0:T(8,128)(2,1)} %copy-done.5, bf16[96,320]{1,0:T(8,128)(2,1)} %copy-done.6, ...), custom_call_target="tpu_custom_call" | custom-call | tf_op jit(solution)/shard_map/dec_last/pallas_call | solution.py:448
  110.4 0.7 slice_bitcast_fusion
  111.7 1.2 collective-permute-done.9
  112.9 0.6 copy.60
  113.5 0.3 copy.59
  113.8 1.4 %maximum_select_fusion = bf16[1,2,6,128,320]{4,3,2,1,0:T(8,128)(2,1)S(1)} fusion(bf16[1,1,6,128,320]{4,3,2,1,0:T(8,128)(2,1)S(1)} %bitcast.34, bf16[1,1,6,128,320]{4,3,2,1,0:T(8,128)(2,1)} %bitcast.35, bf16[1,1,6,128,320]{4,3,2,1,0:T(8,128)(2,1)S(1)} %bitcast.33, pred[]{:T(512)S(6)} %eq.9), kind=kLoop, calls=%fused_computation.1 | loop fusion | flops 1474560 | bytes 2457601 | tf_op jit(solution)/shard_map/jit(_where)/select_n | solution.py:460
  115.2 1.4 %copy.61 = bf16[1,2,6,128,320]{3,4,2,1,0:T(8,128)(2,1)} copy(bf16[1,2,6,128,320]{4,3,2,1,0:T(8,128)(2,1)S(1)} %maximum_select_fusion) | data formatting | bytes 1966080
  (56 shorter events, 1.7 us)
Async XLA Ops:
  0.6 14.8 %copy-start = (bf16[320,1280]{1,0:T(8,128)(2,1)S(1)}, bf16[320,1280]{1,0:T(8,128)(2,1)}, u32[]{:S(2)}) copy-start(bf16[320,1280]{1,0:T(8,128)(2,1)} %param.23) | copy-start | bytes 2457604
  0.6 20.3 %copy-start.2 = (bf16[1,2,6,128,320]{3,4,2,1,0:T(8,128)(2,1)S(1)}, bf16[1,2,6,128,320]{3,4,2,1,0:T(8,128)(2,1)}, u32[]{:S(2)}) copy-start(bf16[1,2,6,128,320]{3,4,2,1,0:T(8,128)(2,1)} %param.13) | copy-start | bytes 2949124
  1.5 20.6 %collective-permute-start = (bf16[2,3,256]{2,1,0:T(4,128)(2,1)S(1)}, bf16[2,3,256]{2,1,0:T(4,128)(2,1)S(1)}, u32[]{:S(2)}, u32[]{:S(2)}) collective-permute-start(bf16[2,3,256]{2,1,0:T(4,128)(2,1)S(1)} %get-tuple-element.52), channel_id=1, source_target_pairs={{0,1},{1,2},{2,3},{3,4},{4,5},{5,6},{6,7},{8,9},{9,10},{10,11},{11... | collective-permute-start | bytes 9224 | tf_op jit(solution)/shard_map/ppermute | solution.py:343
  6.4 15.7 %collective-permute-start.1 = (bf16[2,3,256]{2,1,0:T(4,128)(2,1)S(1)}, bf16[2,3,256]{2,1,0:T(4,128)(2,1)S(1)}, u32[]{:S(2)}, u32[]{:S(2)}) collective-permute-start(bf16[2,3,256]{2,1,0:T(4,128)(2,1)S(1)} %get-tuple-element.53), channel_id=1, source_target_pairs={{1,0},{2,1},{3,2},{4,3},{5,4},{6,5},{7,6},{9,8},{10,9},{11,10},{12... | collective-permute-start | bytes 9224 | tf_op jit(solution)/shard_map/ppermute | solution.py:346
  8.7 7.6 %collective-permute-start.3 = (bf16[2,1,128,320]{2,3,1,0:T(8,128)(2,1)S(1)}, bf16[2,1,128,320]{2,3,1,0:T(8,128)(2,1)S(1)}, u32[]{:S(2)}, u32[]{:S(2)}) collective-permute-start(bf16[2,1,128,320]{2,3,1,0:T(8,128)(2,1)S(1)} %get-tuple-element.38), channel_id=1, source_target_pairs={{0,1},{1,2},{2,3},{3,4},{4,5},{5,6},{6,7},{8,9},{9,10},{10,11},{11... | collective-permute-start | bytes 491528 | tf_op jit(solution)/shard_map/ppermute | solution.py:343
  13.3 7.7 %collective-permute-start.4 = (bf16[2,1,128,320]{2,3,1,0:T(8,128)(2,1)S(1)}, bf16[2,1,128,320]{2,3,1,0:T(8,128)(2,1)S(1)}, u32[]{:S(2)}, u32[]{:S(2)}) collective-permute-start(bf16[2,1,128,320]{2,3,1,0:T(8,128)(2,1)S(1)} %get-tuple-element.39), channel_id=1, source_target_pairs={{1,0},{2,1},{3,2},{4,3},{5,4},{6,5},{7,6},{9,8},{10,9},{11,10},{12... | collective-permute-start | bytes 491528 | tf_op jit(solution)/shard_map/ppermute | solution.py:346
  21.2 0.9 copy-start.9
  21.2 2.2 %copy-start.10 = (bf16[3,3,320,4]{2,3,1,0:T(4,128)(2,1)S(1)}, bf16[3,3,320,4]{2,3,1,0:T(4,128)(2,1)}, u32[]{:S(2)}) copy-start(bf16[3,3,320,4]{2,3,1,0:T(4,128)(2,1)} %param.22) | copy-start | bytes 69124
  21.2 2.2 %copy-start.11 = (bf16[4,320]{1,0:T(4,128)(2,1)S(1)}, bf16[4,320]{1,0:T(4,128)(2,1)}, u32[]{:S(2)}) copy-start(bf16[4,320]{1,0:T(4,128)(2,1)} %param.15) | copy-start | bytes 7684
  21.2 3.5 %copy-start.3 = (bf16[640,320]{0,1:T(8,128)(2,1)S(1)}, bf16[640,320]{0,1:T(8,128)(2,1)}, u32[]{:S(2)}) copy-start(bf16[640,320]{0,1:T(8,128)(2,1)} %param.19) | copy-start | bytes 1228804
  21.2 4.4 %copy-start.4 = (bf16[640,320]{0,1:T(8,128)(2,1)S(1)}, bf16[640,320]{0,1:T(8,128)(2,1)}, u32[]{:S(2)}) copy-start(bf16[640,320]{0,1:T(8,128)(2,1)} %param.20) | copy-start | bytes 1228804
  21.3 11.1 %collective-permute-start.5 = (bf16[8,128,320]{1,2,0:T(8,128)(2,1)S(1)}, bf16[8,128,320]{1,2,0:T(8,128)(2,1)}, u32[]{:S(2)}, u32[]{:S(2)}) collective-permute-start(bf16[8,128,320]{1,2,0:T(8,128)(2,1)S(1)} %get-tuple-element.37), channel_id=1, source_target_pairs={{0,8},{8,0},{1,9},{9,1},{2,10},{10,2},{3,11},{11,3},{4,12},{12,4},... | collective-permute-start | bytes 1966088 | tf_op jit(solution)/shard_map/ppermute | solution.py:340
  22.2 9.6 %collective-permute-start.2 = (f32[12,256]{1,0:T(8,128)S(1)}, f32[12,256]{1,0:T(8,128)S(1)}, u32[]{:S(2)}, u32[]{:S(2)}) collective-permute-start(f32[12,256]{1,0:T(8,128)S(1)} %get-tuple-element.41), channel_id=1, source_target_pairs={{0,8},{8,0},{1,9},{9,1},{2,10},{10,2},{3,11},{11,3},{4,12},{12,4},... | collective-permute-start | bytes 36872 | tf_op jit(solution)/shard_map/ppermute | solution.py:340
  40.1 30.9 %collective-permute-start.6 = (bf16[192,640]{1,0:T(8,128)(2,1)}, bf16[192,640]{1,0:T(8,128)(2,1)S(1)}, u32[]{:S(2)}, u32[]{:S(2)}) collective-permute-start(bf16[192,640]{1,0:T(8,128)(2,1)} %get-tuple-element.17.q_ref), channel_id=1, source_target_pairs={{0,8},{8,0},{1,9},{9,1},{2,10},{10,2},{3,11},{11,3},{4,12},{12,4},... | collective-permute-start | bytes 737288 | tf_op jit(solution)/shard_map/ppermute | solution.py:340
  53.5 5.4 %copy-start.12 = (s32[2]{0:T(128)S(1)}, s32[2]{0:T(128)}, u32[]{:S(2)}) copy-start(s32[2]{0:T(128)} %param.14) | copy-start | bytes 28
  58.4 23.1 %collective-permute-start.10 = (bf16[192,640]{1,0:T(8,128)(2,1)}, bf16[192,640]{1,0:T(8,128)(2,1)S(1)}, u32[]{:S(2)}, u32[]{:S(2)}) collective-permute-start(bf16[192,640]{1,0:T(8,128)(2,1)} %get-tuple-element.27.q_ref), channel_id=1, source_target_pairs={{0,8},{8,0},{1,9},{9,1},{2,10},{10,2},{3,11},{11,3},{4,12},{12,4},... | collective-permute-start | bytes 737288 | tf_op jit(solution)/shard_map/ppermute | solution.py:340
  71.0 0.7 copy-start.8
  75.3 10.9 %collective-permute-start.7 = (bf16[96,320]{1,0:T(8,128)(2,1)}, bf16[96,320]{1,0:T(8,128)(2,1)S(1)}, u32[]{:S(2)}, u32[]{:S(2)}) collective-permute-start(bf16[96,320]{1,0:T(8,128)(2,1)} %get-tuple-element.22), channel_id=1, source_target_pairs={{0,1},{1,2},{2,3},{3,4},{4,5},{5,6},{6,7},{8,9},{9,10},{10,11},{11... | collective-permute-start | bytes 184328 | tf_op jit(solution)/shard_map/ppermute | solution.py:343
  80.1 6.5 %collective-permute-start.8 = (bf16[96,320]{1,0:T(8,128)(2,1)}, bf16[96,320]{1,0:T(8,128)(2,1)S(1)}, u32[]{:S(2)}, u32[]{:S(2)}) collective-permute-start(bf16[96,320]{1,0:T(8,128)(2,1)} %get-tuple-element.23), channel_id=1, source_target_pairs={{1,0},{2,1},{3,2},{4,3},{5,4},{6,5},{7,6},{9,8},{10,9},{11,10},{12... | collective-permute-start | bytes 184328 | tf_op jit(solution)/shard_map/ppermute | solution.py:346
  81.6 0.7 copy-start.7
  86.2 10.0 %copy-start.1 = (bf16[6,128,320]{2,1,0:T(8,128)(2,1)S(1)}, bf16[6,128,320]{2,1,0:T(8,128)(2,1)}, u32[]{:S(2)}) copy-start(bf16[6,128,320]{2,1,0:T(8,128)(2,1)} %mid_last.1) | copy-start | bytes 1474564
  86.2 0.6 copy-start.5
  86.5 0.6 copy-start.6
  96.6 16.9 %collective-permute-start.11 = (bf16[6,128,320]{1,2,0:T(8,128)(2,1)S(1)}, bf16[6,128,320]{1,2,0:T(8,128)(2,1)S(1)}, u32[]{:S(2)}, u32[]{:S(2)}) collective-permute-start(bf16[6,128,320]{1,2,0:T(8,128)(2,1)S(1)} %copy.58), channel_id=1, source_target_pairs={{0,8},{8,0},{1,9},{9,1},{2,10},{10,2},{3,11},{11,3},{4,12},{12,4},... | collective-permute-start | bytes 1474568 | tf_op jit(solution)/shard_map/ppermute | solution.py:340
  111.6 1.2 %collective-permute-start.9 = (f32[6,256]{1,0:T(8,128)S(1)}, f32[6,256]{1,0:T(8,128)S(1)}, u32[]{:S(2)}, u32[]{:S(2)}) collective-permute-start(f32[6,256]{1,0:T(8,128)S(1)} %get-tuple-element.43), channel_id=1, source_target_pairs={{0,8},{8,0},{1,9},{9,1},{2,10},{10,2},{3,11},{11,3},{4,12},{12,4},... | collective-permute-start | bytes 18440 | tf_op jit(solution)/shard_map/ppermute | solution.py:340

commit v2 on v1

v2 whole, which is shorter than its diff:
```python
import functools
import math

import jax
import jax.numpy as jnp
from jax import lax
from jax.experimental import pallas as pl
from jax.experimental.pallas import tpu as pltpu
from jax.sharding import PartitionSpec as P

EPSILON = 1e-06
LAT8 = 8
TILE = 16
F32 = jnp.float32
BF16 = jnp.bfloat16

VMEM = pl.BlockSpec(memory_space=pltpu.VMEM)
SMEM = pl.BlockSpec(memory_space=pltpu.SMEM)
ANY = pl.BlockSpec(memory_space=pl.ANY)


def act(values):
    scale = lax.rsqrt(jnp.mean(values * values, axis=0, keepdims=True) + EPSILON)
    half = values * (0.5 * scale)
    return half + half * jnp.tanh(half)


def dot(left, right):
    return jnp.dot(left, right, preferred_element_type=F32)


def shifted(values, by):
    count = values.shape[1]
    column = lax.broadcasted_iota(jnp.int32, values.shape, 1)
    edge = 0 if by == 1 else count - 1
    return jnp.where(column == edge, 0.0, pltpu.roll(values, by % count, 1))


def call(kernel, outs, in_specs, scratch=(), copies=0, name=None):
    shapes = [pltpu.VMEM(s, d) for s, d in scratch]
    if copies:
        shapes.append(pltpu.SemaphoreType.DMA((copies,)))
    return pl.pallas_call(
        kernel,
        out_shape=[jax.ShapeDtypeStruct(s, d) for s, d in outs],
        in_specs=in_specs,
        out_specs=[VMEM] * len(outs),
        scratch_shapes=shapes,
        name=name,
    )


def edges_of():
    place = lax.axis_index("rows")
    return (place == 0, place == lax.axis_size("rows") - 1)


def coefficient(times_ref, step):
    stamp = jnp.full((LAT8, 128), times_ref[step], jnp.int32)
    return (stamp.astype(F32) + 1.0) / 1000.0


def prep_kernel(gated_ref, enc_ref, dec_ref, down_ref, tmid_ref, time_ref, enc_out, dec_out, down_out, tmid_out, bias_out):
    chans = enc_ref.shape[3]
    for src, dst in ((enc_ref, enc_out), (dec_ref, dec_out)):
        for dy in range(3):
            for dx in range(3):
                dst[dx * chans : (dx + 1) * chans, dy * chans : (dy + 1) * chans] = src[dy, dx].T
    for dy in range(3):
        for dx in range(3):
            lane = (3 * dy + dx) * chans
            down_out[:, lane : lane + chans] = down_ref[dy, dx].T
        tmid_out[dy] = tmid_ref[dy].T
    biases = dot(gated_ref[...], time_ref[...])
    turned = biases.T
    for step in range(bias_out.shape[0]):
        bias_out[step] = jnp.broadcast_to(turned[:, step : step + 1], bias_out.shape[1:])


def spread_rows(acat_ref, row, value, cols, chans):
    for dy in range(3):
        start = pl.multiple_of((row - dy + 2) * cols, cols)
        acat_ref[dy * chans : (dy + 1) * chans, pl.ds(start, cols)] = value


def conv_sum(acc_ref, row, cols, chans):
    span = pl.ds(pl.multiple_of(row * cols, cols), cols)
    return (
        acc_ref[chans : 2 * chans, span]
        + shifted(acc_ref[:chans, span], 1)
        + shifted(acc_ref[2 * chans :, span], -1)
    )


def encode_rows(read_row, w_in, wcat_ref, bias_ref, copies, border, out_ref, lift_ref, acat_ref, acc_ref):
    count, chans, cols = out_ref.shape
    is_first, is_last = edges_of()

    def front(row, carry):
        lifted = lax.dot_general(
            w_in, read_row(row), (((0,), (0,)), ((), ())), preferred_element_type=F32
        )
        lift_ref[row] = lifted
        spread_rows(acat_ref, row, act(lifted).astype(BF16), cols, chans)
        return carry

    lax.fori_loop(0, count + 2, front, 0)
    for copy in copies:
        copy.wait()
    acc_ref[...] = dot(wcat_ref[...], acat_ref[:, 2 * cols : (2 + count) * cols])

    def back(row, carry):
        total = lift_ref[row + 1] + conv_sum(acc_ref, row, cols, chans) + bias_ref[...]
        outside = ((row < border) & is_first) | ((row >= count - border) & is_last)
        out_ref[row] = jnp.where(outside, 0.0, total).astype(BF16)
        return carry

    lax.fori_loop(0, count, back, 0)


def fetches(pairs, sems):
    copies = [pltpu.make_async_copy(s, d, sems.at[i]) for i, (s, d) in enumerate(pairs)]
    for copy in copies:
        copy.start()
    return copies


def enc_first_kernel(
    x_ref, taps_ref, wcat_hbm, bias_hbm, out_ref, wcat_ref, bias_ref, lift_ref, acat_ref, acc_ref, sems
):
    chans = out_ref.shape[1]
    copies = fetches(((wcat_hbm, wcat_ref), (bias_hbm.at[0, :chans], bias_ref)), sems)
    encode_rows(
        lambda row: x_ref[row].astype(BF16), taps_ref[9 * LAT8 :, :], wcat_ref, bias_ref, copies, 2,
        out_ref, lift_ref, acat_ref, acc_ref,
    )


def neighbour(even, one, two, above):
    return jnp.where(even, two, one) if above else jnp.where(even, one, two)


def enc_last_kernel(
    base_ref, near_ref, one_ref, two_ref, taps_ref, wcat_hbm, bias_hbm,
    out_ref, x_ref, ext_ref, wcat_ref, bias_ref, lift_ref, acat_ref, acc_ref, sems,
):
    chans = out_ref.shape[1]
    copies = fetches(((wcat_hbm, wcat_ref), (bias_hbm.at[1, :chans], bias_ref)), sems)
    rows = base_ref.shape[0]
    even = lax.axis_index("rows") % 2 == 0
    is_first, is_last = edges_of()
    packed = one_ref.shape[0] - 2 * TILE

    def received(above):
        high = neighbour(even, one_ref[packed : packed + TILE, :], two_ref[packed : packed + TILE, :], above)
        low = neighbour(even, one_ref[packed + TILE :, :], two_ref[packed + TILE :, :], above)
        both = high.astype(F32) + low.astype(F32)
        return both[:LAT8], both[LAT8:]

    from_up, base_up = received(True)
    from_down, base_down = received(False)
    x_ref[...] = base_ref[...]
    x_ref[0] = x_ref[0] - from_up
    x_ref[rows - 1] = x_ref[rows - 1] - from_down
    ext_ref[0] = jnp.where(is_first, 0.0, base_up - near_ref[0]).astype(BF16)
    ext_ref[rows + 1] = jnp.where(is_last, 0.0, base_down - near_ref[1]).astype(BF16)
    ext_ref[1 : rows + 1] = x_ref[...].astype(BF16)
    encode_rows(
        lambda row: ext_ref[row], taps_ref[9 * LAT8 :, :], wcat_ref, bias_ref, copies, 0,
        out_ref, lift_ref, acat_ref, acc_ref,
    )


def down_rows(read_row, w_ref, bias_ref, copies, low_ref, q_ref, acat_ref, cols):
    half = cols // 2
    low_rows = low_ref.shape[1] // half
    chans = acat_ref.shape[0] // 9
    source = lax.broadcasted_iota(jnp.int32, (cols, 2 * cols), 0)
    target = lax.broadcasted_iota(jnp.int32, (cols, 2 * cols), 1)
    wanted = 2 * (target % half) + target // cols
    pick = jnp.where(source == wanted, 1.0, 0.0).astype(BF16)
    column = lax.broadcasted_iota(jnp.int32, (chans, cols), 1)
    for row in range(2 * low_rows + 1):
        gate = act(read_row(row).astype(F32)).astype(BF16)
        both = dot(gate, pick)
        even, odd = both[:, :cols], both[:, cols:]
        before = jnp.where(column % half == 0, 0.0, pltpu.roll(odd, 1, 1))
        parts = [part.astype(BF16) for part in (before, even, odd)]
        for dy in range(3):
            if (row - dy) % 2 or not 0 <= (row - dy) // 2 < low_rows:
                continue
            low = (row - dy) // 2
            lane = (low % 2) * half
            for dx, part in enumerate(parts):
                start = (3 * dy + dx) * chans
                acat_ref[start : start + chans, low * half : (low + 1) * half] = part[:, lane : lane + half]
    for copy in copies:
        copy.wait()
    low_ref[...] = dot(w_ref[...], acat_ref[...])
    for low in range(0, low_ref.shape[1], cols):
        wide = min(cols, low_ref.shape[1] - low)
        total = low_ref[:, low : low + wide] + bias_ref[:, :wide]
        low_ref[:, low : low + wide] = total
        q_ref[:, low : low + wide] = act(total).astype(BF16)


def down_first_kernel(
    own_ref, got_ref, one_ref, two_ref, far_ref, w_hbm, bias_hbm,
    low_ref, q_ref, enc_ref, mid_ref, w_ref, bias_ref, acat_ref, sems,
):
    count, chans, cols = got_ref.shape
    mid = low_ref.shape[0]
    copies = fetches(((w_hbm, w_ref), (bias_hbm.at[0, chans : chans + mid], bias_ref)), sems)
    segment = lax.axis_index("segment")
    first = segment == 0
    even = lax.axis_index("rows") % 2 == 0
    for row in range(count + 2):
        if 1 <= row <= count:
            own, got = own_ref[0, segment, row - 1], got_ref[row - 1]
        else:
            own = neighbour(even, one_ref[segment, :chans], two_ref[segment, :chans], row == 0)
            got = neighbour(even, far_ref[0, :chans], far_ref[1, :chans], row == 0)
        enc_ref[row] = jnp.where(first, own, got)
        mid_ref[row] = jnp.where(first, got, own)
    down_rows(lambda row: enc_ref[row], w_ref, bias_ref, copies, low_ref, q_ref, acat_ref, cols)


def down_last_kernel(enc_ref, w_hbm, bias_hbm, low_ref, q_ref, w_ref, bias_ref, acat_ref, sems):
    chans, cols = enc_ref.shape[1:]
    mid = low_ref.shape[0]
    copies = fetches(((w_hbm, w_ref), (bias_hbm.at[1, chans : chans + mid], bias_ref)), sems)
    down_rows(lambda row: enc_ref[row + 1], w_ref, bias_ref, copies, low_ref, q_ref, acat_ref, cols)


def raise_rows(low_ref, q_ref, other_ref, w_tmid_ref, w_up_ref):
    far = 2 - 2 * lax.axis_index("segment")
    mixed = low_ref[...] + dot(w_tmid_ref[1], q_ref[...]) + dot(w_tmid_ref[far], other_ref[...])
    return dot(w_up_ref[...], mixed.astype(BF16)).astype(BF16)


def doubling(half, rows):
    source = lax.broadcasted_iota(jnp.int32, (rows * half, 2 * rows * half), 0)
    target = lax.broadcasted_iota(jnp.int32, (rows * half, 2 * rows * half), 1)
    return jnp.where(source == target // 2, 1.0, 0.0).astype(BF16)


def mid_first_kernel(
    low_ref, q_ref, other_ref, w_tmid_ref, w_up_ref, base_ref, near_ref, raised_ref, one_ref, two_ref
):
    raised_ref[...] = raise_rows(low_ref, q_ref, other_ref, w_tmid_ref, w_up_ref)
    rows, _, cols = base_ref.shape
    half = cols // 2
    packed = raised_ref.shape[0] // 2
    start = raised_ref.shape[1] - half
    even = lax.axis_index("rows") % 2 == 0

    def bundle(index, lane, edge):
        piece = raised_ref[:, lane : lane + half]
        sent = jnp.concatenate([near_ref[index], base_ref[edge]], axis=0)
        high = sent.astype(BF16)
        low = (sent - high.astype(F32)).astype(BF16)
        folded = jnp.concatenate([piece[:packed], piece[packed:]], axis=1)
        return jnp.concatenate([folded, high, low], axis=0)

    up = bundle(0, 0, 0)
    down = bundle(1, start, rows - 1)
    one_ref[...] = jnp.where(even, down, up)
    two_ref[...] = jnp.where(even, up, down)


def mid_last_kernel(low_ref, q_ref, other_ref, w_tmid_ref, w_up_ref, out_ref):
    raised = raise_rows(low_ref, q_ref, other_ref, w_tmid_ref, w_up_ref)
    rows, _, cols = out_ref.shape
    half = cols // 2
    wide = dot(raised, doubling(half, rows // 2)).astype(BF16)
    for row in range(rows):
        low = row // 2
        out_ref[row] = wide[:, low * cols : (low + 1) * cols]


def decode_rows(count, cols, wcat_ref, w_skip_ref, bias_ref, copies, border, taps_ref, jcat_ref, mixed_ref, acat_ref, acc_ref, o_ref):
    chans = bias_ref.shape[0]
    is_first, is_last = edges_of()
    mixed_ref[...] = dot(w_skip_ref[...], jcat_ref[...])

    def front(row, carry):
        mixed = mixed_ref[:, pl.ds(pl.multiple_of(row * cols, cols), cols)]
        spread_rows(acat_ref, row, act(mixed).astype(BF16), cols, chans)
        return carry

    lax.fori_loop(0, count + 2, front, 0)
    for copy in copies:
        copy.wait()
    acc_ref[...] = dot(wcat_ref[...], acat_ref[:, 2 * cols : (2 + count) * cols])

    def back(row, carry):
        mixed = mixed_ref[:, pl.ds(pl.multiple_of((row + 1) * cols, cols), cols)]
        value = act(mixed + conv_sum(acc_ref, row, cols, chans) + bias_ref[...])
        outside = ((row < border) & is_first) | ((row >= count - border) & is_last)
        span = pl.ds(pl.multiple_of(row * cols, cols), cols)
        o_ref[:, span] = jnp.where(outside, 0.0, value).astype(BF16)
        return carry

    lax.fori_loop(0, count, back, 0)
    taps = dot(taps_ref[: 9 * LAT8, :], o_ref[...])
    span = 3 * LAT8
    parts = []
    for row in range(count):
        tap = taps[:, row * cols : (row + 1) * cols]
        parts.append(shifted(tap[:span], 1) + tap[span : 2 * span] + shifted(tap[2 * span :], -1))
    return parts


def tap_sum(parts, row):
    total = None
    for dy in range(3):
        source = row + dy - 1
        if 0 <= source < len(parts):
            piece = parts[source][dy * LAT8 : (dy + 1) * LAT8]
            total = piece if total is None else total + piece
    return total


def dec_first_kernel(
    times_ref, enc_ref, mid_ref, x_ref, w_skip_ref, taps_ref, wcat_hbm, bias_hbm,
    base_ref, near_ref, jcat_ref, wcat_ref, bias_ref, mixed_ref, acat_ref, acc_ref, o_ref, sems,
):
    rows = base_ref.shape[0]
    chans, cols = enc_ref.shape[1:]
    start = bias_hbm.shape[1] - chans
    copies = fetches(((wcat_hbm, wcat_ref), (bias_hbm.at[0, start:], bias_ref)), sems)
    for row in range(rows + 2):
        jcat_ref[:chans, row * cols : (row + 1) * cols] = mid_ref[row]
        jcat_ref[chans:, row * cols : (row + 1) * cols] = enc_ref[row]
    parts = decode_rows(
        rows, cols, wcat_ref, w_skip_ref, bias_ref, copies, 0, taps_ref, jcat_ref, mixed_ref, acat_ref, acc_ref, o_ref
    )
    coef = coefficient(times_ref, 0)
    halo = (x_ref.shape[0] - rows) // 2
    near_ref[0] = coef * tap_sum(parts, -1)
    near_ref[1] = coef * tap_sum(parts, rows)
    for row in range(rows):
        base_ref[row] = x_ref[halo + row] - coef * tap_sum(parts, row)


def dec_last_kernel(
    times_ref, enc_ref, mid_ref, one_ref, two_ref, x_ref, w_skip_ref, taps_ref, wcat_hbm, bias_hbm,
    next_ref, jcat_ref, wcat_ref, bias_ref, mixed_ref, acat_ref, acc_ref, o_ref, sems,
):
    rows = x_ref.shape[0]
    chans, cols = enc_ref.shape[1:]
    start = bias_hbm.shape[1] - chans
    copies = fetches(((wcat_hbm, wcat_ref), (bias_hbm.at[1, start:], bias_ref)), sems)
    half = cols // 2
    inner = rows // 2
    even = lax.axis_index("rows") % 2 == 0
    packed = chans // 2
    wide = dot(mid_ref[...], doubling(half, inner)).astype(BF16)
    twice = doubling(half, 1)
    for low in range(inner + 2):
        if 1 <= low <= inner:
            piece = wide[:, (low - 1) * cols : low * cols]
        else:
            folded = neighbour(even, one_ref[:packed, :], two_ref[:packed, :], low == 0)
            piece = dot(jnp.concatenate([folded[:, :half], folded[:, half:]], axis=0), twice).astype(BF16)
        for row in (2 * low, 2 * low + 1):
            jcat_ref[:chans, row * cols : (row + 1) * cols] = piece
            jcat_ref[chans:, row * cols : (row + 1) * cols] = enc_ref[row]
    parts = decode_rows(
        rows + 2, cols, wcat_ref, w_skip_ref, bias_ref, copies, 1, taps_ref, jcat_ref, mixed_ref, acat_ref, acc_ref, o_ref
    )
    coef = coefficient(times_ref, 1)
    for row in range(rows):
        next_ref[row] = x_ref[row] - coef * tap_sum(parts, row + 1)


def gated_times(timesteps, half):
    freqs = jnp.exp(-math.log(10000.0) * jnp.arange(half).astype(F32) / half)
    angles = timesteps.astype(F32)[:, None] * freqs[None, :]
    embedded = jnp.concatenate([jnp.sin(angles), jnp.cos(angles)], axis=1)
    gated = jax.nn.silu(embedded).astype(BF16)
    return jnp.pad(gated, ((0, TILE - gated.shape[0]), (0, 0)))


def body(latent, stale, timesteps, w_in, w_enc, w_down, w_tmid, w_up, w_skip, w_dec, w_out, w_time):
    segment = lax.axis_index("segment")
    first = segment == 0
    size = lax.axis_size("rows")
    even = lax.axis_index("rows") % 2 == 0
    chan_major = stale.transpose(0, 1, 2, 4, 3)
    state = chan_major[0]
    frames, rows, chans, cols = state.shape
    mid = w_down.shape[3]
    lat = w_in.shape[0]
    half = cols // 2
    low = (rows // 2) * half
    halo = 3
    assert frames == 2 and lax.axis_size("segment") == 2

    def paired(start):
        return [p for i in range(start, size - 1, 2) for p in ((i, i + 1), (i + 1, i))]

    def swap(value):
        return lax.ppermute(value, "segment", [(0, 1), (1, 0)])

    def exchange(one, two):
        return lax.ppermute(one, "rows", paired(0)), lax.ppermute(two, "rows", paired(1))

    def mine(value, axis=0):
        return lax.dynamic_index_in_dim(value, segment, axis, keepdims=False)

    def theirs(value, axis=0):
        return lax.dynamic_index_in_dim(value, 1 - segment, axis, keepdims=False)

    def edge_rows(state_rows, latent_rows):
        flat = latent_rows.astype(BF16).reshape(frames, -1, cols)
        spare = -flat.shape[1] % TILE
        return jnp.concatenate([state_rows, jnp.pad(flat, ((0, 0), (0, spare), (0, 0)))], axis=1)

    last = edge_rows(state[:, rows - 1], latent[:, rows - halo :])
    top = edge_rows(state[:, 0], latent[:, :halo])
    one, two = exchange(jnp.where(even, last, top), jnp.where(even, top, last))
    got = swap(theirs(state))
    x_got = swap(theirs(latent))
    far = swap(jnp.stack([theirs(one), theirs(two)]))

    def latent_rows(piece):
        return piece[chans : chans + halo * latent.shape[2] // cols].reshape(halo, latent.shape[2]).astype(F32)

    def columns(own, one_piece, two_piece):
        above = jnp.where(even, two_piece, one_piece)
        below = jnp.where(even, one_piece, two_piece)
        return jnp.concatenate([latent_rows(above), own, latent_rows(below)], axis=0)

    near_cols = columns(mine(latent), mine(one), mine(two))
    far_cols = columns(x_got, far[0], far[1])
    x_full = jnp.concatenate(
        [jnp.where(first, near_cols, far_cols), jnp.where(first, far_cols, near_cols)], axis=1
    )
    x_t = x_full.reshape(rows + 2 * halo, cols, lat).transpose(0, 2, 1)
    x_t = jnp.pad(x_t, ((0, 0), (0, LAT8 - lat), (0, 0)))

    taps = jnp.pad(w_out.transpose(1, 0, 3, 2), ((0, 0), (0, 0), (0, LAT8 - lat), (0, 0)))
    taps = jnp.concatenate(
        [taps.reshape(9 * LAT8, chans), jnp.pad(w_in, ((0, LAT8 - lat), (0, 0)))], axis=0
    )
    w_up_t = w_up.T
    w_skip_t = w_skip.T
    wide = 3 * chans
    total = w_time.shape[1]

    enc_cat, dec_cat, w_down_t, w_tmid_t, bias = call(
        prep_kernel,
        [
            ((wide, wide), BF16),
            ((wide, wide), BF16),
            ((mid, 3 * wide), BF16),
            ((3, mid, mid), BF16),
            ((timesteps.shape[0], total, cols), F32),
        ],
        [VMEM] * 6,
        name="prep",
    )(gated_times(timesteps, w_time.shape[0] // 2), w_enc, w_dec, w_down, w_tmid, w_time)

    def enc_scratch(count):
        return [
            ((wide, wide), BF16),
            ((chans, cols), F32),
            ((count + 2, chans, cols), F32),
            ((wide, (count + 4) * cols), BF16),
            ((wide, count * cols), F32),
        ]

    def dec_scratch(count):
        return [
            ((2 * chans, (count + 2) * cols), BF16),
            ((wide, wide), BF16),
            ((chans, cols), F32),
            ((chans, (count + 2) * cols), F32),
            ((wide, (count + 4) * cols), BF16),
            ((wide, count * cols), F32),
            ((chans, count * cols), BF16),
        ]

    down_scratch = [((mid, 3 * wide), BF16), ((mid, cols), F32), ((3 * wide, low), BF16)]
    down_outs = [((mid, low), F32), ((mid, low), BF16)]
    ext = ((rows + 2, chans, cols), BF16)
    low0, q0, enc0, mid0 = call(
        down_first_kernel, down_outs + [ext, ext], [VMEM] * 5 + [ANY] * 2, down_scratch, 2, "down_first"
    )(chan_major, got, one, two, far, w_down_t, bias)
    q0_other = swap(q0)

    (enc1,) = call(
        enc_first_kernel,
        [((rows + 4, chans, cols), BF16)],
        [VMEM] * 2 + [ANY] * 2,
        enc_scratch(rows + 4),
        2,
        "enc_first",
    )(x_t, taps, enc_cat, bias)

    base, near = call(
        dec_first_kernel,
        [((rows, LAT8, cols), F32), ((2, LAT8, cols), F32)],
        [SMEM] + [VMEM] * 5 + [ANY] * 2,
        dec_scratch(rows),
        2,
        "dec_first",
    )(timesteps, enc0, mid0, x_t, w_skip_t, taps, dec_cat, bias)

    bundle = ((chans // 2 + 2 * TILE, cols), BF16)
    mid1, to_one, to_two = call(
        mid_first_kernel, [((chans, low), BF16), bundle, bundle], [VMEM] * 7, name="mid_first"
    )(low0, q0, q0_other, w_tmid_t, w_up_t, base, near)
    got_one, got_two = exchange(to_one, to_two)

    low1, q1 = call(
        down_last_kernel, down_outs, [VMEM] + [ANY] * 2, down_scratch, 2, "down_last"
    )(enc1, w_down_t, bias)
    q1_other = swap(q1)

    (mid2,) = call(mid_last_kernel, [((rows, chans, cols), BF16)], [VMEM] * 5, name="mid_last")(
        low1, q1, q1_other, w_tmid_t, w_up_t
    )

    enc2, x1 = call(
        enc_last_kernel,
        [((rows, chans, cols), BF16), ((rows, LAT8, cols), F32)],
        [VMEM] * 5 + [ANY] * 2,
        [((rows + 2, LAT8, cols), BF16)] + enc_scratch(rows),
        2,
        "enc_last",
    )(base, near, got_one, got_two, taps, enc_cat, bias)

    feat_other = swap(jnp.where(first, mid2, enc2))

    (x2,) = call(
        dec_last_kernel,
        [((rows, LAT8, cols), F32)],
        [SMEM] + [VMEM] * 7 + [ANY] * 2,
        dec_scratch(rows + 2),
        2,
        "dec_last",
    )(timesteps, enc1, mid1, got_one, got_two, x1, w_skip_t, taps, dec_cat, bias)

    flat = x2[:, :lat].transpose(0, 2, 1).reshape(rows, cols * lat)
    halves = jnp.stack([flat[:, : cols * lat // 2], flat[:, cols * lat // 2 :]])
    x_keep, x_far = mine(halves), swap(theirs(halves))
    result = jnp.where(first, jnp.stack([x_keep, x_far]), jnp.stack([x_far, x_keep]))
    features = jnp.where(first, jnp.stack([enc2, feat_other]), jnp.stack([feat_other, mid2]))
    return (result, features.transpose(0, 1, 3, 2)[None])


def solution(mesh):
    placed = (
        P("clips", "rows", "segment"),
        P("segment", "clips", "rows", None, None),
        P("clips"),
    ) + (P(),) * 9
    return jax.shard_map(
        body,
        mesh=mesh,
        in_specs=placed,
        out_specs=(P("clips", "rows", "segment"), P("segment", "clips", "rows", None, None)),
        check_vma=False,
    )
```

time: 118 us -> 100 us (0.85)
  the two profiles are of different devices: /device:TPU:0 before, /device:TPU:13 now
where the time goes in v2:
time: 100 us; the launch traced here: 99.3 us
  Pallas kernels  64.3 us (64%)
  starting transfers between devices  13.2 us (13%)
  local copies, waits for them, and re-layouts  12.3 us (12%)
  waiting for transfers between devices  4.51 us (5%)
  other arithmetic  3.98 us (4%)
  between operations  1.08 us (1%)
    pallas_call x1, Pallas kernels, body(): call(prep_kernel, [((wide, wide), BF16), ((wide, wide), BF16), ((mid, 3 *...  11.7 us
    pallas_call x1, Pallas kernels, body(): call(enc_first_kernel, [((rows + 4, chans, cols), BF16)], [VMEM] * 2 + [A...  9.53 us
    pallas_call x1, Pallas kernels, body(): call(dec_last_kernel, [((rows, LAT8, cols), F32)], [SMEM] + [VMEM] * 7 +...  8.79 us
    ppermute x2, starting transfers between devices, exchange(): lax.ppermute(two, 'rows', paired(1))  8.01 us
    pallas_call x1, Pallas kernels, body(): call(dec_first_kernel, [((rows, LAT8, cols), F32), ((2, LAT8, cols), F32)...  7.1 us
    pallas_call x1, Pallas kernels, body(): call(enc_last_kernel, [((rows, chans, cols), BF16), ((rows, LAT8, cols),...  6.9 us
    pallas_call x1, Pallas kernels, body(): call(down_first_kernel, down_outs + [ext, ext], [VMEM] * 5 + [ANY] * 2, d...  6.48 us
    pallas_call x1, Pallas kernels, body(): call(down_last_kernel, down_outs, [VMEM] + [ANY] * 2, down_scratch, 2, 'd...  5.54 us
  transfers between devices with their start and end apart: 11, of which 3 were waited for; matrix products, arithmetic and copies ran while one was open for 10% of the time, Pallas kernels for 51%

profile of v2, /device:TPU:13, one launch (start us, length us, event | category | flops | bytes accessed | tf_op | source)
XLA Modules:
  0.0 99.3 jit_solution(5076060529041830208)
XLA Ops:
  0.6 0.8 dynamic-slice_reduce_fusion
  1.5 0.7 collective-permute-start.3
  2.2 1.1 %dynamic-slice_bitcast_fusion = bf16[6,320,128]{2,1,0:T(8,128)(2,1)S(1)} fusion(bf16[1,2,6,128,320]{3,4,2,1,0:T(8,128)(2,1)} %param.13, s32[]{:T(128)S(6)} %select_n.107), kind=kLoop, calls=%fused_computation.4 | loop fusion | bytes 983044 | tf_op jit(solution)/shard_map/jit(dynamic_index_in_dim)/squeeze | solution.py:413
  3.4 0.7 convert.8
  4.1 1.3 %copy.39 = bf16[1,2,6,128,320]{3,4,1,2,0:T(8,128)(2,1)S(1)} copy(bf16[1,2,6,128,320]{3,4,2,1,0:T(8,128)(2,1)} %param.13) | data formatting | bytes 1966080 | tf_op args[1]
  5.6 0.3 collective-permute-start.1
  5.9 4.1 %collective-permute-start = (bf16[2,336,128]{2,1,0:T(8,128)(2,1)S(1)}, bf16[2,336,128]{2,1,0:T(8,128)(2,1)S(1)}, u32[]{:S(2)}, u32[]{:S(2)}) collective-permute-start(bf16[2,336,128]{2,1,0:T(8,128)(2,1)S(1)} %get-tuple-element.47), channel_id=1, source_target_pairs={{1,2},{2,1},{3,4},{4,3},{5,6},{6,5},{9,10},{10,9},{11,12},{12,11},... | collective-permute-start | bytes 516104 | tf_op jit(solution)/shard_map/ppermute | solution.py:407
  10.0 0.1 multiply_sine_fusion
  10.2 0.9 collective-permute-done.1.one_ref
  11.1 2.8 %collective-permute-done.two_ref = bf16[2,336,128]{2,1,0:T(8,128)(2,1)S(1)} collective-permute-done((bf16[2,336,128]{2,1,0:T(8,128)(2,1)S(1)}, bf16[2,336,128]{2,1,0:T(8,128)(2,1)S(1)}, u32[]{:S(2)}, u32[]{:S(2)}) %collective-permute-start) | collective-permute-done | bytes 172064 | tf_op jit(solution)/shard_map/ppermute | solution.py:407
  13.9 2.3 %collective-permute-start.2 = (bf16[2,336,128]{2,1,0:T(8,128)(2,1)S(1)}, bf16[2,336,128]{2,1,0:T(8,128)(2,1)S(1)}, u32[]{:S(2)}, u32[]{:S(2)}) collective-permute-start(bf16[2,336,128]{2,1,0:T(8,128)(2,1)S(1)} %pad_maximum_fusion), channel_id=1, source_target_pairs={{0,8},{8,0},{1,9},{9,1},{2,10},{10,2},{3,11},{11,3},{4,12},{12,4},... | collective-permute-start | bytes 516104 | tf_op jit(solution)/shard_map/ppermute | solution.py:404
  16.3 0.6 fusion.6.taps_ref
  17.0 0.6 pad.28.gated_ref
  17.6 0.2 concatenate.32
  17.8 0.1 copy.24
  17.9 1.0 %copy.31.own_ref = bf16[1,2,6,320,128]{4,3,2,1,0:T(8,128)(2,1)} copy(bf16[1,2,6,320,128]{4,3,1,2,0:T(8,128)(2,1)S(1)} %bitcast.40) | data formatting | bytes 1966080 | tf_op jit(solution)/shard_map/transpose | solution.py:390
  18.9 11.7 %prep.1 = (bf16[960,960]{1,0:T(8,128)(2,1)}, bf16[960,960]{1,0:T(8,128)(2,1)}, bf16[640,2880]{1,0:T(8,128)(2,1)}, bf16[3,640,640]{2,1,0:T(8,128)(2,1)}, f32[2,1280,128]{2,1,0:T(8,128)}) custom-call(bf16[16,320]{1,0:T(8,128)(2,1)} %pad.28.gated_ref, bf16[3,3,320,320]{3,2,1,0:T(8,128)(2,1)} %enc_ref.1, bf16[3,3,320,320]{3,2,1,0:T(8,128)(2,1)} %dec_ref.1, ...), custom_call_target="tpu_custom_call" | custom-call | tf_op jit(solution)/shard_map/prep/pallas_call | solution.py:452
  30.6 0.2 concatenate.34
  30.8 0.1 copy.28
  31.0 0.1 reshape.84
  31.2 0.1 reshape.85
  31.5 0.1 reshape.83
  31.7 0.1 reshape.82
  32.0 0.8 copy-done.3
  32.8 6.5 %down_first.1 = (f32[640,192]{1,0:T(8,128)}, bf16[640,192]{1,0:T(8,128)(2,1)}, bf16[8,320,128]{2,1,0:T(8,128)(2,1)}, bf16[8,320,128]{2,1,0:T(8,128)(2,1)}) custom-call(bf16[1,2,6,320,128]{4,3,2,1,0:T(8,128)(2,1)} %copy.31.own_ref, bf16[6,320,128]{2,1,0:T(8,128)(2,1)} %copy-done.3, bf16[2,336,128]{2,1,0:T(8,128)(2,1)} %copy-done.4, ...), custom_call_target="tpu_custom_call" | custom-call | tf_op jit(solution)/shard_map/down_first/pallas_call | solution.py:488
  39.4 0.6 pad.25.x_ref
  40.0 9.5 %enc_first.1.enc_ref = bf16[10,320,128]{2,1,0:T(8,128)(2,1)} custom-call(f32[12,8,128]{2,1,0:T(8,128)} %pad.25.x_ref, bf16[80,320]{1,0:T(8,128)(2,1)} %fusion.6.taps_ref, bf16[960,960]{1,0:T(8,128)(2,1)} %get-tuple-element.20.wcat_hbm, f32[2,1280,128]{2,1,0:T(8,128)} %get-tuple-element.21.bias_hbm), custom_call_target="tpu_custom_call" | custom-call | tf_op jit(solution)/shard_map/enc_first/pallas_call | solution.py:493
  49.6 5.5 %down_last.1 = (f32[640,192]{1,0:T(8,128)}, bf16[640,192]{1,0:T(8,128)(2,1)}) custom-call(bf16[10,320,128]{2,1,0:T(8,128)(2,1)} %enc_first.1.enc_ref, bf16[640,2880]{1,0:T(8,128)(2,1)} %get-tuple-element.22.w_hbm, f32[2,1280,128]{2,1,0:T(8,128)} %get-tuple-element.21.bias_hbm), custom_call_target="tpu_custom_call" | custom-call | tf_op jit(solution)/shard_map/down_last/pallas_call | solution.py:517
  55.1 0.6 collective-permute-start.9
  55.7 7.1 %dec_first.1 = (f32[6,8,128]{2,1,0:T(8,128)}, f32[2,8,128]{2,1,0:T(8,128)}) custom-call(s32[2]{0:T(128)} %times_ref.3, bf16[8,320,128]{2,1,0:T(8,128)(2,1)} %get-tuple-element.26.enc_ref, bf16[8,320,128]{2,1,0:T(8,128)(2,1)} %get-tuple-element.27.mid_ref, f32[12,8,128]{2,1,0:T(8,128)} %pad.25.x_ref, bf16[320,640]{1,0:T(8,128)(2,1)} %bitcast.45, ...), custom_call_target="tpu_custom_call" | custom-call | tf_op jit(solution)/shard_map/dec_first/pallas_call | solution.py:502
  62.8 0.7 copy-done.7
  63.5 3.9 %mid_first.1 = (bf16[320,192]{1,0:T(8,128)(2,1)}, bf16[192,128]{1,0:T(8,128)(2,1)}, bf16[192,128]{1,0:T(8,128)(2,1)}) custom-call(f32[640,192]{1,0:T(8,128)} %get-tuple-element.23.low_ref, bf16[640,192]{1,0:T(8,128)(2,1)} %get-tuple-element.24.q_ref, bf16[640,192]{1,0:T(8,128)(2,1)} %copy-done.7, bf16[3,640,640]{2,1,0:T(8,128)(2,1)} %get-tuple-element.25.w_tmid_ref, ...), custom_call_target="tpu_custom_call" | custom-call | tf_op jit(solution)/shard_map/mid_first/pallas_call | solution.py:512
  67.5 0.5 collective-permute-start.6
  68.0 3.9 %collective-permute-start.7 = (bf16[192,128]{1,0:T(8,128)(2,1)}, bf16[192,128]{1,0:T(8,128)(2,1)S(1)}, u32[]{:S(2)}, u32[]{:S(2)}) collective-permute-start(bf16[192,128]{1,0:T(8,128)(2,1)} %get-tuple-element.33), channel_id=1, source_target_pairs={{1,2},{2,1},{3,4},{4,3},{5,6},{6,5},{9,10},{10,9},{11,12},{12,11},... | collective-permute-start | bytes 147464 | tf_op jit(solution)/shard_map/ppermute | solution.py:407
  71.9 0.7 copy-done.6
  72.6 4.3 %mid_last.1 = bf16[6,320,128]{2,1,0:T(8,128)(2,1)} custom-call(f32[640,192]{1,0:T(8,128)} %get-tuple-element.36.low_ref, bf16[640,192]{1,0:T(8,128)(2,1)} %get-tuple-element.37.q_ref, bf16[640,192]{1,0:T(8,128)(2,1)} %copy-done.6, bf16[3,640,640]{2,1,0:T(8,128)(2,1)} %get-tuple-element.25.w_tmid_ref, bf16[320,640]{1,0:T(8,128)(2,1)} %bitcast.44), custom_call_target="tpu_custom_call" | custom-call | tf_op jit(solution)/shard_map/mid_last/pallas_call | solution.py:522
  76.9 0.6 copy-done.8
  77.5 0.6 copy-done.9
  78.2 6.9 %enc_last.1 = (bf16[6,320,128]{2,1,0:T(8,128)(2,1)}, f32[6,8,128]{2,1,0:T(8,128)}) custom-call(f32[6,8,128]{2,1,0:T(8,128)} %get-tuple-element.29.base_ref, f32[2,8,128]{2,1,0:T(8,128)} %get-tuple-element.30.near_ref, bf16[192,128]{1,0:T(8,128)(2,1)} %copy-done.8, bf16[192,128]{1,0:T(8,128)(2,1)} %copy-done.9, bf16[80,320]{1,0:T(8,128)(2,1)} %fusion.6.taps_ref, ...), custom_call_target="tpu_custom_call" | custom-call | tf_op jit(solution)/shard_map/enc_last/pallas_call | solution.py:526
  85.1 1.1 %broadcast_select_fusion = bf16[6,320,128]{2,1,0:T(8,128)(2,1)S(1)} fusion(bf16[6,320,128]{2,1,0:T(8,128)(2,1)S(1)} %copy-done, bf16[6,320,128]{2,1,0:T(8,128)(2,1)} %get-tuple-element.35, pred[]{:T(512)S(6)} %eq.8), kind=kLoop, calls=%fused_computation.5 | loop fusion | flops 245760 | bytes 1474561 | tf_op jit(solution)/shard_map/jit(_where)/select_n | solution.py:535
  86.3 8.8 %dec_last.1 = f32[6,8,128]{2,1,0:T(8,128)} custom-call(s32[2]{0:T(128)} %times_ref.3, bf16[10,320,128]{2,1,0:T(8,128)(2,1)} %enc_first.1.enc_ref, bf16[320,192]{1,0:T(8,128)(2,1)} %get-tuple-element.31.mid_ref, bf16[192,128]{1,0:T(8,128)(2,1)} %copy-done.8, bf16[192,128]{1,0:T(8,128)(2,1)} %copy-done.9, f32[6,8,128]{2,1,0:T(8,128)} %get-tuple-element.34.x_ref, ...), custom_call_target="tpu_custom_call" | custom-call | tf_op jit(solution)/shard_map/dec_last/pallas_call | solution.py:537
  95.1 0.7 slice_bitcast_fusion.2
  95.8 0.2 copy.32
  96.0 0.2 reshape.81
  96.2 0.6 collective-permute-start.8
  96.8 0.8 collective-permute-done.8
  97.6 0.6 copy.33
  98.3 1.1 %fusion = bf16[1,2,6,128,320]{3,4,2,1,0:T(8,128)(2,1)} fusion(bf16[1,6,320,128]{3,2,1,0:T(8,128)(2,1)S(1)} %bitcast.47, bf16[1,6,320,128]{3,2,1,0:T(8,128)(2,1)S(1)} %bitcast.42, bf16[1,6,320,128]{3,2,1,0:T(8,128)(2,1)S(1)} %bitcast.41, pred[]{:T(512)S(6)} %eq.8), kind=kLoop, calls=%fused_computation.1 | loop fusion | flops 1474560 | bytes 2457601 | tf_op jit(solution)/shard_map/broadcast_in_dim | solution.py:551
  (59 shorter events, 1.1 us)
Async XLA Ops:
  0.6 9.4 %copy-start.12 = (s32[2]{0:T(128)S(1)}, s32[2]{0:T(128)}, u32[]{:S(2)}) copy-start(s32[2]{0:T(128)} %times_ref.3) | copy-start | bytes 28
  1.5 8.7 %copy-start.10 = (bf16[3,3,320,4]{2,3,1,0:T(4,128)(2,1)S(1)}, bf16[3,3,320,4]{2,3,1,0:T(4,128)(2,1)}, u32[]{:S(2)}) copy-start(bf16[3,3,320,4]{2,3,1,0:T(4,128)(2,1)} %param.22) | copy-start | bytes 69124
  1.5 29.2 %collective-permute-start.3 = (f32[6,256]{1,0:T(8,128)S(1)}, f32[6,256]{1,0:T(8,128)S(1)}, u32[]{:S(2)}, u32[]{:S(2)}) collective-permute-start(f32[6,256]{1,0:T(8,128)S(1)} %bitcast.50), channel_id=1, source_target_pairs={{0,8},{8,0},{1,9},{9,1},{2,10},{10,2},{3,11},{11,3},{4,12},{12,4},... | collective-permute-start | bytes 18440 | tf_op jit(solution)/shard_map/ppermute | solution.py:404
  3.3 13.0 %copy-start.11 = (bf16[4,320]{1,0:T(4,128)(2,1)S(1)}, bf16[4,320]{1,0:T(4,128)(2,1)}, u32[]{:S(2)}) copy-start(bf16[4,320]{1,0:T(4,128)(2,1)} %param.15) | copy-start | bytes 7684
  3.3 28.7 %collective-permute-start.4 = (bf16[6,320,128]{2,1,0:T(8,128)(2,1)S(1)}, bf16[6,320,128]{2,1,0:T(8,128)(2,1)S(1)}, u32[]{:S(2)}, u32[]{:S(2)}) collective-permute-start(bf16[6,320,128]{2,1,0:T(8,128)(2,1)S(1)} %dynamic-slice_bitcast_fusion), channel_id=1, source_target_pairs={{0,8},{8,0},{1,9},{9,1},{2,10},{10,2},{3,11},{11,3},{4,12},{12,4},... | collective-permute-start | bytes 1474568 | tf_op jit(solution)/shard_map/ppermute | solution.py:404
  5.6 5.5 %collective-permute-start.1 = (bf16[2,336,128]{2,1,0:T(8,128)(2,1)S(1)}, bf16[2,336,128]{2,1,0:T(8,128)(2,1)S(1)}, u32[]{:S(2)}, u32[]{:S(2)}) collective-permute-start(bf16[2,336,128]{2,1,0:T(8,128)(2,1)S(1)} %get-tuple-element.46), channel_id=1, source_target_pairs={{0,1},{1,0},{2,3},{3,2},{4,5},{5,4},{6,7},{7,6},{8,9},{9,8},{10,11... | collective-permute-start | bytes 516104 | tf_op jit(solution)/shard_map/ppermute | solution.py:407
  5.9 8.0 %collective-permute-start = (bf16[2,336,128]{2,1,0:T(8,128)(2,1)S(1)}, bf16[2,336,128]{2,1,0:T(8,128)(2,1)S(1)}, u32[]{:S(2)}, u32[]{:S(2)}) collective-permute-start(bf16[2,336,128]{2,1,0:T(8,128)(2,1)S(1)} %get-tuple-element.47), channel_id=1, source_target_pairs={{1,2},{2,1},{3,4},{4,3},{5,6},{6,5},{9,10},{10,9},{11,12},{12,11},... | collective-permute-start | bytes 516104 | tf_op jit(solution)/shard_map/ppermute | solution.py:407
  11.1 19.9 %copy-start.4 = (bf16[2,336,128]{2,1,0:T(8,128)(2,1)}, bf16[2,336,128]{2,1,0:T(8,128)(2,1)S(1)}, u32[]{:S(2)}) copy-start(bf16[2,336,128]{2,1,0:T(8,128)(2,1)S(1)} %collective-permute-done.1.one_ref) | copy-start | bytes 516100
  13.9 17.1 %copy-start.5 = (bf16[2,336,128]{2,1,0:T(8,128)(2,1)}, bf16[2,336,128]{2,1,0:T(8,128)(2,1)S(1)}, u32[]{:S(2)}) copy-start(bf16[2,336,128]{2,1,0:T(8,128)(2,1)S(1)} %collective-permute-done.two_ref) | copy-start | bytes 516100
  13.9 17.0 %collective-permute-start.2 = (bf16[2,336,128]{2,1,0:T(8,128)(2,1)S(1)}, bf16[2,336,128]{2,1,0:T(8,128)(2,1)S(1)}, u32[]{:S(2)}, u32[]{:S(2)}) collective-permute-start(bf16[2,336,128]{2,1,0:T(8,128)(2,1)S(1)} %pad_maximum_fusion), channel_id=1, source_target_pairs={{0,8},{8,0},{1,9},{9,1},{2,10},{10,2},{3,11},{11,3},{4,12},{12,4},... | collective-permute-start | bytes 516104 | tf_op jit(solution)/shard_map/ppermute | solution.py:404
  31.0 1.0 %copy-start.2 = (bf16[2,336,128]{2,1,0:T(8,128)(2,1)}, bf16[2,336,128]{2,1,0:T(8,128)(2,1)S(1)}, u32[]{:S(2)}) copy-start(bf16[2,336,128]{2,1,0:T(8,128)(2,1)S(1)} %collective-permute-done.2.far_ref) | copy-start | bytes 516100
  32.0 0.8 copy-start.3
  39.2 23.6 %collective-permute-start.5 = (bf16[640,192]{1,0:T(8,128)(2,1)}, bf16[640,192]{1,0:T(8,128)(2,1)S(1)}, u32[]{:S(2)}, u32[]{:S(2)}) collective-permute-start(bf16[640,192]{1,0:T(8,128)(2,1)} %get-tuple-element.24.q_ref), channel_id=1, source_target_pairs={{0,8},{8,0},{1,9},{9,1},{2,10},{10,2},{3,11},{11,3},{4,12},{12,4},... | collective-permute-start | bytes 737288 | tf_op jit(solution)/shard_map/ppermute | solution.py:404
  55.1 16.7 %collective-permute-start.9 = (bf16[640,192]{1,0:T(8,128)(2,1)}, bf16[640,192]{1,0:T(8,128)(2,1)S(1)}, u32[]{:S(2)}, u32[]{:S(2)}) collective-permute-start(bf16[640,192]{1,0:T(8,128)(2,1)} %get-tuple-element.37.q_ref), channel_id=1, source_target_pairs={{0,8},{8,0},{1,9},{9,1},{2,10},{10,2},{3,11},{11,3},{4,12},{12,4},... | collective-permute-start | bytes 737288 | tf_op jit(solution)/shard_map/ppermute | solution.py:404
  62.8 0.7 copy-start.7
  67.5 9.4 %collective-permute-start.6 = (bf16[192,128]{1,0:T(8,128)(2,1)}, bf16[192,128]{1,0:T(8,128)(2,1)S(1)}, u32[]{:S(2)}, u32[]{:S(2)}) collective-permute-start(bf16[192,128]{1,0:T(8,128)(2,1)} %get-tuple-element.32), channel_id=1, source_target_pairs={{0,1},{1,0},{2,3},{3,2},{4,5},{5,4},{6,7},{7,6},{8,9},{9,8},{10,11... | collective-permute-start | bytes 147464 | tf_op jit(solution)/shard_map/ppermute | solution.py:407
  68.0 8.9 %collective-permute-start.7 = (bf16[192,128]{1,0:T(8,128)(2,1)}, bf16[192,128]{1,0:T(8,128)(2,1)S(1)}, u32[]{:S(2)}, u32[]{:S(2)}) collective-permute-start(bf16[192,128]{1,0:T(8,128)(2,1)} %get-tuple-element.33), channel_id=1, source_target_pairs={{1,2},{2,1},{3,4},{4,3},{5,6},{6,5},{9,10},{10,9},{11,12},{12,11},... | collective-permute-start | bytes 147464 | tf_op jit(solution)/shard_map/ppermute | solution.py:407
  71.9 0.7 copy-start.6
  76.9 8.1 %copy-start = (bf16[6,320,128]{2,1,0:T(8,128)(2,1)S(1)}, bf16[6,320,128]{2,1,0:T(8,128)(2,1)}, u32[]{:S(2)}) copy-start(bf16[6,320,128]{2,1,0:T(8,128)(2,1)} %mid_last.1) | copy-start | bytes 1474564
  76.9 0.6 copy-start.8
  77.5 0.6 copy-start.9
  86.2 12.1 %collective-permute-start.10 = (bf16[6,320,128]{2,1,0:T(8,128)(2,1)S(1)}, bf16[6,320,128]{2,1,0:T(8,128)(2,1)S(1)}, u32[]{:S(2)}, u32[]{:S(2)}) collective-permute-start(bf16[6,320,128]{2,1,0:T(8,128)(2,1)S(1)} %broadcast_select_fusion), channel_id=1, source_target_pairs={{0,8},{8,0},{1,9},{9,1},{2,10},{10,2},{3,11},{11,3},{4,12},{12,4},... | collective-permute-start | bytes 1474568 | tf_op jit(solution)/shard_map/ppermute | solution.py:404
  86.2 12.0 %copy-start.1 = (bf16[6,320,128]{2,1,0:T(8,128)(2,1)S(1)}, bf16[6,320,128]{2,1,0:T(8,128)(2,1)}, u32[]{:S(2)}) copy-start(bf16[6,320,128]{2,1,0:T(8,128)(2,1)} %get-tuple-element.35) | copy-start | bytes 1474564
  96.2 1.4 %collective-permute-start.8 = (f32[6,256]{1,0:T(8,128)S(1)}, f32[6,256]{1,0:T(8,128)S(1)}, u32[]{:S(2)}, u32[]{:S(2)}) collective-permute-start(f32[6,256]{1,0:T(8,128)S(1)} %get-tuple-element.55), channel_id=1, source_target_pairs={{0,8},{8,0},{1,9},{9,1},{2,10},{10,2},{3,11},{11,3},{4,12},{12,4},... | collective-permute-start | bytes 18440 | tf_op jit(solution)/shard_map/ppermute | solution.py:404

commit v3 on v2

--- a/solution.py
+++ b/solution.py
@@ -1,4 +1,3 @@
-import functools
 import math
 
 import jax
@@ -8,6 +7,7 @@
 from jax.experimental.pallas import tpu as pltpu
 from jax.sharding import PartitionSpec as P
 
+
 EPSILON = 1e-06
 LAT8 = 8
 TILE = 16
@@ -36,7 +36,7 @@
     return jnp.where(column == edge, 0.0, pltpu.roll(values, by % count, 1))
 
 
-def call(kernel, outs, in_specs, scratch=(), copies=0, name=None):
+def call(kernel, outs, in_specs, scratch=(), copies=0, out_specs=None):
     shapes = [pltpu.VMEM(s, d) for s, d in scratch]
     if copies:
         shapes.append(pltpu.SemaphoreType.DMA((copies,)))
@@ -44,9 +44,8 @@
         kernel,
         out_shape=[jax.ShapeDtypeStruct(s, d) for s, d in outs],
         in_specs=in_specs,
-        out_specs=[VMEM] * len(outs),
+        out_specs=out_specs or [VMEM] * len(outs),
         scratch_shapes=shapes,
-        name=name,
     )
 
 
@@ -58,64 +57,6 @@
 def coefficient(times_ref, step):
     stamp = jnp.full((LAT8, 128), times_ref[step], jnp.int32)
     return (stamp.astype(F32) + 1.0) / 1000.0
-
-
-def prep_kernel(gated_ref, enc_ref, dec_ref, down_ref, tmid_ref, time_ref, enc_out, dec_out, down_out, tmid_out, bias_out):
-    chans = enc_ref.shape[3]
-    for src, dst in ((enc_ref, enc_out), (dec_ref, dec_out)):
-        for dy in range(3):
-            for dx in range(3):
-                dst[dx * chans : (dx + 1) * chans, dy * chans : (dy + 1) * chans] = src[dy, dx].T
-    for dy in range(3):
-        for dx in range(3):
-            lane = (3 * dy + dx) * chans
-            down_out[:, lane : lane + chans] = down_ref[dy, dx].T
-        tmid_out[dy] = tmid_ref[dy].T
-    biases = dot(gated_ref[...], time_ref[...])
-    turned = biases.T
-    for step in range(bias_out.shape[0]):
-        bias_out[step] = jnp.broadcast_to(turned[:, step : step + 1], bias_out.shape[1:])
-
-
-def spread_rows(acat_ref, row, value, cols, chans):
-    for dy in range(3):
-        start = pl.multiple_of((row - dy + 2) * cols, cols)
-        acat_ref[dy * chans : (dy + 1) * chans, pl.ds(start, cols)] = value
-
-
-def conv_sum(acc_ref, row, cols, chans):
-    span = pl.ds(pl.multiple_of(row * cols, cols), cols)
-    return (
-        acc_ref[chans : 2 * chans, span]
-        + shifted(acc_ref[:chans, span], 1)
-        + shifted(acc_ref[2 * chans :, span], -1)
-    )
-
-
-def encode_rows(read_row, w_in, wcat_ref, bias_ref, copies, border, out_ref, lift_ref, acat_ref, acc_ref):
-    count, chans, cols = out_ref.shape
-    is_first, is_last = edges_of()
-
-    def front(row, carry):
-        lifted = lax.dot_general(
-            w_in, read_row(row), (((0,), (0,)), ((), ())), preferred_element_type=F32
-        )
-        lift_ref[row] = lifted
-        spread_rows(acat_ref, row, act(lifted).astype(BF16), cols, chans)
-        return carry
-
-    lax.fori_loop(0, count + 2, front, 0)
-    for copy in copies:
-        copy.wait()
-    acc_ref[...] = dot(wcat_ref[...], acat_ref[:, 2 * cols : (2 + count) * cols])
-
-    def back(row, carry):
-        total = lift_ref[row + 1] + conv_sum(acc_ref, row, cols, chans) + bias_ref[...]
-        outside = ((row < border) & is_first) | ((row >= count - border) & is_last)
-        out_ref[row] = jnp.where(outside, 0.0, total).astype(BF16)
-        return carry
-
-    lax.fori_loop(0, count, back, 0)
 
 
 def fetches(pairs, sems):
@@ -125,14 +66,107 @@
     return copies
 
 
+def prep_kernel(
+    gated_ref, enc_hbm, dec_hbm, down_hbm, tmid_hbm, time_hbm,
+    enc_out, dec_out, down_out, tmid_out, bias_out,
+    enc_ref, dec_ref, down_ref, tmid_ref, time_ref, enc_t, dec_t, down_t, tmid_t, bias_t, sems,
+):
+    pairs = []
+    for hbm, ref in ((enc_hbm, enc_ref), (dec_hbm, dec_ref), (down_hbm, down_ref)):
+        pairs += [(hbm.at[dy], ref.at[dy]) for dy in range(3)]
+    pairs += [(tmid_hbm.at[k], tmid_ref.at[k]) for k in range(3)] + [(time_hbm, time_ref)]
+    copies = fetches(pairs, sems)
+    count = len(pairs)
+    outs = []
+
+    def send(src, dst):
+        copy = pltpu.make_async_copy(src, dst, sems.at[count + len(outs)])
+        copy.start()
+        outs.append(copy)
+
+    arrived = iter(copies)
+    for src, turned, dst in ((enc_ref, enc_t, enc_out), (dec_ref, dec_t, dec_out), (down_ref, down_t, down_out)):
+        chans = src.shape[2]
+        for dy in range(3):
+            next(arrived).wait()
+            for dx in range(3):
+                lane = (3 * dy + dx) * chans
+                turned[:, lane : lane + chans] = src[dy, dx].T
+        send(turned, dst)
+    for k in range(3):
+        next(arrived).wait()
+        tmid_t[k] = tmid_ref[k].T
+        send(tmid_t.at[k], tmid_out.at[k])
+    next(arrived).wait()
+    biases = dot(gated_ref[...], time_ref[...]).T
+    for step in range(bias_t.shape[0]):
+        bias_t[step] = jnp.broadcast_to(biases[:, step : step + 1], bias_t.shape[1:])
+    send(bias_t, bias_out)
+    for copy in outs:
+        copy.wait()
+
+
+def store_taps(taps_ref, row, value):
+    chans, cols = value.shape
+    span = slice(row * cols, (row + 1) * cols)
+    taps_ref[:chans, span] = shifted(value, 1).astype(BF16)
+    taps_ref[chans : 2 * chans, span] = value.astype(BF16)
+    taps_ref[2 * chans :, span] = shifted(value, -1).astype(BF16)
+
+
+def conv_pairs(count, cols, front, back, w_ref, taps_ref, acc_ref, copies):
+    front(0)
+    front(2)
+    for copy in copies:
+        copy.wait()
+    for pair in range(0, count, 2):
+        window = jnp.concatenate(
+            [taps_ref[:, (pair + dy) * cols : (pair + dy + 2) * cols] for dy in range(3)], axis=0
+        )
+        acc_ref[:, pair * cols : (pair + 2) * cols] = dot(w_ref[...], window)
+        if pair + 4 <= count:
+            front(pair + 4)
+        if pair:
+            back(pair - 2)
+    back(count - 2)
+
+
+def encode_rows(read_pair, w_in, w_ref, bias_ref, copies, border, out_ref, lift_ref, taps_ref, acc_ref):
+    count, _, cols = out_ref.shape
+    is_first, is_last = edges_of()
+
+    def front(row):
+        lifted = dot(w_in, read_pair(row))
+        lift_ref[:, row * cols : (row + 2) * cols] = lifted
+        for k in range(2):
+            store_taps(taps_ref, row + k, act(lifted[:, k * cols : (k + 1) * cols]))
+
+    def back(pair):
+        for row in (pair, pair + 1):
+            here = slice(row * cols, (row + 1) * cols)
+            there = slice((row + 1) * cols, (row + 2) * cols)
+            total = lift_ref[:, there] + acc_ref[:, here] + bias_ref[...]
+            if row < border:
+                total = jnp.where(is_first, 0.0, total)
+            if row >= count - border:
+                total = jnp.where(is_last, 0.0, total)
+            out_ref[row] = total.astype(BF16)
+
+    conv_pairs(count, cols, front, back, w_ref, taps_ref, acc_ref, copies)
+
+
+def turned_w_in(w_small_ref):
+    return w_small_ref[9 * LAT8 :, :].astype(F32).T.astype(BF16)
+
+
 def enc_first_kernel(
-    x_ref, taps_ref, wcat_hbm, bias_hbm, out_ref, wcat_ref, bias_ref, lift_ref, acat_ref, acc_ref, sems
+    x_ref, w_small_ref, w_hbm, bias_hbm, out_ref, w_ref, bias_ref, lift_ref, taps_ref, acc_ref, sems
 ):
     chans = out_ref.shape[1]
-    copies = fetches(((wcat_hbm, wcat_ref), (bias_hbm.at[0, :chans], bias_ref)), sems)
+    copies = fetches(((w_hbm, w_ref), (bias_hbm.at[0, :chans], bias_ref)), sems)
     encode_rows(
-        lambda row: x_ref[row].astype(BF16), taps_ref[9 * LAT8 :, :], wcat_ref, bias_ref, copies, 2,
-        out_ref, lift_ref, acat_ref, acc_ref,
+        lambda row: jnp.concatenate([x_ref[row], x_ref[row + 1]], axis=1).astype(BF16),
+        turned_w_in(w_small_ref), w_ref, bias_ref, copies, 2, out_ref, lift_ref, taps_ref, acc_ref,
     )
 
 
@@ -141,11 +175,11 @@
 
 
 def enc_last_kernel(
-    base_ref, near_ref, one_ref, two_ref, taps_ref, wcat_hbm, bias_hbm,
-    out_ref, x_ref, ext_ref, wcat_ref, bias_ref, lift_ref, acat_ref, acc_ref, sems,
+    base_ref, near_ref, one_ref, two_ref, w_small_ref, w_hbm, bias_hbm,
+    out_ref, x_ref, w_ref, bias_ref, lift_ref, taps_ref, acc_ref, sems,
 ):
     chans = out_ref.shape[1]
-    copies = fetches(((wcat_hbm, wcat_ref), (bias_hbm.at[1, :chans], bias_ref)), sems)
+    copies = fetches(((w_hbm, w_ref), (bias_hbm.at[1, :chans], bias_ref)), sems)
     rows = base_ref.shape[0]
     even = lax.axis_index("rows") % 2 == 0
     is_first, is_last = edges_of()
@@ -159,15 +193,19 @@
 
     from_up, base_up = received(True)
     from_down, base_down = received(False)
-    x_ref[...] = base_ref[...]
-    x_ref[0] = x_ref[0] - from_up
-    x_ref[rows - 1] = x_ref[rows - 1] - from_down
-    ext_ref[0] = jnp.where(is_first, 0.0, base_up - near_ref[0]).astype(BF16)
-    ext_ref[rows + 1] = jnp.where(is_last, 0.0, base_down - near_ref[1]).astype(BF16)
-    ext_ref[1 : rows + 1] = x_ref[...].astype(BF16)
+    ext = [base_ref[row] for row in range(rows)]
+    ext[0] = ext[0] - from_up
+    ext[-1] = ext[-1] - from_down
+    for row in range(rows):
+        x_ref[row] = ext[row]
+    ext = (
+        [jnp.where(is_first, 0.0, base_up - near_ref[0])]
+        + ext
+        + [jnp.where(is_last, 0.0, base_down - near_ref[1])]
+    )
     encode_rows(
-        lambda row: ext_ref[row], taps_ref[9 * LAT8 :, :], wcat_ref, bias_ref, copies, 0,
-        out_ref, lift_ref, acat_ref, acc_ref,
+        lambda row: jnp.concatenate(ext[row : row + 2], axis=1).astype(BF16),
+        turned_w_in(w_small_ref), w_ref, bias_ref, copies, 0, out_ref, lift_ref, taps_ref, acc_ref,
     )
 
 
@@ -278,36 +316,34 @@
         out_ref[row] = wide[:, low * cols : (low + 1) * cols]
 
 
-def decode_rows(count, cols, wcat_ref, w_skip_ref, bias_ref, copies, border, taps_ref, jcat_ref, mixed_ref, acat_ref, acc_ref, o_ref):
-    chans = bias_ref.shape[0]
+def decode_rows(count, cols, read_joined, w_ref, w_skip_ref, bias_ref, copies, border, w_small_ref, mixed_ref, taps_ref, acc_ref):
     is_first, is_last = edges_of()
-    mixed_ref[...] = dot(w_skip_ref[...], jcat_ref[...])
-
-    def front(row, carry):
-        mixed = mixed_ref[:, pl.ds(pl.multiple_of(row * cols, cols), cols)]
-        spread_rows(acat_ref, row, act(mixed).astype(BF16), cols, chans)
-        return carry
-
-    lax.fori_loop(0, count + 2, front, 0)
-    for copy in copies:
-        copy.wait()
-    acc_ref[...] = dot(wcat_ref[...], acat_ref[:, 2 * cols : (2 + count) * cols])
-
-    def back(row, carry):
-        mixed = mixed_ref[:, pl.ds(pl.multiple_of((row + 1) * cols, cols), cols)]
-        value = act(mixed + conv_sum(acc_ref, row, cols, chans) + bias_ref[...])
-        outside = ((row < border) & is_first) | ((row >= count - border) & is_last)
-        span = pl.ds(pl.multiple_of(row * cols, cols), cols)
-        o_ref[:, span] = jnp.where(outside, 0.0, value).astype(BF16)
-        return carry
-
-    lax.fori_loop(0, count, back, 0)
-    taps = dot(taps_ref[: 9 * LAT8, :], o_ref[...])
     span = 3 * LAT8
     parts = []
-    for row in range(count):
-        tap = taps[:, row * cols : (row + 1) * cols]
-        parts.append(shifted(tap[:span], 1) + tap[span : 2 * span] + shifted(tap[2 * span :], -1))
+
+    def front(row):
+        mixed = dot(w_skip_ref[...], jnp.concatenate([read_joined(row), read_joined(row + 1)], axis=1))
+        mixed_ref[:, row * cols : (row + 2) * cols] = mixed
+        for k in range(2):
+            store_taps(taps_ref, row + k, act(mixed[:, k * cols : (k + 1) * cols]))
+
+    def back(pair):
+        outs = []
+        for row in (pair, pair + 1):
+            here = slice(row * cols, (row + 1) * cols)
+            there = slice((row + 1) * cols, (row + 2) * cols)
+            value = act(mixed_ref[:, there] + acc_ref[:, here] + bias_ref[...])
+            if row < border:
+                value = jnp.where(is_first, 0.0, value)
+            if row >= count - border:
+                value = jnp.where(is_last, 0.0, value)
+            outs.append(value.astype(BF16))
+        taps = dot(w_small_ref[: 9 * LAT8, :], jnp.concatenate(outs, axis=1))
+        for k in range(2):
+            tap = taps[:, k * cols : (k + 1) * cols]
+            parts.append(shifted(tap[:span], 1) + tap[span : 2 * span] + shifted(tap[2 * span :], -1))
+
+    conv_pairs(count, cols, front, back, w_ref, taps_ref, acc_ref, copies)
     return parts
 
 
@@ -322,18 +358,16 @@
 
 
 def dec_first_kernel(
-    times_ref, enc_ref, mid_ref, x_ref, w_skip_ref, taps_ref, wcat_hbm, bias_hbm,
-    base_ref, near_ref, jcat_ref, wcat_ref, bias_ref, mixed_ref, acat_ref, acc_ref, o_ref, sems,
+    times_ref, enc_ref, mid_ref, x_ref, w_skip_ref, w_small_ref, w_hbm, bias_hbm,
+    base_ref, near_ref, w_ref, bias_ref, mixed_ref, taps_ref, acc_ref, sems,
 ):
     rows = base_ref.shape[0]
     chans, cols = enc_ref.shape[1:]
     start = bias_hbm.shape[1] - chans
-    copies = fetches(((wcat_hbm, wcat_ref), (bias_hbm.at[0, start:], bias_ref)), sems)
-    for row in range(rows + 2):
-        jcat_ref[:chans, row * cols : (row + 1) * cols] = mid_ref[row]
-        jcat_ref[chans:, row * cols : (row + 1) * cols] = enc_ref[row]
+    copies = fetches(((w_hbm, w_ref), (bias_hbm.at[0, start:], bias_ref)), sems)
     parts = decode_rows(
-        rows, cols, wcat_ref, w_skip_ref, bias_ref, copies, 0, taps_ref, jcat_ref, mixed_ref, acat_ref, acc_ref, o_ref
+        rows, cols, lambda row: jnp.concatenate([mid_ref[row], enc_ref[row]], axis=0),
+        w_ref, w_skip_ref, bias_ref, copies, 0, w_small_ref, mixed_ref, taps_ref, acc_ref,
     )
     coef = coefficient(times_ref, 0)
     halo = (x_ref.shape[0] - rows) // 2
@@ -344,30 +378,30 @@
 
 
 def dec_last_kernel(
-    times_ref, enc_ref, mid_ref, one_ref, two_ref, x_ref, w_skip_ref, taps_ref, wcat_hbm, bias_hbm,
-    next_ref, jcat_ref, wcat_ref, bias_ref, mixed_ref, acat_ref, acc_ref, o_ref, sems,
+    times_ref, enc_ref, mid_ref, one_ref, two_ref, x_ref, w_skip_ref, w_small_ref, w_hbm, bias_hbm,
+    next_ref, wide_ref, w_ref, bias_ref, mixed_ref, taps_ref, acc_ref, sems,
 ):
     rows = x_ref.shape[0]
     chans, cols = enc_ref.shape[1:]
     start = bias_hbm.shape[1] - chans
-    copies = fetches(((wcat_hbm, wcat_ref), (bias_hbm.at[1, start:], bias_ref)), sems)
+    copies = fetches(((w_hbm, w_ref), (bias_hbm.at[1, start:], bias_ref)), sems)
     half = cols // 2
     inner = rows // 2
     even = lax.axis_index("rows") % 2 == 0
     packed = chans // 2
-    wide = dot(mid_ref[...], doubling(half, inner)).astype(BF16)
+    wide_ref[:, cols : (inner + 1) * cols] = dot(mid_ref[...], doubling(half, inner)).astype(BF16)
     twice = doubling(half, 1)
-    for low in range(inner + 2):
-        if 1 <= low <= inner:
-            piece = wide[:, (low - 1) * cols : low * cols]
-        else:
-            folded = neighbour(even, one_ref[:packed, :], two_ref[:packed, :], low == 0)
-            piece = dot(jnp.concatenate([folded[:, :half], folded[:, half:]], axis=0), twice).astype(BF16)
-        for row in (2 * low, 2 * low + 1):
-            jcat_ref[:chans, row * cols : (row + 1) * cols] = piece
-            jcat_ref[chans:, row * cols : (row + 1) * cols] = enc_ref[row]
+    for low in (0, inner + 1):
+        folded = neighbour(even, one_ref[:packed, :], two_ref[:packed, :], low == 0)
+        piece = jnp.concatenate([folded[:, :half], folded[:, half:]], axis=0)
+        wide_ref[:, low * cols : (low + 1) * cols] = dot(piece, twice).astype(BF16)
+
+    def joined(row):
+        low = row // 2
+        return jnp.concatenate([wide_ref[:, low * cols : (low + 1) * cols], enc_ref[row]], axis=0)
+
     parts = decode_rows(
-        rows + 2, cols, wcat_ref, w_skip_ref, bias_ref, copies, 1, taps_ref, jcat_ref, mixed_ref, acat_ref, acc_ref, o_ref
+        rows + 2, cols, joined, w_ref, w_skip_ref, bias_ref, copies, 1, w_small_ref, mixed_ref, taps_ref, acc_ref
     )
     coef = coefficient(times_ref, 1)
     for row in range(rows):
@@ -382,7 +416,7 @@
     return jnp.pad(gated, ((0, TILE - gated.shape[0]), (0, 0)))
 
 
-def body(latent, stale, timesteps, w_in, w_enc, w_down, w_tmid, w_up, w_skip, w_dec, w_out, w_time):
+def step_pair(latent, stale, timesteps, w_in, w_enc, w_down, w_tmid, w_up, w_skip, w_dec, w_out, w_time):
     segment = lax.axis_index("segment")
     first = segment == 0
     size = lax.axis_size("rows")
@@ -404,7 +438,9 @@
         return lax.ppermute(value, "segment", [(0, 1), (1, 0)])
 
     def exchange(one, two):
-        return lax.ppermute(one, "rows", paired(0)), lax.ppermute(two, "rows", paired(1))
+        got_one = lax.ppermute(one, "rows", paired(0))
+        got_two = lax.ppermute(two, "rows", paired(1))
+        return got_one, got_two
 
     def mine(value, axis=0):
         return lax.dynamic_index_in_dim(value, segment, axis, keepdims=False)
@@ -449,54 +485,39 @@
     wide = 3 * chans
     total = w_time.shape[1]
 
+    turned = [
+        ((chans, 3 * wide), BF16),
+        ((chans, 3 * wide), BF16),
+        ((mid, 3 * wide), BF16),
+        ((3, mid, mid), BF16),
+        ((timesteps.shape[0], total, cols), F32),
+    ]
+    weights = (w_enc, w_dec, w_down, w_tmid, w_time)
+    gated = gated_times(timesteps, w_time.shape[0] // 2)
     enc_cat, dec_cat, w_down_t, w_tmid_t, bias = call(
-        prep_kernel,
-        [
-            ((wide, wide), BF16),
-            ((wide, wide), BF16),
-            ((mid, 3 * wide), BF16),
-            ((3, mid, mid), BF16),
-            ((timesteps.shape[0], total, cols), F32),
-        ],
-        [VMEM] * 6,
-        name="prep",
-    )(gated_times(timesteps, w_time.shape[0] // 2), w_enc, w_dec, w_down, w_tmid, w_time)
+        prep_kernel, turned, [VMEM] + [ANY] * 5, [(w.shape, BF16) for w in weights] + turned, 20, [ANY] * 5
+    )(gated, *weights)
 
     def enc_scratch(count):
         return [
-            ((wide, wide), BF16),
-            ((chans, cols), F32),
-            ((count + 2, chans, cols), F32),
-            ((wide, (count + 4) * cols), BF16),
-            ((wide, count * cols), F32),
-        ]
-
-    def dec_scratch(count):
-        return [
-            ((2 * chans, (count + 2) * cols), BF16),
-            ((wide, wide), BF16),
+            ((chans, 3 * wide), BF16),
             ((chans, cols), F32),
             ((chans, (count + 2) * cols), F32),
-            ((wide, (count + 4) * cols), BF16),
-            ((wide, count * cols), F32),
-            ((chans, count * cols), BF16),
+            ((wide, (count + 2) * cols), BF16),
+            ((chans, count * cols), F32),
         ]
 
+    dec_scratch = enc_scratch
     down_scratch = [((mid, 3 * wide), BF16), ((mid, cols), F32), ((3 * wide, low), BF16)]
     down_outs = [((mid, low), F32), ((mid, low), BF16)]
     ext = ((rows + 2, chans, cols), BF16)
     low0, q0, enc0, mid0 = call(
-        down_first_kernel, down_outs + [ext, ext], [VMEM] * 5 + [ANY] * 2, down_scratch, 2, "down_first"
+        down_first_kernel, down_outs + [ext, ext], [VMEM] * 5 + [ANY] * 2, down_scratch, 2
     )(chan_major, got, one, two, far, w_down_t, bias)
     q0_other = swap(q0)
 
     (enc1,) = call(
-        enc_first_kernel,
-        [((rows + 4, chans, cols), BF16)],
-        [VMEM] * 2 + [ANY] * 2,
-        enc_scratch(rows + 4),
-        2,
-        "enc_first",
+        enc_first_kernel, [((rows + 4, chans, cols), BF16)], [VMEM] * 2 + [ANY] * 2, enc_scratch(rows + 4), 2
     )(x_t, taps, enc_cat, bias)
 
     base, near = call(
@@ -505,31 +526,25 @@
         [SMEM] + [VMEM] * 5 + [ANY] * 2,
         dec_scratch(rows),
         2,
-        "dec_first",
     )(timesteps, enc0, mid0, x_t, w_skip_t, taps, dec_cat, bias)
 
     bundle = ((chans // 2 + 2 * TILE, cols), BF16)
     mid1, to_one, to_two = call(
-        mid_first_kernel, [((chans, low), BF16), bundle, bundle], [VMEM] * 7, name="mid_first"
+        mid_first_kernel, [((chans, low), BF16), bundle, bundle], [VMEM] * 7
     )(low0, q0, q0_other, w_tmid_t, w_up_t, base, near)
     got_one, got_two = exchange(to_one, to_two)
 
-    low1, q1 = call(
-        down_last_kernel, down_outs, [VMEM] + [ANY] * 2, down_scratch, 2, "down_last"
-    )(enc1, w_down_t, bias)
+    low1, q1 = call(down_last_kernel, down_outs, [VMEM] + [ANY] * 2, down_scratch, 2)(enc1, w_down_t, bias)
     q1_other = swap(q1)
 
-    (mid2,) = call(mid_last_kernel, [((rows, chans, cols), BF16)], [VMEM] * 5, name="mid_last")(
-        low1, q1, q1_other, w_tmid_t, w_up_t
-    )
+    (mid2,) = call(mid_last_kernel, [((rows, chans, cols), BF16)], [VMEM] * 5)(low1, q1, q1_other, w_tmid_t, w_up_t)
 
     enc2, x1 = call(
         enc_last_kernel,
         [((rows, chans, cols), BF16), ((rows, LAT8, cols), F32)],
         [VMEM] * 5 + [ANY] * 2,
-        [((rows + 2, LAT8, cols), BF16)] + enc_scratch(rows),
+        enc_scratch(rows),
         2,
-        "enc_last",
     )(base, near, got_one, got_two, taps, enc_cat, bias)
 
     feat_other = swap(jnp.where(first, mid2, enc2))
@@ -538,9 +553,8 @@
         dec_last_kernel,
         [((rows, LAT8, cols), F32)],
         [SMEM] + [VMEM] * 7 + [ANY] * 2,
-        dec_scratch(rows + 2),
+        [((chans, (rows // 2 + 2) * cols), BF16)] + dec_scratch(rows + 2),
         2,
-        "dec_last",
     )(timesteps, enc1, mid1, got_one, got_two, x1, w_skip_t, taps, dec_cat, bias)
 
     flat = x2[:, :lat].transpose(0, 2, 1).reshape(rows, cols * lat)
@@ -558,7 +572,7 @@
         P("clips"),
     ) + (P(),) * 9
     return jax.shard_map(
-        body,
+        step_pair,
         mesh=mesh,
         in_specs=placed,
         out_specs=(P("clips", "rows", "segment"), P("segment", "clips", "rows", None, None)),

time: 100 us -> 91.9 us (0.919)
  the two profiles are of different devices: /device:TPU:13 before, /device:TPU:7 now
where the time goes in v3:
time: 91.9 us; the launch traced here: 91 us
  Pallas kernels  55.9 us (61%)
  starting transfers between devices  13.2 us (14%)
  local copies, waits for them, and re-layouts  12.3 us (13%)
  waiting for transfers between devices  4.51 us (5%)
  other arithmetic  3.98 us (4%)
  between operations  1.09 us (1%)
    pallas_call x1, Pallas kernels, step_pair(): call(prep_kernel, turned, [VMEM] + [ANY] * 5, [(w.shape, BF16) for w in w...  9.64 us
    ppermute x2, starting transfers between devices, exchange(): got_two = lax.ppermute(two, 'rows', paired(1))  8.52 us
    pallas_call x1, Pallas kernels, step_pair(): call(dec_first_kernel, [((rows, LAT8, cols), F32), ((2, LAT8, cols), F32)...  7.29 us
    pallas_call x1, Pallas kernels, step_pair(): call(dec_last_kernel, [((rows, LAT8, cols), F32)], [SMEM] + [VMEM] * 7 +...  6.79 us
    pallas_call x1, Pallas kernels, step_pair(): call(enc_first_kernel, [((rows + 4, chans, cols), BF16)], [VMEM] * 2 + [A...  6.54 us
    pallas_call x1, Pallas kernels, step_pair(): call(down_first_kernel, down_outs + [ext, ext], [VMEM] * 5 + [ANY] * 2, d...  6.48 us
    pallas_call x1, Pallas kernels, step_pair(): call(down_last_kernel, down_outs, [VMEM] + [ANY] * 2, down_scratch, 2)  5.57 us
    unnamed x30, local copies, waits for them, and re-layouts  5.43 us
  transfers between devices with their start and end apart: 11, of which 3 were waited for; matrix products, arithmetic and copies ran while one was open for 11% of the time, Pallas kernels for 48%

profile of v3, /device:TPU:7, one launch (start us, length us, event | category | flops | bytes accessed | tf_op | source)
XLA Modules:
  0.0 91.0 jit_solution(3301463406666621636)
XLA Ops:
  0.6 0.8 dynamic-slice_reduce_fusion
  1.5 0.7 collective-permute-start.3
  2.2 1.1 %dynamic-slice_bitcast_fusion = bf16[6,320,128]{2,1,0:T(8,128)(2,1)S(1)} fusion(bf16[1,2,6,128,320]{3,4,2,1,0:T(8,128)(2,1)} %param.13, s32[]{:T(128)S(6)} %select_n.107), kind=kLoop, calls=%fused_computation.4 | loop fusion | bytes 983044 | tf_op jit(solution)/shard_map/jit(dynamic_index_in_dim)/squeeze | solution.py:449
  3.3 0.1 collective-permute-start.4
  3.4 0.7 convert.8
  4.1 1.3 %copy.39 = bf16[1,2,6,128,320]{3,4,1,2,0:T(8,128)(2,1)S(1)} copy(bf16[1,2,6,128,320]{3,4,2,1,0:T(8,128)(2,1)} %param.13) | data formatting | bytes 1966080 | tf_op args[1]
  5.6 0.3 collective-permute-start.1
  5.9 4.1 %collective-permute-start = (bf16[2,336,128]{2,1,0:T(8,128)(2,1)S(1)}, bf16[2,336,128]{2,1,0:T(8,128)(2,1)S(1)}, u32[]{:S(2)}, u32[]{:S(2)}) collective-permute-start(bf16[2,336,128]{2,1,0:T(8,128)(2,1)S(1)} %get-tuple-element.47), channel_id=1, source_target_pairs={{1,2},{2,1},{3,4},{4,3},{5,6},{6,5},{9,10},{10,9},{11,12},{12,11},... | collective-permute-start | bytes 516104 | tf_op jit(solution)/shard_map/ppermute | solution.py:442
  10.0 0.1 multiply_sine_fusion
  10.2 0.9 collective-permute-done.1.one_ref
  11.1 2.8 %collective-permute-done.two_ref = bf16[2,336,128]{2,1,0:T(8,128)(2,1)S(1)} collective-permute-done((bf16[2,336,128]{2,1,0:T(8,128)(2,1)S(1)}, bf16[2,336,128]{2,1,0:T(8,128)(2,1)S(1)}, u32[]{:S(2)}, u32[]{:S(2)}) %collective-permute-start) | collective-permute-done | bytes 172064 | tf_op jit(solution)/shard_map/ppermute | solution.py:442
  13.9 2.3 %collective-permute-start.2 = (bf16[2,336,128]{2,1,0:T(8,128)(2,1)S(1)}, bf16[2,336,128]{2,1,0:T(8,128)(2,1)S(1)}, u32[]{:S(2)}, u32[]{:S(2)}) collective-permute-start(bf16[2,336,128]{2,1,0:T(8,128)(2,1)S(1)} %pad_maximum_fusion), channel_id=1, source_target_pairs={{0,8},{8,0},{1,9},{9,1},{2,10},{10,2},{3,11},{11,3},{4,12},{12,4},... | collective-permute-start | bytes 516104 | tf_op jit(solution)/shard_map/ppermute | solution.py:438
  16.3 0.6 fusion.6.w_small_ref
  17.0 0.6 pad.28.gated_ref
  17.6 0.2 concatenate.32
  17.8 0.1 copy.24
  17.9 1.0 %copy.31.own_ref = bf16[1,2,6,320,128]{4,3,2,1,0:T(8,128)(2,1)} copy(bf16[1,2,6,320,128]{4,3,1,2,0:T(8,128)(2,1)S(1)} %bitcast.40) | data formatting | bytes 1966080 | tf_op jit(solution)/shard_map/transpose | solution.py:424
  18.9 9.6 %shard_map.131 = (bf16[320,2880]{1,0:T(8,128)(2,1)}, bf16[320,2880]{1,0:T(8,128)(2,1)}, bf16[640,2880]{1,0:T(8,128)(2,1)}, bf16[3,640,640]{2,1,0:T(8,128)(2,1)}, f32[2,1280,128]{2,1,0:T(8,128)}) custom-call(bf16[16,320]{1,0:T(8,128)(2,1)} %pad.28.gated_ref, bf16[3,3,320,320]{3,2,1,0:T(8,128)(2,1)} %enc_hbm.1, bf16[3,3,320,320]{3,2,1,0:T(8,128)(2,1)} %dec_hbm.1, ...), custom_call_target="tpu_custom_call" | custom-call | tf_op jit(solution)/shard_map/pallas_call | solution.py:497
  28.6 0.2 concatenate.34
  28.8 0.1 copy.28
  29.0 0.1 reshape.84
  29.2 0.1 reshape.85
  29.4 0.1 reshape.83
  29.6 0.1 reshape.82
  29.9 0.8 copy-done.3
  30.7 6.5 %shard_map.133 = (f32[640,192]{1,0:T(8,128)}, bf16[640,192]{1,0:T(8,128)(2,1)}, bf16[8,320,128]{2,1,0:T(8,128)(2,1)}, bf16[8,320,128]{2,1,0:T(8,128)(2,1)}) custom-call(bf16[1,2,6,320,128]{4,3,2,1,0:T(8,128)(2,1)} %copy.31.own_ref, bf16[6,320,128]{2,1,0:T(8,128)(2,1)} %copy-done.3, bf16[2,336,128]{2,1,0:T(8,128)(2,1)} %copy-done.4, ...), custom_call_target="tpu_custom_call" | custom-call | tf_op jit(solution)/shard_map/pallas_call | solution.py:514
  37.4 0.6 pad.25.x_ref
  38.0 6.5 %shard_map.132.enc_ref = bf16[10,320,128]{2,1,0:T(8,128)(2,1)} custom-call(f32[12,8,128]{2,1,0:T(8,128)} %pad.25.x_ref, bf16[80,320]{1,0:T(8,128)(2,1)} %fusion.6.w_small_ref, bf16[320,2880]{1,0:T(8,128)(2,1)} %get-tuple-element.20.w_hbm, f32[2,1280,128]{2,1,0:T(8,128)} %get-tuple-element.21.bias_hbm), custom_call_target="tpu_custom_call" | custom-call | tf_op jit(solution)/shard_map/pallas_call | solution.py:519
  44.5 5.6 %shard_map.138 = (f32[640,192]{1,0:T(8,128)}, bf16[640,192]{1,0:T(8,128)(2,1)}) custom-call(bf16[10,320,128]{2,1,0:T(8,128)(2,1)} %shard_map.132.enc_ref, bf16[640,2880]{1,0:T(8,128)(2,1)} %get-tuple-element.22.w_hbm, f32[2,1280,128]{2,1,0:T(8,128)} %get-tuple-element.21.bias_hbm), custom_call_target="tpu_custom_call" | custom-call | tf_op jit(solution)/shard_map/pallas_call | solution.py:537
  50.1 0.6 collective-permute-start.9
  50.7 7.3 %shard_map.134 = (f32[6,8,128]{2,1,0:T(8,128)}, f32[2,8,128]{2,1,0:T(8,128)}) custom-call(s32[2]{0:T(128)} %times_ref.3, bf16[8,320,128]{2,1,0:T(8,128)(2,1)} %get-tuple-element.26.enc_ref, bf16[8,320,128]{2,1,0:T(8,128)(2,1)} %get-tuple-element.27.mid_ref, f32[12,8,128]{2,1,0:T(8,128)} %pad.25.x_ref, bf16[320,640]{1,0:T(8,128)(2,1)} %bitcast.45, ...), custom_call_target="tpu_custom_call" | custom-call | tf_op jit(solution)/shard_map/pallas_call | solution.py:523
  58.0 0.8 copy-done.7
  58.7 3.9 %shard_map.135 = (bf16[320,192]{1,0:T(8,128)(2,1)}, bf16[192,128]{1,0:T(8,128)(2,1)}, bf16[192,128]{1,0:T(8,128)(2,1)}) custom-call(f32[640,192]{1,0:T(8,128)} %get-tuple-element.23.low_ref, bf16[640,192]{1,0:T(8,128)(2,1)} %get-tuple-element.24.q_ref, bf16[640,192]{1,0:T(8,128)(2,1)} %copy-done.7, bf16[3,640,640]{2,1,0:T(8,128)(2,1)} %get-tuple-element.25.w_tmid_ref, ...), custom_call_target="tpu_custom_call" | custom-call | tf_op jit(solution)/shard_map/pallas_call | solution.py:532
  62.7 4.4 %collective-permute-start.7 = (bf16[192,128]{1,0:T(8,128)(2,1)}, bf16[192,128]{1,0:T(8,128)(2,1)S(1)}, u32[]{:S(2)}, u32[]{:S(2)}) collective-permute-start(bf16[192,128]{1,0:T(8,128)(2,1)} %get-tuple-element.33), channel_id=1, source_target_pairs={{1,2},{2,1},{3,4},{4,3},{5,6},{6,5},{9,10},{10,9},{11,12},{12,11},... | collective-permute-start | bytes 147464 | tf_op jit(solution)/shard_map/ppermute | solution.py:442
  67.1 0.7 copy-done.6
  67.8 4.3 %shard_map.139 = bf16[6,320,128]{2,1,0:T(8,128)(2,1)} custom-call(f32[640,192]{1,0:T(8,128)} %get-tuple-element.36.low_ref, bf16[640,192]{1,0:T(8,128)(2,1)} %get-tuple-element.37.q_ref, bf16[640,192]{1,0:T(8,128)(2,1)} %copy-done.6, bf16[3,640,640]{2,1,0:T(8,128)(2,1)} %get-tuple-element.25.w_tmid_ref, bf16[320,640]{1,0:T(8,128)(2,1)} %bitcast.44), custom_call_target="tpu_custom_call" | custom-call | tf_op jit(solution)/shard_map/pallas_call | solution.py:540
  72.2 0.6 copy-done.8
  72.8 0.6 copy-done.9
  73.4 5.4 %shard_map.136 = (bf16[6,320,128]{2,1,0:T(8,128)(2,1)}, f32[6,8,128]{2,1,0:T(8,128)}) custom-call(f32[6,8,128]{2,1,0:T(8,128)} %get-tuple-element.29.base_ref, f32[2,8,128]{2,1,0:T(8,128)} %get-tuple-element.30.near_ref, bf16[192,128]{1,0:T(8,128)(2,1)} %copy-done.8, bf16[192,128]{1,0:T(8,128)(2,1)} %copy-done.9, bf16[80,320]{1,0:T(8,128)(2,1)} %fusion.6.w_small_ref, ...), custom_call_target="tpu_custom_call" | custom-call | tf_op jit(solution)/shard_map/pallas_call | solution.py:542
  78.8 1.1 %broadcast_select_fusion = bf16[6,320,128]{2,1,0:T(8,128)(2,1)S(1)} fusion(bf16[6,320,128]{2,1,0:T(8,128)(2,1)S(1)} %copy-done, bf16[6,320,128]{2,1,0:T(8,128)(2,1)} %get-tuple-element.35, pred[]{:T(512)S(6)} %eq.8), kind=kLoop, calls=%fused_computation.5 | loop fusion | flops 245760 | bytes 1474561 | tf_op jit(solution)/shard_map/jit(_where)/select_n | solution.py:550
  80.0 6.8 %shard_map.137 = f32[6,8,128]{2,1,0:T(8,128)} custom-call(s32[2]{0:T(128)} %times_ref.3, bf16[10,320,128]{2,1,0:T(8,128)(2,1)} %shard_map.132.enc_ref, bf16[320,192]{1,0:T(8,128)(2,1)} %get-tuple-element.31.mid_ref, bf16[192,128]{1,0:T(8,128)(2,1)} %copy-done.8, bf16[192,128]{1,0:T(8,128)(2,1)} %copy-done.9, f32[6,8,128]{2,1,0:T(8,128)} %get-tuple-element.34.x_ref, ...), custom_call_target="tpu_custom_call" | custom-call | tf_op jit(solution)/shard_map/pallas_call | solution.py:552
  86.8 0.7 slice_bitcast_fusion.2
  87.5 0.2 copy.32
  87.7 0.2 reshape.81
  88.0 0.5 collective-permute-start.8
  88.5 0.8 collective-permute-done.8
  89.3 0.6 copy.33
  90.0 1.1 %fusion = bf16[1,2,6,128,320]{3,4,2,1,0:T(8,128)(2,1)} fusion(bf16[1,6,320,128]{3,2,1,0:T(8,128)(2,1)S(1)} %bitcast.47, bf16[1,6,320,128]{3,2,1,0:T(8,128)(2,1)S(1)} %bitcast.42, bf16[1,6,320,128]{3,2,1,0:T(8,128)(2,1)S(1)} %bitcast.41, pred[]{:T(512)S(6)} %eq.8), kind=kLoop, calls=%fused_computation.1 | loop fusion | flops 1474560 | bytes 2457601 | tf_op jit(solution)/shard_map/broadcast_in_dim | solution.py:565
  (59 shorter events, 1.0 us)
Async XLA Ops:
  0.6 9.4 %copy-start.12 = (s32[2]{0:T(128)S(1)}, s32[2]{0:T(128)}, u32[]{:S(2)}) copy-start(s32[2]{0:T(128)} %times_ref.3) | copy-start | bytes 28
  1.5 8.7 %copy-start.10 = (bf16[3,3,320,4]{2,3,1,0:T(4,128)(2,1)S(1)}, bf16[3,3,320,4]{2,3,1,0:T(4,128)(2,1)}, u32[]{:S(2)}) copy-start(bf16[3,3,320,4]{2,3,1,0:T(4,128)(2,1)} %param.22) | copy-start | bytes 69124
  1.5 27.1 %collective-permute-start.3 = (f32[6,256]{1,0:T(8,128)S(1)}, f32[6,256]{1,0:T(8,128)S(1)}, u32[]{:S(2)}, u32[]{:S(2)}) collective-permute-start(f32[6,256]{1,0:T(8,128)S(1)} %bitcast.50), channel_id=1, source_target_pairs={{0,8},{8,0},{1,9},{9,1},{2,10},{10,2},{3,11},{11,3},{4,12},{12,4},... | collective-permute-start | bytes 18440 | tf_op jit(solution)/shard_map/ppermute | solution.py:438
  3.3 13.0 %copy-start.11 = (bf16[4,320]{1,0:T(4,128)(2,1)S(1)}, bf16[4,320]{1,0:T(4,128)(2,1)}, u32[]{:S(2)}) copy-start(bf16[4,320]{1,0:T(4,128)(2,1)} %param.15) | copy-start | bytes 7684
  3.3 26.6 %collective-permute-start.4 = (bf16[6,320,128]{2,1,0:T(8,128)(2,1)S(1)}, bf16[6,320,128]{2,1,0:T(8,128)(2,1)S(1)}, u32[]{:S(2)}, u32[]{:S(2)}) collective-permute-start(bf16[6,320,128]{2,1,0:T(8,128)(2,1)S(1)} %dynamic-slice_bitcast_fusion), channel_id=1, source_target_pairs={{0,8},{8,0},{1,9},{9,1},{2,10},{10,2},{3,11},{11,3},{4,12},{12,4},... | collective-permute-start | bytes 1474568 | tf_op jit(solution)/shard_map/ppermute | solution.py:438
  5.6 5.5 %collective-permute-start.1 = (bf16[2,336,128]{2,1,0:T(8,128)(2,1)S(1)}, bf16[2,336,128]{2,1,0:T(8,128)(2,1)S(1)}, u32[]{:S(2)}, u32[]{:S(2)}) collective-permute-start(bf16[2,336,128]{2,1,0:T(8,128)(2,1)S(1)} %get-tuple-element.46), channel_id=1, source_target_pairs={{0,1},{1,0},{2,3},{3,2},{4,5},{5,4},{6,7},{7,6},{8,9},{9,8},{10,11... | collective-permute-start | bytes 516104 | tf_op jit(solution)/shard_map/ppermute | solution.py:441
  5.9 8.0 %collective-permute-start = (bf16[2,336,128]{2,1,0:T(8,128)(2,1)S(1)}, bf16[2,336,128]{2,1,0:T(8,128)(2,1)S(1)}, u32[]{:S(2)}, u32[]{:S(2)}) collective-permute-start(bf16[2,336,128]{2,1,0:T(8,128)(2,1)S(1)} %get-tuple-element.47), channel_id=1, source_target_pairs={{1,2},{2,1},{3,4},{4,3},{5,6},{6,5},{9,10},{10,9},{11,12},{12,11},... | collective-permute-start | bytes 516104 | tf_op jit(solution)/shard_map/ppermute | solution.py:442
  11.1 17.9 %copy-start.4 = (bf16[2,336,128]{2,1,0:T(8,128)(2,1)}, bf16[2,336,128]{2,1,0:T(8,128)(2,1)S(1)}, u32[]{:S(2)}) copy-start(bf16[2,336,128]{2,1,0:T(8,128)(2,1)S(1)} %collective-permute-done.1.one_ref) | copy-start | bytes 516100
  13.9 15.0 %copy-start.5 = (bf16[2,336,128]{2,1,0:T(8,128)(2,1)}, bf16[2,336,128]{2,1,0:T(8,128)(2,1)S(1)}, u32[]{:S(2)}) copy-start(bf16[2,336,128]{2,1,0:T(8,128)(2,1)S(1)} %collective-permute-done.two_ref) | copy-start | bytes 516100
  13.9 15.0 %collective-permute-start.2 = (bf16[2,336,128]{2,1,0:T(8,128)(2,1)S(1)}, bf16[2,336,128]{2,1,0:T(8,128)(2,1)S(1)}, u32[]{:S(2)}, u32[]{:S(2)}) collective-permute-start(bf16[2,336,128]{2,1,0:T(8,128)(2,1)S(1)} %pad_maximum_fusion), channel_id=1, source_target_pairs={{0,8},{8,0},{1,9},{9,1},{2,10},{10,2},{3,11},{11,3},{4,12},{12,4},... | collective-permute-start | bytes 516104 | tf_op jit(solution)/shard_map/ppermute | solution.py:438
  28.9 1.0 %copy-start.2 = (bf16[2,336,128]{2,1,0:T(8,128)(2,1)}, bf16[2,336,128]{2,1,0:T(8,128)(2,1)S(1)}, u32[]{:S(2)}) copy-start(bf16[2,336,128]{2,1,0:T(8,128)(2,1)S(1)} %collective-permute-done.2.far_ref) | copy-start | bytes 516100
  29.9 0.8 copy-start.3
  37.2 20.8 %collective-permute-start.5 = (bf16[640,192]{1,0:T(8,128)(2,1)}, bf16[640,192]{1,0:T(8,128)(2,1)S(1)}, u32[]{:S(2)}, u32[]{:S(2)}) collective-permute-start(bf16[640,192]{1,0:T(8,128)(2,1)} %get-tuple-element.24.q_ref), channel_id=1, source_target_pairs={{0,8},{8,0},{1,9},{9,1},{2,10},{10,2},{3,11},{11,3},{4,12},{12,4},... | collective-permute-start | bytes 737288 | tf_op jit(solution)/shard_map/ppermute | solution.py:438
  50.1 17.0 %collective-permute-start.9 = (bf16[640,192]{1,0:T(8,128)(2,1)}, bf16[640,192]{1,0:T(8,128)(2,1)S(1)}, u32[]{:S(2)}, u32[]{:S(2)}) collective-permute-start(bf16[640,192]{1,0:T(8,128)(2,1)} %get-tuple-element.37.q_ref), channel_id=1, source_target_pairs={{0,8},{8,0},{1,9},{9,1},{2,10},{10,2},{3,11},{11,3},{4,12},{12,4},... | collective-permute-start | bytes 737288 | tf_op jit(solution)/shard_map/ppermute | solution.py:438
  58.0 0.8 copy-start.7
  62.7 9.5 %collective-permute-start.6 = (bf16[192,128]{1,0:T(8,128)(2,1)}, bf16[192,128]{1,0:T(8,128)(2,1)S(1)}, u32[]{:S(2)}, u32[]{:S(2)}) collective-permute-start(bf16[192,128]{1,0:T(8,128)(2,1)} %get-tuple-element.32), channel_id=1, source_target_pairs={{0,1},{1,0},{2,3},{3,2},{4,5},{5,4},{6,7},{7,6},{8,9},{9,8},{10,11... | collective-permute-start | bytes 147464 | tf_op jit(solution)/shard_map/ppermute | solution.py:441
  62.7 9.5 %collective-permute-start.7 = (bf16[192,128]{1,0:T(8,128)(2,1)}, bf16[192,128]{1,0:T(8,128)(2,1)S(1)}, u32[]{:S(2)}, u32[]{:S(2)}) collective-permute-start(bf16[192,128]{1,0:T(8,128)(2,1)} %get-tuple-element.33), channel_id=1, source_target_pairs={{1,2},{2,1},{3,4},{4,3},{5,6},{6,5},{9,10},{10,9},{11,12},{12,11},... | collective-permute-start | bytes 147464 | tf_op jit(solution)/shard_map/ppermute | solution.py:442
  67.1 0.8 copy-start.6
  72.1 6.6 %copy-start = (bf16[6,320,128]{2,1,0:T(8,128)(2,1)S(1)}, bf16[6,320,128]{2,1,0:T(8,128)(2,1)}, u32[]{:S(2)}) copy-start(bf16[6,320,128]{2,1,0:T(8,128)(2,1)} %shard_map.139) | copy-start | bytes 1474564
  72.1 0.6 copy-start.8
  72.8 0.6 copy-start.9
  79.9 10.1 %collective-permute-start.10 = (bf16[6,320,128]{2,1,0:T(8,128)(2,1)S(1)}, bf16[6,320,128]{2,1,0:T(8,128)(2,1)S(1)}, u32[]{:S(2)}, u32[]{:S(2)}) collective-permute-start(bf16[6,320,128]{2,1,0:T(8,128)(2,1)S(1)} %broadcast_select_fusion), channel_id=1, source_target_pairs={{0,8},{8,0},{1,9},{9,1},{2,10},{10,2},{3,11},{11,3},{4,12},{12,4},... | collective-permute-start | bytes 1474568 | tf_op jit(solution)/shard_map/ppermute | solution.py:438
  79.9 10.0 %copy-start.1 = (bf16[6,320,128]{2,1,0:T(8,128)(2,1)S(1)}, bf16[6,320,128]{2,1,0:T(8,128)(2,1)}, u32[]{:S(2)}) copy-start(bf16[6,320,128]{2,1,0:T(8,128)(2,1)} %get-tuple-element.35) | copy-start | bytes 1474564
  88.0 1.4 %collective-permute-start.8 = (f32[6,256]{1,0:T(8,128)S(1)}, f32[6,256]{1,0:T(8,128)S(1)}, u32[]{:S(2)}, u32[]{:S(2)}) collective-permute-start(f32[6,256]{1,0:T(8,128)S(1)} %get-tuple-element.55), channel_id=1, source_target_pairs={{0,8},{8,0},{1,9},{9,1},{2,10},{10,2},{3,11},{11,3},{4,12},{12,4},... | collective-permute-start | bytes 18440 | tf_op jit(solution)/shard_map/ppermute | solution.py:438

commit v4 on v3

v4 whole, which is shorter than its diff:
```python
import math

import jax
import jax.numpy as jnp
from jax import lax
from jax.experimental import pallas as pl
from jax.experimental.pallas import tpu as pltpu
from jax.sharding import PartitionSpec as P


EPSILON = 1e-06
LAT8 = 8
TILE = 16
F32 = jnp.float32
BF16 = jnp.bfloat16

VMEM = pl.BlockSpec(memory_space=pltpu.VMEM)
SMEM = pl.BlockSpec(memory_space=pltpu.SMEM)
ANY = pl.BlockSpec(memory_space=pl.ANY)


def act(values):
    scale = lax.rsqrt(jnp.mean(values * values, axis=0, keepdims=True) + EPSILON)
    half = values * (0.5 * scale)
    return half + half * jnp.tanh(half)


def dot(left, right):
    return jnp.dot(left, right, preferred_element_type=F32)


def shifted(values, by):
    count = values.shape[1]
    column = lax.broadcasted_iota(jnp.int32, values.shape, 1)
    edge = 0 if by == 1 else count - 1
    return jnp.where(column == edge, 0.0, pltpu.roll(values, by % count, 1))


def call(kernel, outs, in_specs, scratch=(), copies=0, out_specs=None):
    shapes = [pltpu.VMEM(s, d) for s, d in scratch]
    if copies:
        shapes.append(pltpu.SemaphoreType.DMA((copies,)))
    return pl.pallas_call(
        kernel,
        out_shape=[jax.ShapeDtypeStruct(s, d) for s, d in outs],
        in_specs=in_specs,
        out_specs=out_specs or [VMEM] * len(outs),
        scratch_shapes=shapes,
    )


def edges_of():
    place = lax.axis_index("rows")
    return (place == 0, place == lax.axis_size("rows") - 1)


def coefficient(times_ref, step):
    stamp = jnp.full((LAT8, 128), times_ref[step], jnp.int32)
    return (stamp.astype(F32) + 1.0) / 1000.0


def one_hot_sum(values, hot):
    high = values.astype(BF16)
    rest = values - high.astype(F32)
    middle = rest.astype(BF16)
    low = (rest - middle.astype(F32)).astype(BF16)
    return (dot(high, hot) + dot(middle, hot)) + dot(low, hot)


def one_hot(shape, matches):
    rows = lax.broadcasted_iota(jnp.int32, shape, 0)
    lanes = lax.broadcasted_iota(jnp.int32, shape, 1)
    return jnp.where(matches(rows, lanes), 1.0, 0.0).astype(BF16)


def split_latent(values, cols, exact):
    lat = values.shape[1] // cols
    lane = lax.broadcasted_iota(jnp.int32, (LAT8, values.shape[1]), 1)
    chan = lax.broadcasted_iota(jnp.int32, (LAT8, values.shape[1]), 0)
    wide = jnp.concatenate(
        [jnp.where(lane % lat == chan, values[row : row + 1], 0.0) for row in range(values.shape[0])], axis=0
    )
    hot = one_hot((values.shape[1], cols), lambda r, c: r // lat == c)
    split = one_hot_sum(wide, hot) if exact else dot(wide.astype(BF16), hot)
    return [split[row * LAT8 : (row + 1) * LAT8] for row in range(values.shape[0])]


def join_latent(pieces, lat):
    cols = pieces[0].shape[1]
    hot = one_hot((cols, cols * lat), lambda r, c: c // lat == r)
    wide = one_hot_sum(jnp.concatenate(pieces, axis=0), hot)
    lane = lax.broadcasted_iota(jnp.int32, wide.shape, 1)
    chan = lax.broadcasted_iota(jnp.int32, wide.shape, 0) % LAT8
    wide = jnp.where(lane % lat == chan, wide, 0.0)
    return [
        jnp.sum(wide[row * LAT8 : (row + 1) * LAT8], axis=0, keepdims=True) for row in range(len(pieces))
    ]


def whole_columns(first, near, far):
    return jnp.concatenate([jnp.where(first, near, far), jnp.where(first, far, near)], axis=1)


def spread_bias(bias_ref, step):
    bias_ref[...] = jnp.broadcast_to(bias_ref[:, step : step + 1], bias_ref.shape)


def edges_kernel(latent_ref, stale_hbm, one_hbm, two_hbm, state_hbm, latent_out, part_ref, sems):
    segment = lax.axis_index("segment")
    even = lax.axis_index("rows") % 2 == 0
    rows, _, width = latent_ref.shape
    chans, cols = stale_hbm.shape[3:]
    pieces = width // cols
    halo = 3
    index_one = jnp.where(even, rows - 1, 0)
    index_two = jnp.where(even, 0, rows - 1)
    pairs = [(stale_hbm.at[0, 1 - segment], state_hbm)]
    for slot, frame in enumerate((segment, 1 - segment)):
        pairs.append((stale_hbm.at[0, frame, index_one], one_hbm.at[slot, pl.ds(0, chans)]))
        pairs.append((stale_hbm.at[0, frame, index_two], two_hbm.at[slot, pl.ds(0, chans)]))
    copies = fetches(pairs, sems)
    first = segment == 0
    frames = [jnp.where(first, latent_ref[:, k, :], latent_ref[:, 1 - k, :]) for k in range(2)]
    latent_out[...] = frames[1]
    late = []
    for slot in range(2):
        last, top = frames[slot][rows - halo :], frames[slot][:halo]
        for which, piece in enumerate((jnp.where(even, last, top), jnp.where(even, top, last))):
            flat = [piece[:, k * cols : (k + 1) * cols] for k in range(pieces)]
            flat.append(jnp.zeros((TILE - pieces * halo, cols), F32))
            part_ref[which, slot] = jnp.concatenate(flat, axis=0).astype(BF16)
            target = (one_hbm, two_hbm)[which].at[slot, pl.ds(chans, TILE)]
            late.append((part_ref.at[which, slot], target))
    for offset, (src, dst) in enumerate(late):
        copy = pltpu.make_async_copy(src, dst, sems.at[len(pairs) + offset])
        copy.start()
        copies.append(copy)
    for copy in copies:
        copy.wait()


def fetches(pairs, sems):
    copies = [pltpu.make_async_copy(s, d, sems.at[i]) for i, (s, d) in enumerate(pairs)]
    for copy in copies:
        copy.start()
    return copies


def prep_kernel(
    gated_ref, enc_hbm, dec_hbm, down_hbm, time_hbm, enc_out, dec_out, down_out, bias_out,
    enc_ref, dec_ref, down_ref, time_ref, enc_t, dec_t, down_t, bias_t, sems,
):
    pairs = []
    for hbm, ref in ((dec_hbm, dec_ref), (down_hbm, down_ref), (enc_hbm, enc_ref)):
        pairs += [(hbm.at[dy], ref.at[dy]) for dy in range(3)]
    pairs += [(time_hbm, time_ref)]
    copies = fetches(pairs, sems)
    count = len(pairs)
    outs = []

    def send(src, dst):
        copy = pltpu.make_async_copy(src, dst, sems.at[count + len(outs)])
        copy.start()
        outs.append(copy)

    arrived = iter(copies)
    for src, turned, dst in ((dec_ref, dec_t, dec_out), (down_ref, down_t, down_out), (enc_ref, enc_t, enc_out)):
        chans = src.shape[2]
        for dy in range(3):
            next(arrived).wait()
            for dx in range(3):
                lane = (3 * dy + dx) * chans
                turned[:, lane : lane + chans] = src[dy, dx].T
        send(turned, dst)
    next(arrived).wait()
    biases = dot(gated_ref[...], time_ref[...]).T
    bias_t[:, : biases.shape[1]] = biases
    bias_t[:, biases.shape[1] :] = jnp.zeros((bias_t.shape[0], bias_t.shape[1] - biases.shape[1]), F32)
    send(bias_t, bias_out)
    for copy in outs:
        copy.wait()


def turn_kernel(tmid_hbm, out_ref, tmid_ref, sems):
    far = 2 - 2 * lax.axis_index("segment")
    copies = fetches(((tmid_hbm.at[1], tmid_ref.at[0]), (tmid_hbm.at[far], tmid_ref.at[1])), sems)
    for k, copy in enumerate(copies):
        copy.wait()
        out_ref[k] = tmid_ref[k].T


def store_taps(taps_ref, row, value):
    chans, cols = value.shape
    span = slice(row * cols, (row + 1) * cols)
    taps_ref[:chans, span] = shifted(value, 1).astype(BF16)
    taps_ref[chans : 2 * chans, span] = value.astype(BF16)
    taps_ref[2 * chans :, span] = shifted(value, -1).astype(BF16)


def conv_pairs(count, cols, front, back, w_ref, taps_ref, acc_ref, ready):
    front(0)
    front(2)
    ready()
    for pair in range(0, count, 2):
        window = jnp.concatenate(
            [taps_ref[:, (pair + dy) * cols : (pair + dy + 2) * cols] for dy in range(3)], axis=0
        )
        acc_ref[:, pair * cols : (pair + 2) * cols] = dot(w_ref[...], window)
        if pair + 4 <= count:
            front(pair + 4)
        if pair:
            back(pair - 2)
    back(count - 2)


def encode_rows(ext, w_in, w_ref, bias_ref, ready, border, out_ref, lift_ref, taps_ref, acc_ref):
    count, _, cols = out_ref.shape
    is_first, is_last = edges_of()

    def front(row):
        lifted = dot(w_in, jnp.concatenate(ext[row : row + 2], axis=1).astype(BF16))
        lift_ref[:, row * cols : (row + 2) * cols] = lifted
        for k in range(2):
            store_taps(taps_ref, row + k, act(lifted[:, k * cols : (k + 1) * cols]))

    def back(pair):
        for row in (pair, pair + 1):
            here = slice(row * cols, (row + 1) * cols)
            there = slice((row + 1) * cols, (row + 2) * cols)
            total = lift_ref[:, there] + acc_ref[:, here] + bias_ref[...]
            if row < border:
                total = jnp.where(is_first, 0.0, total)
            if row >= count - border:
                total = jnp.where(is_last, 0.0, total)
            out_ref[row] = total.astype(BF16)

    conv_pairs(count, cols, front, back, w_ref, taps_ref, acc_ref, ready)


def turned_w_in(w_small_ref):
    return w_small_ref[9 * LAT8 :, :].astype(F32).T.astype(BF16)


def neighbour(even, one, two, above):
    return jnp.where(even, two, one) if above else jnp.where(even, one, two)


def down_rows(read_row, w_ref, bias_ref, ready, low_ref, q_ref, acat_ref, cols):
    half = cols // 2
    low_rows = low_ref.shape[1] // half
    chans = acat_ref.shape[0] // 9
    source = lax.broadcasted_iota(jnp.int32, (cols, 2 * cols), 0)
    target = lax.broadcasted_iota(jnp.int32, (cols, 2 * cols), 1)
    wanted = 2 * (target % half) + target // cols
    pick = jnp.where(source == wanted, 1.0, 0.0).astype(BF16)
    column = lax.broadcasted_iota(jnp.int32, (chans, cols), 1)
    for row in range(2 * low_rows + 1):
        gate = act(read_row(row).astype(F32)).astype(BF16)
        both = dot(gate, pick)
        even, odd = both[:, :cols], both[:, cols:]
        before = jnp.where(column % half == 0, 0.0, pltpu.roll(odd, 1, 1))
        parts = [part.astype(BF16) for part in (before, even, odd)]
        for dy in range(3):
            if (row - dy) % 2 or not 0 <= (row - dy) // 2 < low_rows:
                continue
            low = (row - dy) // 2
            lane = (low % 2) * half
            for dx, part in enumerate(parts):
                start = (3 * dy + dx) * chans
                acat_ref[start : start + chans, low * half : (low + 1) * half] = part[:, lane : lane + half]
    ready()
    low_ref[...] = dot(w_ref[...], acat_ref[...])
    for low in range(0, low_ref.shape[1], cols):
        wide = min(cols, low_ref.shape[1] - low)
        total = low_ref[:, low : low + wide] + bias_ref[:, :wide]
        low_ref[:, low : low + wide] = total
        q_ref[:, low : low + wide] = act(total).astype(BF16)


def raise_rows(low_ref, q_ref, other_ref, w_tmid_ref, w_up_ref):
    mixed = low_ref[...] + dot(w_tmid_ref[0], q_ref[...]) + dot(w_tmid_ref[1], other_ref[...])
    return dot(w_up_ref[...], mixed.astype(BF16)).astype(BF16)


def doubling(half, rows):
    source = lax.broadcasted_iota(jnp.int32, (rows * half, 2 * rows * half), 0)
    target = lax.broadcasted_iota(jnp.int32, (rows * half, 2 * rows * half), 1)
    return jnp.where(source == target // 2, 1.0, 0.0).astype(BF16)


def mid_first_kernel(
    low_ref, q_ref, other_ref, w_tmid_ref, w_up_ref, base_ref, near_ref, raised_ref, one_ref, two_ref
):
    raised_ref[...] = raise_rows(low_ref, q_ref, other_ref, w_tmid_ref, w_up_ref)
    rows, _, cols = base_ref.shape
    half = cols // 2
    packed = raised_ref.shape[0] // 2
    start = raised_ref.shape[1] - half
    even = lax.axis_index("rows") % 2 == 0

    def bundle(index, lane, edge):
        piece = raised_ref[:, lane : lane + half]
        sent = jnp.concatenate([near_ref[index], base_ref[edge]], axis=0)
        high = sent.astype(BF16)
        low = (sent - high.astype(F32)).astype(BF16)
        folded = jnp.concatenate([piece[:packed], piece[packed:]], axis=1)
        return jnp.concatenate([folded, high, low], axis=0)

    up = bundle(0, 0, 0)
    down = bundle(1, start, rows - 1)
    one_ref[...] = jnp.where(even, down, up)
    two_ref[...] = jnp.where(even, up, down)


def decode_rows(count, cols, read_joined, w_ref, w_skip_ref, bias_ref, ready, border, w_small_ref, mixed_ref, taps_ref, acc_ref):
    is_first, is_last = edges_of()
    span = 3 * LAT8
    parts = []

    def front(row):
        mixed = dot(w_skip_ref[...], jnp.concatenate([read_joined(row), read_joined(row + 1)], axis=1))
        mixed_ref[:, row * cols : (row + 2) * cols] = mixed
        for k in range(2):
            store_taps(taps_ref, row + k, act(mixed[:, k * cols : (k + 1) * cols]))

    def back(pair):
        outs = []
        for row in (pair, pair + 1):
            here = slice(row * cols, (row + 1) * cols)
            there = slice((row + 1) * cols, (row + 2) * cols)
            value = act(mixed_ref[:, there] + acc_ref[:, here] + bias_ref[...])
            if row < border:
                value = jnp.where(is_first, 0.0, value)
            if row >= count - border:
                value = jnp.where(is_last, 0.0, value)
            outs.append(value.astype(BF16))
        taps = dot(w_small_ref[: 9 * LAT8, :], jnp.concatenate(outs, axis=1))
        for k in range(2):
            tap = taps[:, k * cols : (k + 1) * cols]
            parts.append(shifted(tap[:span], 1) + tap[span : 2 * span] + shifted(tap[2 * span :], -1))

    conv_pairs(count, cols, front, back, w_ref, taps_ref, acc_ref, ready)
    return parts


def tap_sum(parts, row):
    total = None
    for dy in range(3):
        source = row + dy - 1
        if 0 <= source < len(parts):
            piece = parts[source][dy * LAT8 : (dy + 1) * LAT8]
            total = piece if total is None else total + piece
    return total


def waiter(copies, bias_ref, step):
    def ready():
        for copy in copies:
            copy.wait()
        spread_bias(bias_ref, step)

    return ready


def first_kernel(
    times_ref, latent_ref, x_got_ref, got_ref, one_ref, two_ref, far_ref, w_skip_ref, w_small_ref,
    stale_hbm, w_dec_hbm, w_down_hbm, bias_hbm,
    base_ref, near_ref, low_ref, q_ref,
    own_ref, enc_ref, mid_ref, w_dec_ref, w_down_ref, b_dec_ref, b_mid_ref, mixed_ref, taps_ref, acc_ref, acat_ref, sems,
):
    rows, chans, cols = got_ref.shape
    mid = low_ref.shape[0]
    total = bias_hbm.shape[0]
    segment = lax.axis_index("segment")
    first = segment == 0
    even = lax.axis_index("rows") % 2 == 0
    copies = fetches(
        (
            (stale_hbm.at[0, segment], own_ref),
            (w_dec_hbm, w_dec_ref),
            (bias_hbm.at[total - chans :], b_dec_ref),
            (w_down_hbm, w_down_ref),
            (bias_hbm.at[chans : chans + mid], b_mid_ref),
        ),
        sems,
    )
    copies[0].wait()
    for row in range(rows + 2):
        if 1 <= row <= rows:
            own, got = own_ref[row - 1], got_ref[row - 1]
        else:
            own = neighbour(even, one_ref[0, :chans], two_ref[0, :chans], row == 0)
            got = neighbour(even, far_ref[0, :chans], far_ref[1, :chans], row == 0)
        enc_ref[row] = jnp.where(first, own, got)
        mid_ref[row] = jnp.where(first, got, own)
    parts = decode_rows(
        rows, cols, lambda row: jnp.concatenate([mid_ref[row], enc_ref[row]], axis=0),
        w_dec_ref, w_skip_ref, b_dec_ref, waiter(copies[1:3], b_dec_ref, 0), 0, w_small_ref,
        mixed_ref, taps_ref, acc_ref,
    )
    mine = jnp.where(first, latent_ref[:, 0, :], latent_ref[:, 1, :])
    x_rows = split_latent(whole_columns(first, mine, x_got_ref[...]), cols, True)
    coef = coefficient(times_ref, 0)
    near_ref[0] = coef * tap_sum(parts, -1)
    near_ref[1] = coef * tap_sum(parts, rows)
    for row in range(rows):
        base_ref[row] = x_rows[row] - coef * tap_sum(parts, row)
    down_rows(
        lambda row: enc_ref[row], w_down_ref, b_mid_ref, waiter(copies[3:], b_mid_ref, 0),
        low_ref, q_ref, acat_ref, cols,
    )


def second_kernel(
    latent_ref, x_got_ref, one_ref, two_ref, far_ref, w_small_ref, w_enc_hbm, w_down_hbm, bias_hbm,
    enc_ref, low_ref, q_ref,
    w_enc_ref, w_down_ref, b_enc_ref, b_mid_ref, lift_ref, taps_ref, acc_ref, acat_ref, sems,
):
    _, chans, cols = enc_ref.shape
    mid = low_ref.shape[0]
    first = lax.axis_index("segment") == 0
    even = lax.axis_index("rows") % 2 == 0
    copies = fetches(
        (
            (w_enc_hbm, w_enc_ref),
            (bias_hbm.at[:chans], b_enc_ref),
            (w_down_hbm, w_down_ref),
            (bias_hbm.at[chans : chans + mid], b_mid_ref),
        ),
        sems,
    )
    halo = 3
    pieces = latent_ref.shape[2] // cols

    def received(block):
        block = block[chans:].astype(F32)
        return jnp.concatenate([block[k * halo : (k + 1) * halo] for k in range(pieces)], axis=1)

    def halo_rows(above):
        near = neighbour(even, received(one_ref[0]), received(two_ref[0]), above)
        far = neighbour(even, received(far_ref[0]), received(far_ref[1]), above)
        return whole_columns(first, near, far)

    mine = jnp.where(first, latent_ref[:, 0, :], latent_ref[:, 1, :])
    values = jnp.concatenate(
        [halo_rows(True), whole_columns(first, mine, x_got_ref[...]), halo_rows(False)], axis=0
    )
    encode_rows(
        split_latent(values, cols, False), turned_w_in(w_small_ref), w_enc_ref, b_enc_ref,
        waiter(copies[:2], b_enc_ref, 0), 2, enc_ref, lift_ref, taps_ref, acc_ref,
    )
    down_rows(
        lambda row: enc_ref[row + 1], w_down_ref, b_mid_ref, waiter(copies[2:], b_mid_ref, 1),
        low_ref, q_ref, acat_ref, cols,
    )


def third_kernel(
    low_ref, q_ref, other_ref, base_ref, near_ref, one_ref, two_ref, w_small_ref, w_up_ref,
    w_enc_hbm, w_tmid_hbm, bias_hbm,
    send_ref, keep_ref, x_ref,
    enc_ref, w_enc_ref, w_tmid_ref, b_enc_ref, lift_ref, taps_ref, acc_ref, sems,
):
    rows, chans, cols = enc_ref.shape
    first = lax.axis_index("segment") == 0
    even = lax.axis_index("rows") % 2 == 0
    is_first, is_last = edges_of()
    copies = fetches(
        ((w_enc_hbm, w_enc_ref), (bias_hbm.at[:chans], b_enc_ref), (w_tmid_hbm, w_tmid_ref)), sems
    )
    packed = one_ref.shape[0] - 2 * TILE

    def received(above):
        high = neighbour(even, one_ref[packed : packed + TILE, :], two_ref[packed : packed + TILE, :], above)
        low = neighbour(even, one_ref[packed + TILE :, :], two_ref[packed + TILE :, :], above)
        both = high.astype(F32) + low.astype(F32)
        return both[:LAT8], both[LAT8:]

    from_up, base_up = received(True)
    from_down, base_down = received(False)
    ext = [base_ref[row] for row in range(rows)]
    ext[0] = ext[0] - from_up
    ext[-1] = ext[-1] - from_down
    for row in range(rows):
        x_ref[row] = ext[row]
    ext = (
        [jnp.where(is_first, 0.0, base_up - near_ref[0])]
        + ext
        + [jnp.where(is_last, 0.0, base_down - near_ref[1])]
    )
    encode_rows(
        ext, turned_w_in(w_small_ref), w_enc_ref, b_enc_ref, waiter(copies[:2], b_enc_ref, 1), 0,
        enc_ref, lift_ref, taps_ref, acc_ref,
    )
    copies[2].wait()
    raised = raise_rows(low_ref, q_ref, other_ref, w_tmid_ref, w_up_ref)
    wide = dot(raised, doubling(cols // 2, rows // 2)).astype(BF16)
    for row in range(rows):
        low = row // 2
        mid = wide[:, low * cols : (low + 1) * cols]
        enc = enc_ref[row]
        send_ref[row] = jnp.where(first, mid, enc)
        keep_ref[row] = jnp.where(first, enc, mid)


def last_kernel(
    times_ref, enc_ref, mid_ref, one_ref, two_ref, x_ref, w_skip_ref, w_small_ref, w_hbm, bias_hbm,
    send_ref, keep_ref, wide_ref, w_ref, bias_ref, mixed_ref, taps_ref, acc_ref, sems,
):
    rows = x_ref.shape[0]
    chans, cols = enc_ref.shape[1:]
    total = bias_hbm.shape[0]
    copies = fetches(((w_hbm, w_ref), (bias_hbm.at[total - chans :], bias_ref)), sems)
    half = cols // 2
    inner = rows // 2
    first = lax.axis_index("segment") == 0
    even = lax.axis_index("rows") % 2 == 0
    packed = chans // 2
    wide_ref[:, cols : (inner + 1) * cols] = dot(mid_ref[...], doubling(half, inner)).astype(BF16)
    twice = doubling(half, 1)
    for low in (0, inner + 1):
        folded = neighbour(even, one_ref[:packed, :], two_ref[:packed, :], low == 0)
        piece = jnp.concatenate([folded[:, :half], folded[:, half:]], axis=0)
        wide_ref[:, low * cols : (low + 1) * cols] = dot(piece, twice).astype(BF16)

    def joined(row):
        low = row // 2
        return jnp.concatenate([wide_ref[:, low * cols : (low + 1) * cols], enc_ref[row]], axis=0)

    parts = decode_rows(
        rows + 2, cols, joined, w_ref, w_skip_ref, bias_ref, waiter(copies, bias_ref, 1), 1, w_small_ref,
        mixed_ref, taps_ref, acc_ref,
    )
    coef = coefficient(times_ref, 1)
    width = send_ref.shape[1]
    pieces = [x_ref[row] - coef * tap_sum(parts, row + 1) for row in range(rows)]
    for row, flat in enumerate(join_latent(pieces, 2 * width // cols)):
        near, far = flat[:, :width], flat[:, width:]
        keep_ref[row : row + 1, :] = jnp.where(first, near, far)
        send_ref[row : row + 1, :] = jnp.where(first, far, near)


def gated_times(timesteps, half):
    freqs = jnp.exp(-math.log(10000.0) * jnp.arange(half).astype(F32) / half)
    angles = timesteps.astype(F32)[:, None] * freqs[None, :]
    embedded = jnp.concatenate([jnp.sin(angles), jnp.cos(angles)], axis=1)
    gated = jax.nn.silu(embedded).astype(BF16)
    return jnp.pad(gated, ((0, TILE - gated.shape[0]), (0, 0)))


def step_pair(latent, stale, timesteps, w_in, w_enc, w_down, w_tmid, w_up, w_skip, w_dec, w_out, w_time):
    first = lax.axis_index("segment") == 0
    size = lax.axis_size("rows")
    chan_major = stale.transpose(0, 1, 2, 4, 3)
    _, frames, rows, chans, cols = chan_major.shape
    row_major = latent.transpose(1, 0, 2)
    mid = w_down.shape[3]
    lat = w_in.shape[0]
    width = latent.shape[2]
    half = cols // 2
    low = (rows // 2) * half
    wide = 3 * chans
    total = w_time.shape[1]
    assert frames == 2 and lax.axis_size("segment") == 2 and 2 * width == cols * lat

    def paired(start):
        return [p for i in range(start, size - 1, 2) for p in ((i, i + 1), (i + 1, i))]

    def swap(value):
        return lax.ppermute(value, "segment", [(0, 1), (1, 0)])

    def exchange(one, two):
        got_one = lax.ppermute(one, "rows", paired(0))
        got_two = lax.ppermute(two, "rows", paired(1))
        return got_one, got_two

    payload = ((2, chans + TILE, cols), BF16)
    to_one, to_two, to_state, to_latent = call(
        edges_kernel,
        [payload, payload, ((rows, chans, cols), BF16), ((rows, width), F32)],
        [VMEM, ANY],
        [((2, 2, TILE, cols), BF16)],
        9,
        [ANY] * 3 + [VMEM],
    )(row_major, chan_major)
    one, two = exchange(to_one, to_two)
    got = swap(to_state)
    x_got = swap(to_latent)
    far = swap(jnp.stack([one[1], two[1]]))

    taps = jnp.pad(w_out.transpose(1, 0, 3, 2), ((0, 0), (0, 0), (0, LAT8 - lat), (0, 0)))
    w_small = jnp.concatenate(
        [taps.reshape(9 * LAT8, chans), jnp.pad(w_in, ((0, LAT8 - lat), (0, 0)))], axis=0
    )
    w_up_t = w_up.T
    w_skip_t = w_skip.T

    turned = [
        ((chans, 3 * wide), BF16),
        ((chans, 3 * wide), BF16),
        ((mid, 3 * wide), BF16),
        ((total, cols), F32),
    ]
    weights = (w_enc, w_dec, w_down, w_time)
    gated = gated_times(timesteps, w_time.shape[0] // 2)
    w_enc_t, w_dec_t, w_down_t, bias = call(
        prep_kernel, turned, [VMEM] + [ANY] * 4, [(w.shape, BF16) for w in weights] + turned, 14, [ANY] * 4
    )(gated, *weights)

    def conv_scratch(count):
        return [
            ((chans, (count + 2) * cols), F32),
            ((wide, (count + 2) * cols), BF16),
            ((chans, count * cols), F32),
        ]

    w_conv = ((chans, 3 * wide), BF16)
    w_wide = ((mid, 3 * wide), BF16)
    b_conv = ((chans, cols), F32)
    b_wide = ((mid, cols), F32)
    acat = ((3 * wide, low), BF16)
    down_outs = [((mid, low), F32), ((mid, low), BF16)]
    ext = ((rows + 2, chans, cols), BF16)

    base, near, low0, q0 = call(
        first_kernel,
        [((rows, LAT8, cols), F32), ((2, LAT8, cols), F32)] + down_outs,
        [SMEM] + [VMEM] * 8 + [ANY] * 4,
        [((rows, chans, cols), BF16), ext, ext, w_conv, w_wide, b_conv, b_wide] + conv_scratch(rows) + [acat],
        5,
    )(timesteps, row_major, x_got, got, one, two, far, w_skip_t, w_small, chan_major, w_dec_t, w_down_t, bias)
    q0_other = swap(q0)

    (w_tmid_t,) = call(turn_kernel, [((2, mid, mid), BF16)], [ANY], [((2, mid, mid), BF16)], 2)(w_tmid)

    bundle = ((chans // 2 + 2 * TILE, cols), BF16)
    mid1, to_one, to_two = call(
        mid_first_kernel, [((chans, low), BF16), bundle, bundle], [VMEM] * 7
    )(low0, q0, q0_other, w_tmid_t, w_up_t, base, near)
    got_one, got_two = exchange(to_one, to_two)

    enc1, low1, q1 = call(
        second_kernel,
        [((rows + 4, chans, cols), BF16)] + down_outs,
        [VMEM] * 6 + [ANY] * 3,
        [w_conv, w_wide, b_conv, b_wide] + conv_scratch(rows + 4) + [acat],
        4,
    )(row_major, x_got, one, two, far, w_small, w_enc_t, w_down_t, bias)
    q1_other = swap(q1)

    feat_send, feat_keep, x1 = call(
        third_kernel,
        [((rows, chans, cols), BF16)] * 2 + [((rows, LAT8, cols), F32)],
        [VMEM] * 9 + [ANY] * 3,
        [((rows, chans, cols), BF16), w_conv, ((2, mid, mid), BF16), b_conv] + conv_scratch(rows),
        3,
    )(low1, q1, q1_other, base, near, got_one, got_two, w_small, w_up_t, w_enc_t, w_tmid_t, bias)
    feat_got = swap(feat_send)

    x_send, x_keep = call(
        last_kernel,
        [((rows, width), F32)] * 2,
        [SMEM] + [VMEM] * 7 + [ANY] * 2,
        [((chans, (rows // 2 + 2) * cols), BF16), w_conv, b_conv] + conv_scratch(rows + 2),
        2,
    )(timesteps, enc1, mid1, got_one, got_two, x1, w_skip_t, w_small, w_dec_t, bias)
    x_far = swap(x_send)

    features = jnp.where(first, jnp.stack([feat_keep, feat_got]), jnp.stack([feat_got, feat_keep]))
    result = jnp.where(first, jnp.stack([x_keep, x_far]), jnp.stack([x_far, x_keep]))
    return (result, features.transpose(0, 1, 3, 2)[None])


def solution(mesh):
    placed = (
        P("clips", "rows", "segment"),
        P("segment", "clips", "rows", None, None),
        P("clips"),
    ) + (P(),) * 9
    return jax.shard_map(
        step_pair,
        mesh=mesh,
        in_specs=placed,
        out_specs=(P("clips", "rows", "segment"), P("segment", "clips", "rows", None, None)),
        check_vma=False,
    )
```

time: 91.9 us -> 106 us (1.15)
  the two profiles are of different devices: /device:TPU:7 before, /device:TPU:11 now
where the time goes in v4:
time: 106 us
  Pallas kernels  75.7 us (71%)
  starting transfers between devices  11 us (10%)
  waiting for transfers between devices  9.62 us (9%)
  local copies, waits for them, and re-layouts  4.23 us (4%)
  other arithmetic  4.07 us (4%)
    pallas_call x1, Pallas kernels, step_pair(): call(edges_kernel, [payload, payload, ((rows, chans, cols), BF16), ((rows...  27.3 us
    pallas_call x1, Pallas kernels, step_pair(): call(first_kernel, [((rows, LAT8, cols), F32), ((2, LAT8, cols), F32)] +...  9.64 us
    pallas_call x1, Pallas kernels, step_pair(): call(second_kernel, [((rows + 4, chans, cols), BF16)] + down_outs, [VMEM]...  9.13 us
    pallas_call x1, Pallas kernels, step_pair(): call(prep_kernel, turned, [VMEM] + [ANY] * 4, [(w.shape, BF16) for w in w...  8.03 us
    pallas_call x1, Pallas kernels, step_pair(): call(third_kernel, [((rows, chans, cols), BF16)] * 2 + [((rows, LAT8, col...  8.02 us
    ppermute x2, waiting for transfers between devices, exchange(): got_two = lax.ppermute(two, 'rows', paired(1))  7.57 us
    pallas_call x1, Pallas kernels, step_pair(): call(last_kernel, [((rows, width), F32)] * 2, [SMEM] + [VMEM] * 7 + [ANY]...  6.99 us
    ppermute x7, starting transfers between devices, swap(): return lax.ppermute(value, 'segment', [(0, 1), (1, 0)])  5 us
  transfers between devices with their start and end apart: 11, of which 4 were waited for; matrix products, arithmetic and copies ran while one was open for 5% of the time, Pallas kernels for 29%

profile of v4, /device:TPU:11, one launch (start us, length us, event | category | flops | bytes accessed | tf_op | source)
XLA Modules:
  0.0 105.5 jit_solution(14950362112645137325)
XLA Ops:
  0.6 27.3 %shard_map.131 = (bf16[2,336,128]{2,1,0:T(8,128)(2,1)}, bf16[2,336,128]{2,1,0:T(8,128)(2,1)}, bf16[6,320,128]{2,1,0:T(8,128)(2,1)}, f32[6,256]{1,0:T(8,128)}) custom-call(f32[6,2,256]{2,1,0:T(2,128)} %bitcast.23, bf16[1,2,6,320,128]{4,3,2,1,0:T(8,128)(2,1)} %bitcast.14), custom_call_target="tpu_custom_call" | custom-call | tf_op jit(solution)/shard_map/pallas_call | solution.py:578
  27.9 0.7 collective-permute-start
  28.7 1.2 %collective-permute-start.1 = (bf16[2,336,128]{2,1,0:T(8,128)(2,1)}, bf16[2,336,128]{2,1,0:T(8,128)(2,1)S(1)}, u32[]{:S(2)}, u32[]{:S(2)}) collective-permute-start(bf16[2,336,128]{2,1,0:T(8,128)(2,1)} %get-tuple-element.26), channel_id=1, source_target_pairs={{0,1},{1,0},{2,3},{3,2},{4,5},{5,4},{6,7},{7,6},{8,9},{9,8},{10,11... | collective-permute-start | bytes 516104 | tf_op jit(solution)/shard_map/ppermute | solution.py:573
  29.9 2.0 %collective-permute-start.2 = (bf16[2,336,128]{2,1,0:T(8,128)(2,1)}, bf16[2,336,128]{2,1,0:T(8,128)(2,1)S(1)}, u32[]{:S(2)}, u32[]{:S(2)}) collective-permute-start(bf16[2,336,128]{2,1,0:T(8,128)(2,1)} %get-tuple-element.27), channel_id=1, source_target_pairs={{1,2},{2,1},{3,4},{4,3},{5,6},{6,5},{9,10},{10,9},{11,12},{12,11},... | collective-permute-start | bytes 516104 | tf_op jit(solution)/shard_map/ppermute | solution.py:574
  31.9 0.7 collective-permute-start.4
  32.7 0.8 copy.16
  33.4 0.7 convert_element_type.19
  34.1 0.1 multiply_sine_fusion
  34.2 4.3 %collective-permute-done.2.two_ref = bf16[2,336,128]{2,1,0:T(8,128)(2,1)S(1)} collective-permute-done((bf16[2,336,128]{2,1,0:T(8,128)(2,1)}, bf16[2,336,128]{2,1,0:T(8,128)(2,1)S(1)}, u32[]{:S(2)}, u32[]{:S(2)}) %collective-permute-start.2) | collective-permute-done | bytes 172064 | tf_op jit(solution)/shard_map/ppermute | solution.py:574
  38.5 0.0 collective-permute-done.1.one_ref
  38.5 0.0 copy-start
  38.6 1.3 %collective-permute-start.3 = (bf16[2,336,128]{2,1,0:T(8,128)(2,1)S(1)}, bf16[2,336,128]{2,1,0:T(8,128)(2,1)S(1)}, u32[]{:S(2)}, u32[]{:S(2)}) collective-permute-start(bf16[2,336,128]{2,1,0:T(8,128)(2,1)S(1)} %pad_maximum_fusion), channel_id=1, source_target_pairs={{0,8},{8,0},{1,9},{9,1},{2,10},{10,2},{3,11},{11,3},{4,12},{12,4},... | collective-permute-start | bytes 516104 | tf_op jit(solution)/shard_map/ppermute | solution.py:570
  39.8 1.3 %fusion.2.w_small_ref = bf16[80,320]{1,0:T(8,128)(2,1)} fusion(bf16[4,320]{1,0:T(4,128)(2,1)} %param.15, bf16[72,320]{1,0:T(8,128)(2,1)S(1)} %bitcast.22), kind=kLoop, calls=%fused_computation.5 | loop fusion | flops 153600 | bytes 99840 | tf_op jit(solution)/shard_map/concatenate | solution.py:592
  41.2 0.1 fusion.3
  41.2 0.6 pad.14.gated_ref
  41.9 8.0 %shard_map.132 = (bf16[320,2880]{1,0:T(8,128)(2,1)}, bf16[320,2880]{1,0:T(8,128)(2,1)}, bf16[640,2880]{1,0:T(8,128)(2,1)}, f32[1280,128]{1,0:T(8,128)}) custom-call(bf16[16,320]{1,0:T(8,128)(2,1)} %pad.14.gated_ref, bf16[3,3,320,320]{3,2,1,0:T(8,128)(2,1)} %enc_hbm.1, bf16[3,3,320,320]{3,2,1,0:T(8,128)(2,1)} %dec_hbm.1, bf16[3,3,320,640]{3,2,1,0:T(8,128)(2,1)} %down_hbm.1, ...), custom_call_target="tpu_custom_call" | custom-call | tf_op jit(solution)/shard_map/pallas_call | solution.py:606
  49.9 0.0 collective-permute-done.x_got_ref
  49.9 0.0 copy-start.9
  50.0 0.0 collective-permute-done.3.far_ref
  50.0 0.0 collective-permute-done.4.got_ref
  50.0 0.0 copy-start.3
  50.0 0.5 copy-done.9
  50.5 0.1 copy-done.2
  50.6 0.2 copy-done.3
  50.8 9.6 %shard_map.134 = (f32[6,8,128]{2,1,0:T(8,128)}, f32[2,8,128]{2,1,0:T(8,128)}, f32[640,192]{1,0:T(8,128)}, bf16[640,192]{1,0:T(8,128)(2,1)}) custom-call(s32[2]{0:T(128)} %times_ref.3, f32[6,2,256]{2,1,0:T(2,128)} %bitcast.24, f32[6,256]{1,0:T(8,128)} %copy-done.9, bf16[6,320,128]{2,1,0:T(8,128)(2,1)} %copy-done.3, bf16[2,336,128]{2,1,0:T(8,128)(2,1)} %copy-done, ...), custom_call_target="tpu_custom_call" | custom-call | tf_op jit(solution)/shard_map/pallas_call | solution.py:625
  60.4 0.1 collective-permute-start.5
  60.5 9.1 %shard_map.133 = (bf16[10,320,128]{2,1,0:T(8,128)(2,1)}, f32[640,192]{1,0:T(8,128)}, bf16[640,192]{1,0:T(8,128)(2,1)}) custom-call(f32[6,2,256]{2,1,0:T(2,128)} %bitcast.25, f32[6,256]{1,0:T(8,128)} %copy-done.9, bf16[2,336,128]{2,1,0:T(8,128)(2,1)} %copy-done, bf16[2,336,128]{2,1,0:T(8,128)(2,1)} %copy-done.1, bf16[2,336,128]{2,1,0:T(8,128)(2,1)} %copy-done.2, ...), custom_call_target="tpu_custom_call" | custom-call | tf_op jit(solution)/shard_map/pallas_call | solution.py:642
  69.7 0.6 collective-permute-start.8
  70.2 2.9 %shard_map.135.w_tmid_ref.w_tmid_hbm = bf16[2,640,640]{2,1,0:T(8,128)(2,1)} custom-call(bf16[3,640,640]{2,1,0:T(8,128)(2,1)} %tmid_hbm.1), custom_call_target="tpu_custom_call" | custom-call | tf_op jit(solution)/shard_map/pallas_call | solution.py:634
  73.2 0.0 collective-permute-done.5.other_ref
  73.2 0.7 copy-done.5
  73.9 3.7 %shard_map.136 = (bf16[320,192]{1,0:T(8,128)(2,1)}, bf16[192,128]{1,0:T(8,128)(2,1)}, bf16[192,128]{1,0:T(8,128)(2,1)}) custom-call(f32[640,192]{1,0:T(8,128)} %get-tuple-element.34.low_ref, bf16[640,192]{1,0:T(8,128)(2,1)} %get-tuple-element.35.q_ref, bf16[640,192]{1,0:T(8,128)(2,1)} %copy-done.5, bf16[2,640,640]{2,1,0:T(8,128)(2,1)} %shard_map.135.w_tmid_ref.w_tmid_hbm, ...), custom_call_target="tpu_custom_call" | custom-call | tf_op jit(solution)/shard_map/pallas_call | solution.py:637
  77.6 0.9 collective-permute-start.6
  78.5 1.9 %collective-permute-start.7 = (bf16[192,128]{1,0:T(8,128)(2,1)}, bf16[192,128]{1,0:T(8,128)(2,1)S(1)}, u32[]{:S(2)}, u32[]{:S(2)}) collective-permute-start(bf16[192,128]{1,0:T(8,128)(2,1)} %get-tuple-element.40), channel_id=1, source_target_pairs={{1,2},{2,1},{3,4},{4,3},{5,6},{6,5},{9,10},{10,9},{11,12},{12,11},... | collective-permute-start | bytes 147464 | tf_op jit(solution)/shard_map/ppermute | solution.py:574
  80.4 0.0 collective-permute-done.8.other_ref
  80.4 0.7 collective-permute-done.6.one_ref
  81.1 3.3 %collective-permute-done.7.two_ref = bf16[192,128]{1,0:T(8,128)(2,1)S(1)} collective-permute-done((bf16[192,128]{1,0:T(8,128)(2,1)}, bf16[192,128]{1,0:T(8,128)(2,1)S(1)}, u32[]{:S(2)}, u32[]{:S(2)}) %collective-permute-start.7) | collective-permute-done | bytes 49184 | tf_op jit(solution)/shard_map/ppermute | solution.py:574
  84.4 0.0 copy-done.6
  84.4 0.6 copy-done.8
  85.0 8.0 %shard_map.137 = (bf16[6,320,128]{2,1,0:T(8,128)(2,1)}, bf16[6,320,128]{2,1,0:T(8,128)(2,1)}, f32[6,8,128]{2,1,0:T(8,128)}) custom-call(f32[640,192]{1,0:T(8,128)} %get-tuple-element.41.low_ref, bf16[640,192]{1,0:T(8,128)(2,1)} %get-tuple-element.42.q_ref, bf16[640,192]{1,0:T(8,128)(2,1)} %copy-done.6, f32[6,8,128]{2,1,0:T(8,128)} %get-tuple-element.36.base_ref, ...), custom_call_target="tpu_custom_call" | custom-call | tf_op jit(solution)/shard_map/pallas_call | solution.py:651
  93.1 1.5 %collective-permute-start.10 = (bf16[6,320,128]{2,1,0:T(8,128)(2,1)}, bf16[6,320,128]{2,1,0:T(8,128)(2,1)S(1)}, u32[]{:S(2)}, u32[]{:S(2)}) collective-permute-start(bf16[6,320,128]{2,1,0:T(8,128)(2,1)} %get-tuple-element.47), channel_id=1, source_target_pairs={{0,8},{8,0},{1,9},{9,1},{2,10},{10,2},{3,11},{11,3},{4,12},{12,4},... | collective-permute-start | bytes 1474568 | tf_op jit(solution)/shard_map/ppermute | solution.py:570
  94.6 7.0 %shard_map.138 = (f32[6,256]{1,0:T(8,128)}, f32[6,256]{1,0:T(8,128)}) custom-call(s32[2]{0:T(128)} %times_ref.3, bf16[10,320,128]{2,1,0:T(8,128)(2,1)} %get-tuple-element.31.enc_ref, bf16[320,192]{1,0:T(8,128)(2,1)} %get-tuple-element.38.mid_ref, bf16[192,128]{1,0:T(8,128)(2,1)} %copy-done.7, bf16[192,128]{1,0:T(8,128)(2,1)} %copy-done.8, ...), custom_call_target="tpu_custom_call" | custom-call | tf_op jit(solution)/shard_map/pallas_call | solution.py:660
  101.6 0.1 collective-permute-start.9
  101.7 1.3 %collective-permute-done.9 = f32[6,256]{1,0:T(8,128)S(1)} collective-permute-done((f32[6,256]{1,0:T(8,128)}, f32[6,256]{1,0:T(8,128)S(1)}, u32[]{:S(2)}, u32[]{:S(2)}) %collective-permute-start.9) | collective-permute-done | bytes 6176 | tf_op jit(solution)/shard_map/ppermute | solution.py:570
  103.1 0.8 maximum_select_fusion.1
  103.8 0.6 copy.15
  104.4 0.0 collective-permute-done.10
  104.4 1.1 %fusion = bf16[1,2,6,128,320]{3,4,2,1,0:T(8,128)(2,1)} fusion(bf16[1,6,320,128]{3,2,1,0:T(8,128)(2,1)S(1)} %bitcast.21, bf16[1,6,320,128]{3,2,1,0:T(8,128)(2,1)S(1)} %bitcast.20, pred[]{:T(512)S(6)} %eq.3), kind=kLoop, calls=%fused_computation.1 | loop fusion | flops 1474560 | bytes 1966081 | tf_op jit(solution)/shard_map/broadcast_in_dim | solution.py:671
  (16 shorter events, 0.1 us)
Async XLA Ops:
  27.9 22.0 %collective-permute-start = (f32[6,256]{1,0:T(8,128)}, f32[6,256]{1,0:T(8,128)S(1)}, u32[]{:S(2)}, u32[]{:S(2)}) collective-permute-start(f32[6,256]{1,0:T(8,128)} %get-tuple-element.25), channel_id=1, source_target_pairs={{0,8},{8,0},{1,9},{9,1},{2,10},{10,2},{3,11},{11,3},{4,12},{12,4},... | collective-permute-start | bytes 18440 | tf_op jit(solution)/shard_map/ppermute | solution.py:570
  28.7 9.8 %collective-permute-start.1 = (bf16[2,336,128]{2,1,0:T(8,128)(2,1)}, bf16[2,336,128]{2,1,0:T(8,128)(2,1)S(1)}, u32[]{:S(2)}, u32[]{:S(2)}) collective-permute-start(bf16[2,336,128]{2,1,0:T(8,128)(2,1)} %get-tuple-element.26), channel_id=1, source_target_pairs={{0,1},{1,0},{2,3},{3,2},{4,5},{5,4},{6,7},{7,6},{8,9},{9,8},{10,11... | collective-permute-start | bytes 516104 | tf_op jit(solution)/shard_map/ppermute | solution.py:573
  29.9 8.6 %collective-permute-start.2 = (bf16[2,336,128]{2,1,0:T(8,128)(2,1)}, bf16[2,336,128]{2,1,0:T(8,128)(2,1)S(1)}, u32[]{:S(2)}, u32[]{:S(2)}) collective-permute-start(bf16[2,336,128]{2,1,0:T(8,128)(2,1)} %get-tuple-element.27), channel_id=1, source_target_pairs={{1,2},{2,1},{3,4},{4,3},{5,6},{6,5},{9,10},{10,9},{11,12},{12,11},... | collective-permute-start | bytes 516104 | tf_op jit(solution)/shard_map/ppermute | solution.py:574
  31.9 18.0 %collective-permute-start.4 = (bf16[6,320,128]{2,1,0:T(8,128)(2,1)}, bf16[6,320,128]{2,1,0:T(8,128)(2,1)S(1)}, u32[]{:S(2)}, u32[]{:S(2)}) collective-permute-start(bf16[6,320,128]{2,1,0:T(8,128)(2,1)} %get-tuple-element.32), channel_id=1, source_target_pairs={{0,8},{8,0},{1,9},{9,1},{2,10},{10,2},{3,11},{11,3},{4,12},{12,4},... | collective-permute-start | bytes 1474568 | tf_op jit(solution)/shard_map/ppermute | solution.py:570
  38.5 11.4 %copy-start.1 = (bf16[2,336,128]{2,1,0:T(8,128)(2,1)}, bf16[2,336,128]{2,1,0:T(8,128)(2,1)S(1)}, u32[]{:S(2)}) copy-start(bf16[2,336,128]{2,1,0:T(8,128)(2,1)S(1)} %collective-permute-done.2.two_ref) | copy-start | bytes 516100
  38.5 11.4 %copy-start = (bf16[2,336,128]{2,1,0:T(8,128)(2,1)}, bf16[2,336,128]{2,1,0:T(8,128)(2,1)S(1)}, u32[]{:S(2)}) copy-start(bf16[2,336,128]{2,1,0:T(8,128)(2,1)S(1)} %collective-permute-done.1.one_ref) | copy-start | bytes 516100
  38.6 11.4 %collective-permute-start.3 = (bf16[2,336,128]{2,1,0:T(8,128)(2,1)S(1)}, bf16[2,336,128]{2,1,0:T(8,128)(2,1)S(1)}, u32[]{:S(2)}, u32[]{:S(2)}) collective-permute-start(bf16[2,336,128]{2,1,0:T(8,128)(2,1)S(1)} %pad_maximum_fusion), channel_id=1, source_target_pairs={{0,8},{8,0},{1,9},{9,1},{2,10},{10,2},{3,11},{11,3},{4,12},{12,4},... | collective-permute-start | bytes 516104 | tf_op jit(solution)/shard_map/ppermute | solution.py:570
  49.9 0.6 copy-start.9
  50.0 0.7 copy-start.2
  50.0 0.8 copy-start.3
  60.4 12.7 %collective-permute-start.5 = (bf16[640,192]{1,0:T(8,128)(2,1)}, bf16[640,192]{1,0:T(8,128)(2,1)S(1)}, u32[]{:S(2)}, u32[]{:S(2)}) collective-permute-start(bf16[640,192]{1,0:T(8,128)(2,1)} %get-tuple-element.35.q_ref), channel_id=1, source_target_pairs={{0,8},{8,0},{1,9},{9,1},{2,10},{10,2},{3,11},{11,3},{4,12},{12,4},... | collective-permute-start | bytes 737288 | tf_op jit(solution)/shard_map/ppermute | solution.py:570
  69.7 10.7 %collective-permute-start.8 = (bf16[640,192]{1,0:T(8,128)(2,1)}, bf16[640,192]{1,0:T(8,128)(2,1)S(1)}, u32[]{:S(2)}, u32[]{:S(2)}) collective-permute-start(bf16[640,192]{1,0:T(8,128)(2,1)} %get-tuple-element.42.q_ref), channel_id=1, source_target_pairs={{0,8},{8,0},{1,9},{9,1},{2,10},{10,2},{3,11},{11,3},{4,12},{12,4},... | collective-permute-start | bytes 737288 | tf_op jit(solution)/shard_map/ppermute | solution.py:570
  73.2 0.8 copy-start.5
  77.6 3.5 %collective-permute-start.6 = (bf16[192,128]{1,0:T(8,128)(2,1)}, bf16[192,128]{1,0:T(8,128)(2,1)S(1)}, u32[]{:S(2)}, u32[]{:S(2)}) collective-permute-start(bf16[192,128]{1,0:T(8,128)(2,1)} %get-tuple-element.39), channel_id=1, source_target_pairs={{0,1},{1,0},{2,3},{3,2},{4,5},{5,4},{6,7},{7,6},{8,9},{9,8},{10,11... | collective-permute-start | bytes 147464 | tf_op jit(solution)/shard_map/ppermute | solution.py:573
  78.5 5.9 %collective-permute-start.7 = (bf16[192,128]{1,0:T(8,128)(2,1)}, bf16[192,128]{1,0:T(8,128)(2,1)S(1)}, u32[]{:S(2)}, u32[]{:S(2)}) collective-permute-start(bf16[192,128]{1,0:T(8,128)(2,1)} %get-tuple-element.40), channel_id=1, source_target_pairs={{1,2},{2,1},{3,4},{4,3},{5,6},{6,5},{9,10},{10,9},{11,12},{12,11},... | collective-permute-start | bytes 147464 | tf_op jit(solution)/shard_map/ppermute | solution.py:574
  80.4 4.0 %copy-start.6 = (bf16[640,192]{1,0:T(8,128)(2,1)}, bf16[640,192]{1,0:T(8,128)(2,1)S(1)}, u32[]{:S(2)}) copy-start(bf16[640,192]{1,0:T(8,128)(2,1)S(1)} %collective-permute-done.8.other_ref) | copy-start | bytes 737284
  81.1 3.3 %copy-start.7 = (bf16[192,128]{1,0:T(8,128)(2,1)}, bf16[192,128]{1,0:T(8,128)(2,1)S(1)}, u32[]{:S(2)}) copy-start(bf16[192,128]{1,0:T(8,128)(2,1)S(1)} %collective-permute-done.6.one_ref) | copy-start | bytes 147460
  84.4 0.6 copy-start.8
  93.1 11.4 %copy-start.4 = (bf16[6,320,128]{2,1,0:T(8,128)(2,1)S(1)}, bf16[6,320,128]{2,1,0:T(8,128)(2,1)}, u32[]{:S(2)}) copy-start(bf16[6,320,128]{2,1,0:T(8,128)(2,1)} %get-tuple-element.46) | copy-start | bytes 1474564
  93.1 11.4 %collective-permute-start.10 = (bf16[6,320,128]{2,1,0:T(8,128)(2,1)}, bf16[6,320,128]{2,1,0:T(8,128)(2,1)S(1)}, u32[]{:S(2)}, u32[]{:S(2)}) collective-permute-start(bf16[6,320,128]{2,1,0:T(8,128)(2,1)} %get-tuple-element.47), channel_id=1, source_target_pairs={{0,8},{8,0},{1,9},{9,1},{2,10},{10,2},{3,11},{11,3},{4,12},{12,4},... | collective-permute-start | bytes 1474568 | tf_op jit(solution)/shard_map/ppermute | solution.py:570
  101.6 1.4 %collective-permute-start.9 = (f32[6,256]{1,0:T(8,128)}, f32[6,256]{1,0:T(8,128)S(1)}, u32[]{:S(2)}, u32[]{:S(2)}) collective-permute-start(f32[6,256]{1,0:T(8,128)} %get-tuple-element.45), channel_id=1, source_target_pairs={{0,8},{8,0},{1,9},{9,1},{2,10},{10,2},{3,11},{11,3},{4,12},{12,4},... | collective-permute-start | bytes 18440 | tf_op jit(solution)/shard_map/ppermute | solution.py:570

commit v5 on v4

--- a/solution.py
+++ b/solution.py
@@ -105,7 +105,7 @@
     bias_ref[...] = jnp.broadcast_to(bias_ref[:, step : step + 1], bias_ref.shape)
 
 
-def edges_kernel(latent_ref, stale_hbm, one_hbm, two_hbm, state_hbm, latent_out, part_ref, sems):
+def edges_kernel(latent_ref, stale_hbm, one_ref, two_ref, state_ref, latent_out, sems):
     segment = lax.axis_index("segment")
     even = lax.axis_index("rows") % 2 == 0
     rows, _, width = latent_ref.shape
@@ -114,27 +114,21 @@
     halo = 3
     index_one = jnp.where(even, rows - 1, 0)
     index_two = jnp.where(even, 0, rows - 1)
-    pairs = [(stale_hbm.at[0, 1 - segment], state_hbm)]
+    pairs = []
     for slot, frame in enumerate((segment, 1 - segment)):
-        pairs.append((stale_hbm.at[0, frame, index_one], one_hbm.at[slot, pl.ds(0, chans)]))
-        pairs.append((stale_hbm.at[0, frame, index_two], two_hbm.at[slot, pl.ds(0, chans)]))
+        pairs.append((stale_hbm.at[0, frame, index_one], one_ref.at[slot, pl.ds(0, chans)]))
+        pairs.append((stale_hbm.at[0, frame, index_two], two_ref.at[slot, pl.ds(0, chans)]))
+    pairs.append((stale_hbm.at[0, 1 - segment], state_ref))
     copies = fetches(pairs, sems)
     first = segment == 0
     frames = [jnp.where(first, latent_ref[:, k, :], latent_ref[:, 1 - k, :]) for k in range(2)]
     latent_out[...] = frames[1]
-    late = []
     for slot in range(2):
         last, top = frames[slot][rows - halo :], frames[slot][:halo]
-        for which, piece in enumerate((jnp.where(even, last, top), jnp.where(even, top, last))):
+        for ref, piece in ((one_ref, jnp.where(even, last, top)), (two_ref, jnp.where(even, top, last))):
             flat = [piece[:, k * cols : (k + 1) * cols] for k in range(pieces)]
             flat.append(jnp.zeros((TILE - pieces * halo, cols), F32))
-            part_ref[which, slot] = jnp.concatenate(flat, axis=0).astype(BF16)
-            target = (one_hbm, two_hbm)[which].at[slot, pl.ds(chans, TILE)]
-            late.append((part_ref.at[which, slot], target))
-    for offset, (src, dst) in enumerate(late):
-        copy = pltpu.make_async_copy(src, dst, sems.at[len(pairs) + offset])
-        copy.start()
-        copies.append(copy)
+            ref[slot, chans:] = jnp.concatenate(flat, axis=0).astype(BF16)
     for copy in copies:
         copy.wait()
 
@@ -576,12 +570,7 @@
 
     payload = ((2, chans + TILE, cols), BF16)
     to_one, to_two, to_state, to_latent = call(
-        edges_kernel,
-        [payload, payload, ((rows, chans, cols), BF16), ((rows, width), F32)],
-        [VMEM, ANY],
-        [((2, 2, TILE, cols), BF16)],
-        9,
-        [ANY] * 3 + [VMEM],
+        edges_kernel, [payload, payload, ((rows, chans, cols), BF16), ((rows, width), F32)], [VMEM, ANY], (), 5
     )(row_major, chan_major)
     one, two = exchange(to_one, to_two)
     got = swap(to_state)
@@ -657,13 +646,14 @@
     )(low1, q1, q1_other, base, near, got_one, got_two, w_small, w_up_t, w_enc_t, w_tmid_t, bias)
     feat_got = swap(feat_send)
 
-    x_send, x_keep = call(
+    last = call(
         last_kernel,
         [((rows, width), F32)] * 2,
         [SMEM] + [VMEM] * 7 + [ANY] * 2,
         [((chans, (rows // 2 + 2) * cols), BF16), w_conv, b_conv] + conv_scratch(rows + 2),
         2,
-    )(timesteps, enc1, mid1, got_one, got_two, x1, w_skip_t, w_small, w_dec_t, bias)
+    )
+    x_send, x_keep = last(timesteps, enc1, mid1, got_one, got_two, x1, w_skip_t, w_small, w_dec_t, bias)
     x_far = swap(x_send)
 
     features = jnp.where(first, jnp.stack([feat_keep, feat_got]), jnp.stack([feat_got, feat_keep]))

time: 106 us -> 81.7 us (0.77)
  the two profiles are of different devices: /device:TPU:11 before, /device:TPU:17 now
where the time goes in v5:
time: 81.7 us; the launch traced here: 81.1 us
  Pallas kernels  51.3 us (63%)
  starting transfers between devices  11.5 us (14%)
  waiting for transfers between devices  9.15 us (11%)
  local copies, waits for them, and re-layouts  4.23 us (5%)
  other arithmetic  4.07 us (5%)
  between operations  0.87 us (1%)
    pallas_call x1, Pallas kernels, step_pair(): call(first_kernel, [((rows, LAT8, cols), F32), ((2, LAT8, cols), F32)] +...  9.64 us
    pallas_call x1, Pallas kernels, step_pair(): call(second_kernel, [((rows + 4, chans, cols), BF16)] + down_outs, [VMEM]...  9.13 us
    pallas_call x1, Pallas kernels, step_pair(): call(prep_kernel, turned, [VMEM] + [ANY] * 4, [(w.shape, BF16) for w in w...  8.03 us
    pallas_call x1, Pallas kernels, step_pair(): call(third_kernel, [((rows, chans, cols), BF16)] * 2 + [((rows, LAT8, col...  8.02 us
    ppermute x2, waiting for transfers between devices, exchange(): got_two = lax.ppermute(two, 'rows', paired(1))  7.59 us
    pallas_call x1, Pallas kernels, step_pair(): last(timesteps, enc1, mid1, got_one, got_two, x1, w_skip_t, w_small, w_de...  6.99 us
    ppermute x7, starting transfers between devices, swap(): return lax.ppermute(value, 'segment', [(0, 1), (1, 0)])  5 us
    ppermute x2, starting transfers between devices, exchange(): got_two = lax.ppermute(two, 'rows', paired(1))  4.38 us
  transfers between devices with their start and end apart: 11, of which 4 were waited for; matrix products, arithmetic and copies ran while one was open for 6% of the time, Pallas kernels for 38%

profile of v5, /device:TPU:17, one launch (start us, length us, event | category | flops | bytes accessed | tf_op | source)
XLA Modules:
  0.0 81.1 jit_solution(4488656702873950494)
XLA Ops:
  0.6 2.9 %shard_map.131 = (bf16[2,336,128]{2,1,0:T(8,128)(2,1)}, bf16[2,336,128]{2,1,0:T(8,128)(2,1)}, bf16[6,320,128]{2,1,0:T(8,128)(2,1)}, f32[6,256]{1,0:T(8,128)}) custom-call(f32[6,2,256]{2,1,0:T(2,128)} %bitcast.23, bf16[1,2,6,320,128]{4,3,2,1,0:T(8,128)(2,1)} %bitcast.14), custom_call_target="tpu_custom_call" | custom-call | tf_op jit(solution)/shard_map/pallas_call | solution.py:572
  3.5 0.7 collective-permute-start
  4.2 1.2 %collective-permute-start.1 = (bf16[2,336,128]{2,1,0:T(8,128)(2,1)}, bf16[2,336,128]{2,1,0:T(8,128)(2,1)S(1)}, u32[]{:S(2)}, u32[]{:S(2)}) collective-permute-start(bf16[2,336,128]{2,1,0:T(8,128)(2,1)} %get-tuple-element.26), channel_id=1, source_target_pairs={{0,1},{1,0},{2,3},{3,2},{4,5},{5,4},{6,7},{7,6},{8,9},{9,8},{10,11... | collective-permute-start | bytes 516104 | tf_op jit(solution)/shard_map/ppermute | solution.py:567
  5.5 2.0 %collective-permute-start.2 = (bf16[2,336,128]{2,1,0:T(8,128)(2,1)}, bf16[2,336,128]{2,1,0:T(8,128)(2,1)S(1)}, u32[]{:S(2)}, u32[]{:S(2)}) collective-permute-start(bf16[2,336,128]{2,1,0:T(8,128)(2,1)} %get-tuple-element.27), channel_id=1, source_target_pairs={{1,2},{2,1},{3,4},{4,3},{5,6},{6,5},{9,10},{10,9},{11,12},{12,11},... | collective-permute-start | bytes 516104 | tf_op jit(solution)/shard_map/ppermute | solution.py:568
  7.5 0.7 collective-permute-start.4
  8.2 0.8 copy.16
  9.0 0.7 convert_element_type.19
  9.6 0.1 multiply_sine_fusion
  9.8 4.3 %collective-permute-done.2.two_ref = bf16[2,336,128]{2,1,0:T(8,128)(2,1)S(1)} collective-permute-done((bf16[2,336,128]{2,1,0:T(8,128)(2,1)}, bf16[2,336,128]{2,1,0:T(8,128)(2,1)S(1)}, u32[]{:S(2)}, u32[]{:S(2)}) %collective-permute-start.2) | collective-permute-done | bytes 172064 | tf_op jit(solution)/shard_map/ppermute | solution.py:568
  14.0 0.0 collective-permute-done.1.one_ref
  14.1 1.3 %collective-permute-start.3 = (bf16[2,336,128]{2,1,0:T(8,128)(2,1)S(1)}, bf16[2,336,128]{2,1,0:T(8,128)(2,1)S(1)}, u32[]{:S(2)}, u32[]{:S(2)}) collective-permute-start(bf16[2,336,128]{2,1,0:T(8,128)(2,1)S(1)} %pad_maximum_fusion), channel_id=1, source_target_pairs={{0,8},{8,0},{1,9},{9,1},{2,10},{10,2},{3,11},{11,3},{4,12},{12,4},... | collective-permute-start | bytes 516104 | tf_op jit(solution)/shard_map/ppermute | solution.py:564
  15.4 1.3 %fusion.2.w_small_ref = bf16[80,320]{1,0:T(8,128)(2,1)} fusion(bf16[4,320]{1,0:T(4,128)(2,1)} %param.15, bf16[72,320]{1,0:T(8,128)(2,1)S(1)} %bitcast.22), kind=kLoop, calls=%fused_computation.5 | loop fusion | flops 153600 | bytes 99840 | tf_op jit(solution)/shard_map/concatenate | solution.py:581
  16.7 0.1 fusion.3
  16.8 0.6 pad.14.gated_ref
  17.4 8.0 %shard_map.132 = (bf16[320,2880]{1,0:T(8,128)(2,1)}, bf16[320,2880]{1,0:T(8,128)(2,1)}, bf16[640,2880]{1,0:T(8,128)(2,1)}, f32[1280,128]{1,0:T(8,128)}) custom-call(bf16[16,320]{1,0:T(8,128)(2,1)} %pad.14.gated_ref, bf16[3,3,320,320]{3,2,1,0:T(8,128)(2,1)} %enc_hbm.1, bf16[3,3,320,320]{3,2,1,0:T(8,128)(2,1)} %dec_hbm.1, bf16[3,3,320,640]{3,2,1,0:T(8,128)(2,1)} %down_hbm.1, ...), custom_call_target="tpu_custom_call" | custom-call | tf_op jit(solution)/shard_map/pallas_call | solution.py:595
  25.5 0.0 copy-done.1
  25.5 0.0 copy-done
  25.5 0.0 collective-permute-done.x_got_ref
  25.5 0.0 copy-start.9
  25.5 0.0 collective-permute-done.3.far_ref
  25.5 0.0 collective-permute-done.4.got_ref
  25.5 0.0 copy-start.3
  25.5 0.5 copy-done.9
  26.1 0.1 copy-done.2
  26.2 0.2 copy-done.3
  26.3 9.6 %shard_map.134 = (f32[6,8,128]{2,1,0:T(8,128)}, f32[2,8,128]{2,1,0:T(8,128)}, f32[640,192]{1,0:T(8,128)}, bf16[640,192]{1,0:T(8,128)(2,1)}) custom-call(s32[2]{0:T(128)} %times_ref.3, f32[6,2,256]{2,1,0:T(2,128)} %bitcast.24, f32[6,256]{1,0:T(8,128)} %copy-done.9, bf16[6,320,128]{2,1,0:T(8,128)(2,1)} %copy-done.3, bf16[2,336,128]{2,1,0:T(8,128)(2,1)} %copy-done, ...), custom_call_target="tpu_custom_call" | custom-call | tf_op jit(solution)/shard_map/pallas_call | solution.py:614
  36.0 0.1 collective-permute-start.5
  36.1 9.1 %shard_map.133 = (bf16[10,320,128]{2,1,0:T(8,128)(2,1)}, f32[640,192]{1,0:T(8,128)}, bf16[640,192]{1,0:T(8,128)(2,1)}) custom-call(f32[6,2,256]{2,1,0:T(2,128)} %bitcast.25, f32[6,256]{1,0:T(8,128)} %copy-done.9, bf16[2,336,128]{2,1,0:T(8,128)(2,1)} %copy-done, bf16[2,336,128]{2,1,0:T(8,128)(2,1)} %copy-done.1, bf16[2,336,128]{2,1,0:T(8,128)(2,1)} %copy-done.2, ...), custom_call_target="tpu_custom_call" | custom-call | tf_op jit(solution)/shard_map/pallas_call | solution.py:631
  45.2 0.6 collective-permute-start.8
  45.8 2.9 %shard_map.135.w_tmid_ref.w_tmid_hbm = bf16[2,640,640]{2,1,0:T(8,128)(2,1)} custom-call(bf16[3,640,640]{2,1,0:T(8,128)(2,1)} %tmid_hbm.1), custom_call_target="tpu_custom_call" | custom-call | tf_op jit(solution)/shard_map/pallas_call | solution.py:623
  48.7 0.0 collective-permute-done.5.other_ref
  48.7 0.7 copy-done.5
  49.5 3.7 %shard_map.136 = (bf16[320,192]{1,0:T(8,128)(2,1)}, bf16[192,128]{1,0:T(8,128)(2,1)}, bf16[192,128]{1,0:T(8,128)(2,1)}) custom-call(f32[640,192]{1,0:T(8,128)} %get-tuple-element.34.low_ref, bf16[640,192]{1,0:T(8,128)(2,1)} %get-tuple-element.35.q_ref, bf16[640,192]{1,0:T(8,128)(2,1)} %copy-done.5, bf16[2,640,640]{2,1,0:T(8,128)(2,1)} %shard_map.135.w_tmid_ref.w_tmid_hbm, ...), custom_call_target="tpu_custom_call" | custom-call | tf_op jit(solution)/shard_map/pallas_call | solution.py:626
  53.2 0.9 %collective-permute-start.6 = (bf16[192,128]{1,0:T(8,128)(2,1)}, bf16[192,128]{1,0:T(8,128)(2,1)S(1)}, u32[]{:S(2)}, u32[]{:S(2)}) collective-permute-start(bf16[192,128]{1,0:T(8,128)(2,1)} %get-tuple-element.39), channel_id=1, source_target_pairs={{0,1},{1,0},{2,3},{3,2},{4,5},{5,4},{6,7},{7,6},{8,9},{9,8},{10,11... | collective-permute-start | bytes 147464 | tf_op jit(solution)/shard_map/ppermute | solution.py:567
  54.0 2.4 %collective-permute-start.7 = (bf16[192,128]{1,0:T(8,128)(2,1)}, bf16[192,128]{1,0:T(8,128)(2,1)S(1)}, u32[]{:S(2)}, u32[]{:S(2)}) collective-permute-start(bf16[192,128]{1,0:T(8,128)(2,1)} %get-tuple-element.40), channel_id=1, source_target_pairs={{1,2},{2,1},{3,4},{4,3},{5,6},{6,5},{9,10},{10,9},{11,12},{12,11},... | collective-permute-start | bytes 147464 | tf_op jit(solution)/shard_map/ppermute | solution.py:568
  56.4 0.0 collective-permute-done.8.other_ref
  56.4 0.2 collective-permute-done.6.one_ref
  56.6 3.3 %collective-permute-done.7.two_ref = bf16[192,128]{1,0:T(8,128)(2,1)S(1)} collective-permute-done((bf16[192,128]{1,0:T(8,128)(2,1)}, bf16[192,128]{1,0:T(8,128)(2,1)S(1)}, u32[]{:S(2)}, u32[]{:S(2)}) %collective-permute-start.7) | collective-permute-done | bytes 49184 | tf_op jit(solution)/shard_map/ppermute | solution.py:568
  60.0 0.6 copy-done.8
  60.6 8.0 %shard_map.137 = (bf16[6,320,128]{2,1,0:T(8,128)(2,1)}, bf16[6,320,128]{2,1,0:T(8,128)(2,1)}, f32[6,8,128]{2,1,0:T(8,128)}) custom-call(f32[640,192]{1,0:T(8,128)} %get-tuple-element.41.low_ref, bf16[640,192]{1,0:T(8,128)(2,1)} %get-tuple-element.42.q_ref, bf16[640,192]{1,0:T(8,128)(2,1)} %copy-done.6, f32[6,8,128]{2,1,0:T(8,128)} %get-tuple-element.36.base_ref, ...), custom_call_target="tpu_custom_call" | custom-call | tf_op jit(solution)/shard_map/pallas_call | solution.py:640
  68.6 1.5 %collective-permute-start.10 = (bf16[6,320,128]{2,1,0:T(8,128)(2,1)}, bf16[6,320,128]{2,1,0:T(8,128)(2,1)S(1)}, u32[]{:S(2)}, u32[]{:S(2)}) collective-permute-start(bf16[6,320,128]{2,1,0:T(8,128)(2,1)} %get-tuple-element.47), channel_id=1, source_target_pairs={{0,8},{8,0},{1,9},{9,1},{2,10},{10,2},{3,11},{11,3},{4,12},{12,4},... | collective-permute-start | bytes 1474568 | tf_op jit(solution)/shard_map/ppermute | solution.py:564
  70.2 7.0 %shard_map.138 = (f32[6,256]{1,0:T(8,128)}, f32[6,256]{1,0:T(8,128)}) custom-call(s32[2]{0:T(128)} %times_ref.3, bf16[10,320,128]{2,1,0:T(8,128)(2,1)} %get-tuple-element.31.enc_ref, bf16[320,192]{1,0:T(8,128)(2,1)} %get-tuple-element.38.mid_ref, bf16[192,128]{1,0:T(8,128)(2,1)} %copy-done.7, bf16[192,128]{1,0:T(8,128)(2,1)} %copy-done.8, ...), custom_call_target="tpu_custom_call" | custom-call | tf_op jit(solution)/shard_map/pallas_call | solution.py:656
  77.1 0.1 collective-permute-start.9
  77.3 1.3 %collective-permute-done.9 = f32[6,256]{1,0:T(8,128)S(1)} collective-permute-done((f32[6,256]{1,0:T(8,128)}, f32[6,256]{1,0:T(8,128)S(1)}, u32[]{:S(2)}, u32[]{:S(2)}) %collective-permute-start.9) | collective-permute-done | bytes 6176 | tf_op jit(solution)/shard_map/ppermute | solution.py:564
  78.6 0.8 maximum_select_fusion.1
  79.4 0.6 copy.15
  80.0 0.0 collective-permute-done.10
  80.0 1.1 %fusion = bf16[1,2,6,128,320]{3,4,2,1,0:T(8,128)(2,1)} fusion(bf16[1,6,320,128]{3,2,1,0:T(8,128)(2,1)S(1)} %bitcast.21, bf16[1,6,320,128]{3,2,1,0:T(8,128)(2,1)S(1)} %bitcast.20, pred[]{:T(512)S(6)} %eq.3), kind=kLoop, calls=%fused_computation.1 | loop fusion | flops 1474560 | bytes 1966081 | tf_op jit(solution)/shard_map/broadcast_in_dim | solution.py:661
  (16 shorter events, 0.1 us)
Async XLA Ops:
  3.5 22.0 %collective-permute-start = (f32[6,256]{1,0:T(8,128)}, f32[6,256]{1,0:T(8,128)S(1)}, u32[]{:S(2)}, u32[]{:S(2)}) collective-permute-start(f32[6,256]{1,0:T(8,128)} %get-tuple-element.25), channel_id=1, source_target_pairs={{0,8},{8,0},{1,9},{9,1},{2,10},{10,2},{3,11},{11,3},{4,12},{12,4},... | collective-permute-start | bytes 18440 | tf_op jit(solution)/shard_map/ppermute | solution.py:564
  4.2 9.8 %collective-permute-start.1 = (bf16[2,336,128]{2,1,0:T(8,128)(2,1)}, bf16[2,336,128]{2,1,0:T(8,128)(2,1)S(1)}, u32[]{:S(2)}, u32[]{:S(2)}) collective-permute-start(bf16[2,336,128]{2,1,0:T(8,128)(2,1)} %get-tuple-element.26), channel_id=1, source_target_pairs={{0,1},{1,0},{2,3},{3,2},{4,5},{5,4},{6,7},{7,6},{8,9},{9,8},{10,11... | collective-permute-start | bytes 516104 | tf_op jit(solution)/shard_map/ppermute | solution.py:567
  5.5 8.6 %collective-permute-start.2 = (bf16[2,336,128]{2,1,0:T(8,128)(2,1)}, bf16[2,336,128]{2,1,0:T(8,128)(2,1)S(1)}, u32[]{:S(2)}, u32[]{:S(2)}) collective-permute-start(bf16[2,336,128]{2,1,0:T(8,128)(2,1)} %get-tuple-element.27), channel_id=1, source_target_pairs={{1,2},{2,1},{3,4},{4,3},{5,6},{6,5},{9,10},{10,9},{11,12},{12,11},... | collective-permute-start | bytes 516104 | tf_op jit(solution)/shard_map/ppermute | solution.py:568
  7.5 18.0 %collective-permute-start.4 = (bf16[6,320,128]{2,1,0:T(8,128)(2,1)}, bf16[6,320,128]{2,1,0:T(8,128)(2,1)S(1)}, u32[]{:S(2)}, u32[]{:S(2)}) collective-permute-start(bf16[6,320,128]{2,1,0:T(8,128)(2,1)} %get-tuple-element.32), channel_id=1, source_target_pairs={{0,8},{8,0},{1,9},{9,1},{2,10},{10,2},{3,11},{11,3},{4,12},{12,4},... | collective-permute-start | bytes 1474568 | tf_op jit(solution)/shard_map/ppermute | solution.py:564
  14.0 11.4 %copy-start.1 = (bf16[2,336,128]{2,1,0:T(8,128)(2,1)}, bf16[2,336,128]{2,1,0:T(8,128)(2,1)S(1)}, u32[]{:S(2)}) copy-start(bf16[2,336,128]{2,1,0:T(8,128)(2,1)S(1)} %collective-permute-done.2.two_ref) | copy-start | bytes 516100
  14.1 11.4 %copy-start = (bf16[2,336,128]{2,1,0:T(8,128)(2,1)}, bf16[2,336,128]{2,1,0:T(8,128)(2,1)S(1)}, u32[]{:S(2)}) copy-start(bf16[2,336,128]{2,1,0:T(8,128)(2,1)S(1)} %collective-permute-done.1.one_ref) | copy-start | bytes 516100
  14.1 11.4 %collective-permute-start.3 = (bf16[2,336,128]{2,1,0:T(8,128)(2,1)S(1)}, bf16[2,336,128]{2,1,0:T(8,128)(2,1)S(1)}, u32[]{:S(2)}, u32[]{:S(2)}) collective-permute-start(bf16[2,336,128]{2,1,0:T(8,128)(2,1)S(1)} %pad_maximum_fusion), channel_id=1, source_target_pairs={{0,8},{8,0},{1,9},{9,1},{2,10},{10,2},{3,11},{11,3},{4,12},{12,4},... | collective-permute-start | bytes 516104 | tf_op jit(solution)/shard_map/ppermute | solution.py:564
  25.5 0.6 copy-start.9
  25.5 0.7 copy-start.2
  25.5 0.8 %copy-start.3 = (bf16[6,320,128]{2,1,0:T(8,128)(2,1)}, bf16[6,320,128]{2,1,0:T(8,128)(2,1)S(1)}, u32[]{:S(2)}) copy-start(bf16[6,320,128]{2,1,0:T(8,128)(2,1)S(1)} %collective-permute-done.4.got_ref) | copy-start | bytes 1474564
  36.0 12.7 %collective-permute-start.5 = (bf16[640,192]{1,0:T(8,128)(2,1)}, bf16[640,192]{1,0:T(8,128)(2,1)S(1)}, u32[]{:S(2)}, u32[]{:S(2)}) collective-permute-start(bf16[640,192]{1,0:T(8,128)(2,1)} %get-tuple-element.35.q_ref), channel_id=1, source_target_pairs={{0,8},{8,0},{1,9},{9,1},{2,10},{10,2},{3,11},{11,3},{4,12},{12,4},... | collective-permute-start | bytes 737288 | tf_op jit(solution)/shard_map/ppermute | solution.py:564
  45.2 11.2 %collective-permute-start.8 = (bf16[640,192]{1,0:T(8,128)(2,1)}, bf16[640,192]{1,0:T(8,128)(2,1)S(1)}, u32[]{:S(2)}, u32[]{:S(2)}) collective-permute-start(bf16[640,192]{1,0:T(8,128)(2,1)} %get-tuple-element.42.q_ref), channel_id=1, source_target_pairs={{0,8},{8,0},{1,9},{9,1},{2,10},{10,2},{3,11},{11,3},{4,12},{12,4},... | collective-permute-start | bytes 737288 | tf_op jit(solution)/shard_map/ppermute | solution.py:564
  48.7 0.8 copy-start.5
  53.2 3.5 %collective-permute-start.6 = (bf16[192,128]{1,0:T(8,128)(2,1)}, bf16[192,128]{1,0:T(8,128)(2,1)S(1)}, u32[]{:S(2)}, u32[]{:S(2)}) collective-permute-start(bf16[192,128]{1,0:T(8,128)(2,1)} %get-tuple-element.39), channel_id=1, source_target_pairs={{0,1},{1,0},{2,3},{3,2},{4,5},{5,4},{6,7},{7,6},{8,9},{9,8},{10,11... | collective-permute-start | bytes 147464 | tf_op jit(solution)/shard_map/ppermute | solution.py:567
  54.0 5.9 %collective-permute-start.7 = (bf16[192,128]{1,0:T(8,128)(2,1)}, bf16[192,128]{1,0:T(8,128)(2,1)S(1)}, u32[]{:S(2)}, u32[]{:S(2)}) collective-permute-start(bf16[192,128]{1,0:T(8,128)(2,1)} %get-tuple-element.40), channel_id=1, source_target_pairs={{1,2},{2,1},{3,4},{4,3},{5,6},{6,5},{9,10},{10,9},{11,12},{12,11},... | collective-permute-start | bytes 147464 | tf_op jit(solution)/shard_map/ppermute | solution.py:568
  56.4 3.5 %copy-start.6 = (bf16[640,192]{1,0:T(8,128)(2,1)}, bf16[640,192]{1,0:T(8,128)(2,1)S(1)}, u32[]{:S(2)}) copy-start(bf16[640,192]{1,0:T(8,128)(2,1)S(1)} %collective-permute-done.8.other_ref) | copy-start | bytes 737284
  56.6 3.3 %copy-start.7 = (bf16[192,128]{1,0:T(8,128)(2,1)}, bf16[192,128]{1,0:T(8,128)(2,1)S(1)}, u32[]{:S(2)}) copy-start(bf16[192,128]{1,0:T(8,128)(2,1)S(1)} %collective-permute-done.6.one_ref) | copy-start | bytes 147460
  60.0 0.6 copy-start.8
  68.6 11.4 %copy-start.4 = (bf16[6,320,128]{2,1,0:T(8,128)(2,1)S(1)}, bf16[6,320,128]{2,1,0:T(8,128)(2,1)}, u32[]{:S(2)}) copy-start(bf16[6,320,128]{2,1,0:T(8,128)(2,1)} %get-tuple-element.46) | copy-start | bytes 1474564
  68.6 11.4 %collective-permute-start.10 = (bf16[6,320,128]{2,1,0:T(8,128)(2,1)}, bf16[6,320,128]{2,1,0:T(8,128)(2,1)S(1)}, u32[]{:S(2)}, u32[]{:S(2)}) collective-permute-start(bf16[6,320,128]{2,1,0:T(8,128)(2,1)} %get-tuple-element.47), channel_id=1, source_target_pairs={{0,8},{8,0},{1,9},{9,1},{2,10},{10,2},{3,11},{11,3},{4,12},{12,4},... | collective-permute-start | bytes 1474568 | tf_op jit(solution)/shard_map/ppermute | solution.py:564
  77.1 1.4 %collective-permute-start.9 = (f32[6,256]{1,0:T(8,128)}, f32[6,256]{1,0:T(8,128)S(1)}, u32[]{:S(2)}, u32[]{:S(2)}) collective-permute-start(f32[6,256]{1,0:T(8,128)} %get-tuple-element.45), channel_id=1, source_target_pairs={{0,8},{8,0},{1,9},{9,1},{2,10},{10,2},{3,11},{11,3},{4,12},{12,4},... | collective-permute-start | bytes 18440 | tf_op jit(solution)/shard_map/ppermute | solution.py:564
